TPU v7x, 32 devices: a whole 2x2x4 slice. The times are simulated.
32 devices in a mesh: batch: 8 (over z, y), seq: 4 (over x, core).
Axes of the slice: x: 2, y: 2, z: 4, core: 2. Of those that a mesh axis runs over, the one named last changes fastest.
Arguments:
- source_tokens: bfloat16 [8, 1024, 1024], P('batch', 'seq'), may hold values from -6 to 6
- target_tokens: bfloat16 [8, 1024, 1024], P('batch', 'seq'), may hold values from -6 to 6
- source_lengths: int32 [8, 16], P('batch'), may hold values from 1 to 512, 1024 in all within a row
- target_lengths: int32 [8, 16], P('batch'), may hold values from 1 to 512, 1024 in all within a row
- projections: bfloat16 [3, 1024, 3072], P(None, 'batch'), may hold values from -0.1875 to 0.1875
- combiners: bfloat16 [3, 1024, 1024], P(None, 'batch'), may hold values from -0.75 to 0.75
- expanders: bfloat16 [2, 1024, 4096], P(None, 'batch'), may hold values from -0.1875 to 0.1875
- reducers: bfloat16 [2, 4096, 1024], P(None, 'batch'), may hold values from -0.09375 to 0.09375
- norm_gains: float32 [5, 1024], replicated, may hold values from 0.5 to 1.5
- norm_shifts: float32 [5, 1024], replicated, may hold values from -1.2 to 1.2
- attention_biases: float32 [3, 3, 1024], replicated, may hold values from -0.6 to 0.6
- expander_biases: float32 [2, 4096], replicated, may hold values from -1.2 to 1.2
- reducer_biases: float32 [2, 1024], replicated, may hold values from -1.2 to 1.2
- source_cotangent: bfloat16 [8, 1024, 1024], P('batch', 'seq'), may hold values from -6 to 6
- target_cotangent: bfloat16 [8, 1024, 1024], P('batch', 'seq'), may hold values from -6 to 6
Outputs:
- encoder_output: bfloat16 [8, 1024, 1024], P('batch', 'seq')
- decoder_output: bfloat16 [8, 1024, 1024], P('batch', 'seq')
- source_gradient: float32 [8, 1024, 1024], P('batch', 'seq')
- target_gradient: float32 [8, 1024, 1024], P('batch', 'seq')
- projections_gradient: float32 [3, 1024, 3072], P(None, 'batch')
- combiners_gradient: float32 [3, 1024, 1024], P(None, 'batch')
- expanders_gradient: float32 [2, 1024, 4096], P(None, 'batch')
- reducers_gradient: float32 [2, 4096, 1024], P(None, 'batch')
- gains_gradient: float32 [5, 1024], replicated
- shifts_gradient: float32 [5, 1024], replicated
- attention_biases_gradient: float32 [3, 3, 1024], replicated
- expander_biases_gradient: float32 [2, 4096], replicated
- reducer_biases_gradient: float32 [2, 1024], replicated
Inputs may be any that keep to these rules, and one draw needn't show every extreme that they name: `source_lengths`: in every row the 16 entries sum to 1024; the last entry counts the padding tokens at the row's end; the largest entry is 512. `target_lengths`: in every row the 16 entries sum to 1024; the last entry counts the padding tokens at the row's end; the largest entry is 512.
All inputs are finite; a program needn't handle non-finite values.
Results may differ from a plain program's by a relative error of at most 0.025.
Values may be sent and summed in bfloat16 or wider, within the bound.
No kernel may reach another device: no remote copies, remote signals or barrier semaphores. Data moves between devices by JAX's collectives and lax.ppermute only.
A program may use at most 384 MiB of HBM per device.

v0:
```python
import jax
import jax.numpy as jnp
from jax import lax
from jax.sharding import PartitionSpec as P

HEADS = 16


epsilon = 1e-05
masked_score = -1e30


def layer_norm(values, gain_vec, offset):
    middle = jnp.mean(values, -1, keepdims=True)
    centred = values - middle
    spread = jnp.mean(centred * centred, -1, keepdims=True)
    return centred * lax.rsqrt(spread + epsilon) * gain_vec + offset


def gelu_exact(values):
    return jax.nn.gelu(values, approximate=False)


def segment_ids(lengths, row_count):
    ends = jnp.cumsum(lengths, axis=-1, dtype=jnp.int32)
    places = jnp.arange(row_count, dtype=jnp.int32)
    return jnp.sum(
        (places[None, :, None] >= ends[:, None, :]).astype(jnp.int32), axis=-1, dtype=jnp.int32
    )


def project(left, weight):
    return jnp.einsum("rsd,de->rse", left, weight, preferred_element_type=jnp.float32)


def project_back(incoming, weight):
    return jnp.einsum("rse,de->rsd", incoming, weight, preferred_element_type=jnp.float32)


def outer_sum(left, incoming):
    return jnp.einsum("rsd,rse->de", left, incoming, preferred_element_type=jnp.float32)


def split_heads(values):
    return values.reshape(values.shape[0], values.shape[1], HEADS, values.shape[2] // HEADS)


def score_scale(model_width):
    return float(model_width // HEADS) ** (-0.5)


def attend_forward(queries, keys_all, values_all, key_mask):
    factor = score_scale(queries.shape[-1])
    raw_scores = (
        jnp.einsum(
            "rqhc,rkhc->rhqk",
            split_heads(queries),
            split_heads(keys_all),
            preferred_element_type=jnp.float32,
        )
        * factor
    )
    scores = jnp.where(key_mask[:, None], raw_scores, masked_score)
    row_max = jnp.max(scores, -1, keepdims=True)
    exponent = jnp.exp(scores - row_max)
    row_sum = jnp.sum(exponent, -1, keepdims=True)
    weights = (exponent / row_sum).astype(jnp.bfloat16)
    mixture = jnp.einsum(
        "rhqk,rkhc->rqhc", weights, split_heads(values_all), preferred_element_type=jnp.float32
    )
    return (mixture.reshape(queries.shape).astype(jnp.bfloat16), row_max + jnp.log(row_sum))


def attend_backward(queries, keys_all, values_all, key_mask, log_total, mixture_gradient):
    factor = score_scale(queries.shape[-1])
    query_heads = split_heads(queries)
    key_heads = split_heads(keys_all)
    value_heads = split_heads(values_all)
    incoming_heads = split_heads(mixture_gradient)
    raw_scores = (
        jnp.einsum("rqhc,rkhc->rhqk", query_heads, key_heads, preferred_element_type=jnp.float32)
        * factor
    )
    weights = jnp.where(key_mask[:, None], jnp.exp(raw_scores - log_total), 0.0)
    value_gradient = jnp.einsum(
        "rhqk,rqhc->rkhc",
        weights.astype(jnp.bfloat16),
        incoming_heads,
        preferred_element_type=jnp.float32,
    )
    weight_gradient = jnp.einsum(
        "rqhc,rkhc->rhqk", incoming_heads, value_heads, preferred_element_type=jnp.float32
    )
    inner_sum = jnp.sum(weights * weight_gradient, -1, keepdims=True)
    score_gradient = (weights * (weight_gradient - inner_sum)).astype(jnp.bfloat16)
    query_gradient = (
        jnp.einsum("rhqk,rkhc->rqhc", score_gradient, key_heads, preferred_element_type=jnp.float32)
        * factor
    )
    key_gradient = (
        jnp.einsum(
            "rhqk,rqhc->rkhc", score_gradient, query_heads, preferred_element_type=jnp.float32
        )
        * factor
    )
    return (
        query_gradient.reshape(queries.shape),
        key_gradient.reshape(keys_all.shape),
        value_gradient.reshape(values_all.shape),
    )


def fetch_attention(projections, combiners, block_id):
    return (
        lax.all_gather(projections[block_id], "batch", axis=0, tiled=True),
        lax.all_gather(combiners[block_id], "batch", axis=0, tiled=True),
    )


def fetch_feedforward(expanders, reducers, block_id):
    return (
        lax.all_gather(expanders[block_id], "batch", axis=0, tiled=True),
        lax.all_gather(reducers[block_id], "batch", axis=0, tiled=True),
    )


def again_attention(projections, combiners, block_id):
    return (
        lax.all_gather(projections[block_id], "batch", axis=0, tiled=True),
        lax.all_gather(combiners[block_id], "batch", axis=0, tiled=True),
    )


def again_feedforward(expanders, reducers, block_id):
    return (
        lax.all_gather(expanders[block_id], "batch", axis=0, tiled=True),
        lax.all_gather(reducers[block_id], "batch", axis=0, tiled=True),
    )


def reduce_weights(gradients):
    shares = (
        lax.psum_scatter(
            gradients[0].astype(jnp.bfloat16), "batch", scatter_dimension=0, tiled=True
        ).astype(jnp.float32),
        lax.psum_scatter(
            gradients[1].astype(jnp.bfloat16), "batch", scatter_dimension=0, tiled=True
        ).astype(jnp.float32),
    )
    return (
        lax.psum(shares[0].astype(jnp.bfloat16), "seq").astype(jnp.float32),
        lax.psum(shares[1].astype(jnp.bfloat16), "seq").astype(jnp.float32),
    )


def self_forward(inputs, key_mask, gain_vec, offset, weights, biases):
    entry_matrix, exit_matrix = weights
    model_width = inputs.shape[-1]
    normed = layer_norm(inputs, gain_vec, offset).astype(jnp.bfloat16)
    projected = project(normed, entry_matrix)
    queries = (projected[..., :model_width] + biases[0]).astype(jnp.bfloat16)
    key_rows = projected[..., model_width : 2 * model_width].astype(jnp.bfloat16)
    value_rows = (projected[..., 2 * model_width :] + biases[1]).astype(jnp.bfloat16)
    keys_all, values_all = (
        lax.all_gather(key_rows, "seq", axis=1, tiled=True),
        lax.all_gather(value_rows, "seq", axis=1, tiled=True),
    )
    mixture, log_total = attend_forward(queries, keys_all, values_all, key_mask)
    result = inputs + project(mixture, exit_matrix) + biases[2]
    return (result, (normed, queries, keys_all, values_all, log_total, mixture))


def cross_forward(inputs, memory_low, key_mask, gain_vec, offset, weights, biases):
    entry_matrix, exit_matrix = weights
    model_width = inputs.shape[-1]
    normed = layer_norm(inputs, gain_vec, offset).astype(jnp.bfloat16)
    queries = (project(normed, entry_matrix[:, :model_width]) + biases[0]).astype(jnp.bfloat16)
    projected = project(memory_low, entry_matrix[:, model_width:])
    key_rows = projected[..., :model_width].astype(jnp.bfloat16)
    value_rows = (projected[..., model_width:] + biases[1]).astype(jnp.bfloat16)
    keys_all, values_all = (
        lax.all_gather(key_rows, "seq", axis=1, tiled=True),
        lax.all_gather(value_rows, "seq", axis=1, tiled=True),
    )
    mixture, log_total = attend_forward(queries, keys_all, values_all, key_mask)
    result = inputs + project(mixture, exit_matrix) + biases[2]
    return (result, (normed, queries, keys_all, values_all, log_total, mixture))


def self_backward(incoming, inputs, key_mask, gain_vec, offset, weights, stored):
    entry_matrix, exit_matrix = weights
    normed, queries, keys_all, values_all, log_total, mixture = stored
    incoming_low = incoming.astype(jnp.bfloat16)
    exit_gradient = outer_sum(mixture, incoming_low)
    exit_bias = jnp.sum(incoming, axis=(0, 1))
    mixture_gradient = project_back(incoming_low, exit_matrix).astype(jnp.bfloat16)
    query_gradient, key_gradient, value_gradient = attend_backward(
        queries, keys_all, values_all, key_mask, log_total, mixture_gradient
    )
    key_gradient, value_gradient = (
        lax.psum_scatter(
            key_gradient.astype(jnp.bfloat16), "seq", scatter_dimension=1, tiled=True
        ).astype(jnp.float32),
        lax.psum_scatter(
            value_gradient.astype(jnp.bfloat16), "seq", scatter_dimension=1, tiled=True
        ).astype(jnp.float32),
    )
    projected_gradient = jnp.concatenate([query_gradient, key_gradient, value_gradient], -1).astype(
        jnp.bfloat16
    )
    entry_gradient = outer_sum(normed, projected_gradient)
    normed_gradient = project_back(projected_gradient, entry_matrix)
    input_gradient, gain_gradient, offset_gradient = jax.vjp(layer_norm, inputs, gain_vec, offset)[
        1
    ](normed_gradient)
    bias_gradient = jnp.stack(
        [jnp.sum(query_gradient, axis=(0, 1)), jnp.sum(value_gradient, axis=(0, 1)), exit_bias]
    )
    return (
        incoming + input_gradient,
        (entry_gradient, exit_gradient),
        gain_gradient,
        offset_gradient,
        bias_gradient,
    )


def cross_backward(incoming, inputs, memory_low, key_mask, gain_vec, offset, weights, stored):
    entry_matrix, exit_matrix = weights
    normed, queries, keys_all, values_all, log_total, mixture = stored
    model_width = inputs.shape[-1]
    incoming_low = incoming.astype(jnp.bfloat16)
    exit_gradient = outer_sum(mixture, incoming_low)
    exit_bias = jnp.sum(incoming, axis=(0, 1))
    mixture_gradient = project_back(incoming_low, exit_matrix).astype(jnp.bfloat16)
    query_gradient, key_gradient, value_gradient = attend_backward(
        queries, keys_all, values_all, key_mask, log_total, mixture_gradient
    )
    key_gradient, value_gradient = (
        lax.psum_scatter(key_gradient, "seq", scatter_dimension=1, tiled=True),
        lax.psum_scatter(value_gradient, "seq", scatter_dimension=1, tiled=True),
    )
    query_low = query_gradient.astype(jnp.bfloat16)
    memory_pair = jnp.concatenate([key_gradient, value_gradient], -1).astype(jnp.bfloat16)
    entry_gradient = jnp.concatenate(
        [outer_sum(normed, query_low), outer_sum(memory_low, memory_pair)], 1
    )
    normed_gradient = project_back(query_low, entry_matrix[:, :model_width])
    memory_gradient = project_back(memory_pair, entry_matrix[:, model_width:])
    input_gradient, gain_gradient, offset_gradient = jax.vjp(layer_norm, inputs, gain_vec, offset)[
        1
    ](normed_gradient)
    bias_gradient = jnp.stack(
        [jnp.sum(query_gradient, axis=(0, 1)), jnp.sum(value_gradient, axis=(0, 1)), exit_bias]
    )
    return (
        incoming + input_gradient,
        memory_gradient,
        (entry_gradient, exit_gradient),
        gain_gradient,
        offset_gradient,
        bias_gradient,
    )


def feedforward_forward(inputs, gain_vec, offset, weights, entry_bias, exit_bias):
    entry_matrix, exit_matrix = weights
    normed = layer_norm(inputs, gain_vec, offset).astype(jnp.bfloat16)
    hidden = project(normed, entry_matrix) + entry_bias
    active = gelu_exact(hidden).astype(jnp.bfloat16)
    result = inputs + project(active, exit_matrix) + exit_bias
    return (result, (normed, hidden, active))


def feedforward_backward(incoming, inputs, gain_vec, offset, weights, stored):
    entry_matrix, exit_matrix = weights
    normed, hidden, active = stored
    incoming_low = incoming.astype(jnp.bfloat16)
    exit_gradient = outer_sum(active, incoming_low)
    exit_bias = jnp.sum(incoming, axis=(0, 1))
    active_gradient = project_back(incoming_low, exit_matrix)
    hidden_gradient = jax.vjp(gelu_exact, hidden)[1](active_gradient)[0]
    entry_bias = jnp.sum(hidden_gradient, axis=(0, 1))
    hidden_low = hidden_gradient.astype(jnp.bfloat16)
    entry_gradient = outer_sum(normed, hidden_low)
    normed_gradient = project_back(hidden_low, entry_matrix)
    input_gradient, gain_gradient, offset_gradient = jax.vjp(layer_norm, inputs, gain_vec, offset)[
        1
    ](normed_gradient)
    return (
        incoming + input_gradient,
        (entry_gradient, exit_gradient),
        gain_gradient,
        offset_gradient,
        (entry_bias, exit_bias),
    )


def per_device(
    source_tokens,
    target_tokens,
    source_lengths,
    target_lengths,
    projections,
    combiners,
    expanders,
    reducers,
    norm_gains,
    norm_shifts,
    attention_biases,
    expander_biases,
    reducer_biases,
    source_cotangent,
    target_cotangent,
):
    local_count = source_tokens.shape[1]
    first_place = lax.axis_index("seq") * local_count
    row_count = local_count * lax.axis_size("seq")
    padding_segment = source_lengths.shape[1] - 1
    source_whole = segment_ids(source_lengths, row_count)
    target_whole = segment_ids(target_lengths, row_count)
    source_here = lax.dynamic_slice_in_dim(source_whole, first_place, local_count, 1)
    target_here = lax.dynamic_slice_in_dim(target_whole, first_place, local_count, 1)
    places = first_place + jnp.arange(local_count, dtype=jnp.int32)
    causal = places[:, None] >= jnp.arange(row_count, dtype=jnp.int32)[None, :]
    encoder_mask = source_here[:, :, None] == source_whole[:, None, :]
    self_mask = (target_here[:, :, None] == target_whole[:, None, :]) & causal[None]
    cross_mask = target_here[:, :, None] == source_whole[:, None, :]
    source_keep = (source_here < padding_segment).astype(jnp.float32)[:, :, None]
    target_keep = (target_here < padding_segment).astype(jnp.float32)[:, :, None]
    source_in = source_tokens.astype(jnp.float32)
    target_in = target_tokens.astype(jnp.float32)
    encoder_weights = fetch_attention(projections, combiners, 0)
    middle, encoder_stored = self_forward(
        source_in, encoder_mask, norm_gains[0], norm_shifts[0], encoder_weights, attention_biases[0]
    )
    encoder_feed = fetch_feedforward(expanders, reducers, 0)
    memory, encoder_feed_stored = feedforward_forward(
        middle, norm_gains[1], norm_shifts[1], encoder_feed, expander_biases[0], reducer_biases[0]
    )
    memory_low = memory.astype(jnp.bfloat16)
    decoder_weights = fetch_attention(projections, combiners, 1)
    self_out, decoder_stored = self_forward(
        target_in, self_mask, norm_gains[2], norm_shifts[2], decoder_weights, attention_biases[1]
    )
    cross_weights = fetch_attention(projections, combiners, 2)
    cross_out, cross_stored = cross_forward(
        self_out,
        memory_low,
        cross_mask,
        norm_gains[3],
        norm_shifts[3],
        cross_weights,
        attention_biases[2],
    )
    decoder_feed = fetch_feedforward(expanders, reducers, 1)
    decoded, decoder_feed_stored = feedforward_forward(
        cross_out,
        norm_gains[4],
        norm_shifts[4],
        decoder_feed,
        expander_biases[1],
        reducer_biases[1],
    )
    incoming = target_cotangent.astype(jnp.float32) * target_keep
    weights = again_feedforward(expanders, reducers, 1)
    incoming, decoder_feed_grads, gain_four, shift_four, decoder_feed_bias = feedforward_backward(
        incoming, cross_out, norm_gains[4], norm_shifts[4], weights, decoder_feed_stored
    )
    decoder_feed_shares = reduce_weights(decoder_feed_grads)
    weights = again_attention(projections, combiners, 2)
    incoming, memory_gradient, cross_grads, gain_three, shift_three, cross_bias = cross_backward(
        incoming,
        self_out,
        memory_low,
        cross_mask,
        norm_gains[3],
        norm_shifts[3],
        weights,
        cross_stored,
    )
    cross_shares = reduce_weights(cross_grads)
    weights = again_attention(projections, combiners, 1)
    target_gradient, decoder_grads, gain_two, shift_two, decoder_bias = self_backward(
        incoming, target_in, self_mask, norm_gains[2], norm_shifts[2], weights, decoder_stored
    )
    decoder_shares = reduce_weights(decoder_grads)
    incoming = source_cotangent.astype(jnp.float32) * source_keep + memory_gradient
    weights = again_feedforward(expanders, reducers, 0)
    incoming, encoder_feed_grads, gain_one, shift_one, encoder_feed_bias = feedforward_backward(
        incoming, middle, norm_gains[1], norm_shifts[1], weights, encoder_feed_stored
    )
    encoder_feed_shares = reduce_weights(encoder_feed_grads)
    weights = again_attention(projections, combiners, 0)
    source_gradient, encoder_grads, gain_zero, shift_zero, encoder_bias = self_backward(
        incoming, source_in, encoder_mask, norm_gains[0], norm_shifts[0], weights, encoder_stored
    )
    encoder_shares = reduce_weights(encoder_grads)
    summed = lax.psum(
        (
            jnp.stack([gain_zero, gain_one, gain_two, gain_three, gain_four]),
            jnp.stack([shift_zero, shift_one, shift_two, shift_three, shift_four]),
            jnp.stack([encoder_bias, decoder_bias, cross_bias]),
            jnp.stack([encoder_feed_bias[0], decoder_feed_bias[0]]),
            jnp.stack([encoder_feed_bias[1], decoder_feed_bias[1]]),
        ),
        ("batch", "seq"),
    )
    return (
        memory_low,
        decoded.astype(jnp.bfloat16),
        source_gradient,
        target_gradient,
        jnp.stack([encoder_shares[0], decoder_shares[0], cross_shares[0]]),
        jnp.stack([encoder_shares[1], decoder_shares[1], cross_shares[1]]),
        jnp.stack([encoder_feed_shares[0], decoder_feed_shares[0]]),
        jnp.stack([encoder_feed_shares[1], decoder_feed_shares[1]]),
        summed[0],
        summed[1],
        summed[2],
        summed[3],
        summed[4],
    )


def solution(mesh):
    in_specs = (
        P("batch", "seq", None),
        P("batch", "seq", None),
        P("batch", None),
        P("batch", None),
        P(None, "batch", None),
        P(None, "batch", None),
        P(None, "batch", None),
        P(None, "batch", None),
        P(),
        P(),
        P(),
        P(),
        P(),
        P("batch", "seq", None),
        P("batch", "seq", None),
    )
    out_specs = (
        P("batch", "seq", None),
        P("batch", "seq", None),
        P("batch", "seq", None),
        P("batch", "seq", None),
        P(None, "batch", None),
        P(None, "batch", None),
        P(None, "batch", None),
        P(None, "batch", None),
        P(),
        P(),
        P(),
        P(),
        P(),
    )
    return jax.shard_map(
        per_device, mesh=mesh, in_specs=in_specs, out_specs=out_specs, check_vma=False
    )
```

profile of v0, /device:TPU:1, one launch (start us, length us, event | category | flops | bytes accessed | tf_op | source)
XLA Modules:
  0.0 2837.1 jit_solution(8205097029043742013)
XLA Ops:
  12.9 98.5 %all-gather.39.cloned.1.call-done = bf16[1,1024,3072]{2,1,0:T(8,128)(2,1)} async-done(((bf16[1,128,3072]{2,1,0:T(8,128)(2,1)}), bf16[1,1024,3072]{2,1,0:T(8,128)(2,1)}) %all-gather.39.cloned.1.call-update) | async-done | bytes 6291472 | tf_op jit(solution)/shard_map/all_gather | solution.py:115
  130.6 80.8 %all-gather.47.cloned.1.call-done = bf16[1,1024,3072]{2,1,0:T(8,128)(2,1)} async-done(((bf16[1,128,3072]{2,1,0:T(8,128)(2,1)}), bf16[1,1024,3072]{2,1,0:T(8,128)(2,1)}) %all-gather.47.cloned.1.call-update) | async-done | bytes 6291472 | tf_op jit(solution)/shard_map/all_gather | solution.py:115
  271.9 37.3 %all-gather.41.cloned.1.call-done = bf16[1,1024,1024]{2,1,0:T(8,128)(2,1)} async-done(((bf16[1,128,1024]{2,1,0:T(8,128)(2,1)}), bf16[1,1024,1024]{2,1,0:T(8,128)(2,1)}) %all-gather.41.cloned.1.call-update) | async-done | bytes 2097168 | tf_op jit(solution)/shard_map/all_gather | solution.py:116
  312.0 123.8 %all-gather.43.cloned.1.call-done = bf16[1,1024,4096]{2,1,0:T(8,128)(2,1)} async-done(((bf16[1,128,4096]{2,1,0:T(8,128)(2,1)}), bf16[1,1024,4096]{2,1,0:T(8,128)(2,1)}) %all-gather.43.cloned.1.call-update) | async-done | bytes 8388624 | tf_op jit(solution)/shard_map/all_gather | solution.py:122
  435.8 16.3 multiply_convert_fusion.6
  452.1 109.6 %all-gather.45.cloned.1.call-done = bf16[1,4096,1024]{2,1,0:T(8,128)(2,1)} async-done(((bf16[1,512,1024]{2,1,0:T(8,128)(2,1)}), bf16[1,4096,1024]{2,1,0:T(8,128)(2,1)}) %all-gather.45.cloned.1.call-update) | async-done | bytes 8388624 | tf_op jit(solution)/shard_map/all_gather | solution.py:123
  568.0 93.0 %all-gather.51.cloned.1.call-done = bf16[1,1024,3072]{2,1,0:T(8,128)(2,1)} async-done(((bf16[1,128,3072]{2,1,0:T(8,128)(2,1)}), bf16[1,1024,3072]{2,1,0:T(8,128)(2,1)}) %all-gather.51.cloned.1.call-update) | async-done | bytes 6291472 | tf_op jit(solution)/shard_map/all_gather | solution.py:115
  671.0 13.3 all-gather.31.cloned.1.call-done
  688.5 19.9 all-gather.33.cloned.1.call-done
  726.0 32.3 %all-gather.49.cloned.1.call-done = bf16[1,1024,1024]{2,1,0:T(8,128)(2,1)} async-done(((bf16[1,128,1024]{2,1,0:T(8,128)(2,1)}), bf16[1,1024,1024]{2,1,0:T(8,128)(2,1)}) %all-gather.49.cloned.1.call-update) | async-done | bytes 2097168 | tf_op jit(solution)/shard_map/all_gather | solution.py:116
  764.4 17.9 all-gather.37.cloned.1.call-done
  785.2 21.9 all-gather.35.cloned.1.call-done
  827.1 29.8 %all-gather.53.cloned.1.call-done = bf16[1,1024,1024]{2,1,0:T(8,128)(2,1)} async-done(((bf16[1,128,1024]{2,1,0:T(8,128)(2,1)}), bf16[1,1024,1024]{2,1,0:T(8,128)(2,1)}) %all-gather.53.cloned.1.call-update) | async-done | bytes 2097168 | tf_op jit(solution)/shard_map/all_gather | solution.py:116
  859.6 124.0 %all-gather.55.cloned.1.call-done = bf16[1,1024,4096]{2,1,0:T(8,128)(2,1)} async-done(((bf16[1,128,4096]{2,1,0:T(8,128)(2,1)}), bf16[1,1024,4096]{2,1,0:T(8,128)(2,1)}) %all-gather.55.cloned.1.call-update) | async-done | bytes 8388624 | tf_op jit(solution)/shard_map/all_gather | solution.py:122
  983.6 16.6 multiply_convert_fusion.5
  1000.2 109.0 %all-gather.57.cloned.1.call-done = bf16[1,4096,1024]{2,1,0:T(8,128)(2,1)} async-done(((bf16[1,512,1024]{2,1,0:T(8,128)(2,1)}), bf16[1,4096,1024]{2,1,0:T(8,128)(2,1)}) %all-gather.57.cloned.1.call-update) | async-done | bytes 8388624 | tf_op jit(solution)/shard_map/all_gather | solution.py:123
  1142.2 14.7 multiply_reduce_fusion.2
  1156.9 13.1 multiply_convert_fusion.2
  1204.6 14.3 multiply_reduce_fusion
  1278.0 13.6 multiply_reduce_fusion.1
  1405.5 33.6 %reduce-scatter.39.cloned.1.call-done = bf16[128,1024]{1,0:T(8,128)(2,1)} async-done(((bf16[1024,1024]{1,0:T(8,128)(2,1)}), bf16[128,1024]{1,0:T(8,128)(2,1)}) %reduce-scatter.39.cloned.1.call-update) | async-done | bytes 262160 | tf_op jit(solution)/shard_map/reduce_scatter | solution.py:146
  1439.0 70.4 %reduce-scatter.37.cloned.1.call-done = bf16[128,1024]{1,0:T(8,128)(2,1)} async-done(((bf16[1024,1024]{1,0:T(8,128)(2,1)}), bf16[128,1024]{1,0:T(8,128)(2,1)}) %reduce-scatter.37.cloned.1.call-update) | async-done | bytes 262160 | tf_op jit(solution)/shard_map/reduce_scatter | solution.py:146
  1509.4 70.5 %reduce-scatter.35.cloned.1.call-done = bf16[128,1024]{1,0:T(8,128)(2,1)} async-done(((bf16[1024,1024]{1,0:T(8,128)(2,1)}), bf16[128,1024]{1,0:T(8,128)(2,1)}) %reduce-scatter.35.cloned.1.call-update) | async-done | bytes 262160 | tf_op jit(solution)/shard_map/reduce_scatter | solution.py:146
  1579.9 153.4 %reduce-scatter.43.cloned.1.call-done = bf16[128,4096]{1,0:T(8,128)(2,1)} async-done(((bf16[1024,4096]{1,0:T(8,128)(2,1)}), bf16[128,4096]{1,0:T(8,128)(2,1)}) %reduce-scatter.43.cloned.1.call-update) | async-done | bytes 1048592 | tf_op jit(solution)/shard_map/reduce_scatter | solution.py:143
  1733.3 151.9 %reduce-scatter.47.cloned.1.call-done = bf16[512,1024]{1,0:T(8,128)(2,1)} async-done(((bf16[4096,1024]{1,0:T(8,128)(2,1)}), bf16[512,1024]{1,0:T(8,128)(2,1)}) %reduce-scatter.47.cloned.1.call-update) | async-done | bytes 1048592 | tf_op jit(solution)/shard_map/reduce_scatter | solution.py:146
  1885.2 119.7 %reduce-scatter.31.cloned.1.call-done = bf16[128,3072]{1,0:T(8,128)(2,1)} async-done(((bf16[1024,3072]{1,0:T(8,128)(2,1)}), bf16[128,3072]{1,0:T(8,128)(2,1)}) %reduce-scatter.31.cloned.1.call-update) | async-done | bytes 786448 | tf_op jit(solution)/shard_map/reduce_scatter | solution.py:143
  2004.9 120.7 %reduce-scatter.33.cloned.1.call-done = bf16[128,3072]{1,0:T(8,128)(2,1)} async-done(((bf16[1024,3072]{1,0:T(8,128)(2,1)}), bf16[128,3072]{1,0:T(8,128)(2,1)}) %reduce-scatter.33.cloned.1.call-update) | async-done | bytes 786448 | tf_op jit(solution)/shard_map/reduce_scatter | solution.py:143
  2125.6 120.6 %reduce-scatter.29.cloned.1.call-done = bf16[128,3072]{1,0:T(8,128)(2,1)} async-done(((bf16[1024,3072]{1,0:T(8,128)(2,1)}), bf16[128,3072]{1,0:T(8,128)(2,1)}) %reduce-scatter.29.cloned.1.call-update) | async-done | bytes 786448 | tf_op jit(solution)/shard_map/reduce_scatter | solution.py:143
  2246.2 152.6 %reduce-scatter.41.cloned.1.call-done = bf16[128,4096]{1,0:T(8,128)(2,1)} async-done(((bf16[1024,4096]{1,0:T(8,128)(2,1)}), bf16[128,4096]{1,0:T(8,128)(2,1)}) %reduce-scatter.41.cloned.1.call-update) | async-done | bytes 1048592 | tf_op jit(solution)/shard_map/reduce_scatter | solution.py:143
  2398.8 152.1 %reduce-scatter.45.cloned.1.call-done = bf16[512,1024]{1,0:T(8,128)(2,1)} async-done(((bf16[4096,1024]{1,0:T(8,128)(2,1)}), bf16[512,1024]{1,0:T(8,128)(2,1)}) %reduce-scatter.45.cloned.1.call-update) | async-done | bytes 1048592 | tf_op jit(solution)/shard_map/reduce_scatter | solution.py:146
  2566.7 124.0 %all-reduce.7.cloned.1.call-done = (bf16[1,128,3072]{2,1,0:T(8,128)(2,1)}, bf16[1,128,3072]{2,1,0:T(8,128)(2,1)}, bf16[1,128,3072]{2,1,0:T(8,128)(2,1)}, bf16[1,...) async-done(((bf16[1,128,3072]{2,1,0:T(8,128)(2,1)}, ...) | async-done | bytes 7340048 | tf_op jit(solution)/shard_map/psum | solution.py:151
  2701.2 122.0 %all-reduce.5.cloned.1.call-done = (f32[5,1024]{1,0:T(8,128)}, f32[5,1024]{1,0:T(8,128)}, f32[3,3,1024]{2,1,0:T(4,128)}, f32[2,4096]{1,0:T(2,128)}, f32[2,1024]{1,0:T(2,128)}) async-done(((f32[5,1024]{1,0:T(8,128)}, f32[5,1024]{1,0:T(8,128)}, f32[3,3,1024]{2,1,0:T(4,128)}, f32[2,4096]{1,0:T(2,128)}, f32[2,1024]{1,0:T(2,128)}), (f32[5,1024]{1,0:T(8,128)}, f32[5,1024]{1,0:T(8,128)}, f32[3,3,1024]{2,1,0:T(4,128)}, ...) | async-done | bytes 118800 | tf_op jit(solution)/shard_map/psum | solution.py:399
  (502 shorter events, 429.5 us)
Async XLA Ops:
  7.2 104.2 %all-gather.39.cloned.1.call-start = ((), (), s32[]{:S(2)}) async-start(), calls=%async_computation.38 | async-start | bytes 7077888 | tf_op jit(solution)/shard_map/all_gather | solution.py:115
  10.4 201.1 %all-gather.47.cloned.1.call-start = ((), (), s32[]{:S(2)}) async-start(), calls=%async_computation.42 | async-start | bytes 7077888 | tf_op jit(solution)/shard_map/all_gather | solution.py:115
  11.1 223.6 %all-gather.29.cloned.1.call-start = ((), (), s32[]{:S(2)}) async-start(), calls=%async_computation.17 | async-start | bytes 2621440 | tf_op jit(solution)/shard_map/all_gather | solution.py:165
  118.7 140.6 %all-gather.27.cloned.1.call-start = ((), (), s32[]{:S(2)}) async-start(), calls=%async_computation.16 | async-start | bytes 2621440 | tf_op jit(solution)/shard_map/all_gather | solution.py:166
  122.4 186.7 %all-gather.41.cloned.1.call-start = ((), (), s32[]{:S(2)}) async-start(), calls=%async_computation.39 | async-start | bytes 2359296 | tf_op jit(solution)/shard_map/all_gather | solution.py:116
  124.6 311.2 %all-gather.43.cloned.1.call-start = ((), (), s32[]{:S(2)}) async-start(), calls=%async_computation.40 | async-start | bytes 9437184 | tf_op jit(solution)/shard_map/all_gather | solution.py:122
  126.2 435.5 %all-gather.45.cloned.1.call-start = ((), (), s32[]{:S(2)}) async-start(), calls=%async_computation.41 | async-start | bytes 9437184 | tf_op jit(solution)/shard_map/all_gather | solution.py:123
  129.3 531.7 %all-gather.51.cloned.1.call-start = ((), (), s32[]{:S(2)}) async-start(), calls=%async_computation.44 | async-start | bytes 7077888 | tf_op jit(solution)/shard_map/all_gather | solution.py:115
  130.1 554.2 %all-gather.31.cloned.1.call-start = ((), (), s32[]{:S(2)}) async-start(), calls=%async_computation.18 | async-start | bytes 2621440 | tf_op jit(solution)/shard_map/all_gather | solution.py:166
  219.1 489.2 %all-gather.33.cloned.1.call-start = ((), (), s32[]{:S(2)}) async-start(), calls=%async_computation.19 | async-start | bytes 2621440 | tf_op jit(solution)/shard_map/all_gather | solution.py:165
  221.4 536.9 %all-gather.49.cloned.1.call-start = ((), (), s32[]{:S(2)}) async-start(), calls=%async_computation.43 | async-start | bytes 2359296 | tf_op jit(solution)/shard_map/all_gather | solution.py:116
  222.1 560.2 %all-gather.37.cloned.1.call-start = ((), (), s32[]{:S(2)}) async-start(), calls=%async_computation.21 | async-start | bytes 2621440 | tf_op jit(solution)/shard_map/all_gather | solution.py:182
  666.7 140.4 %all-gather.35.cloned.1.call-start = ((), (), s32[]{:S(2)}) async-start(), calls=%async_computation.20 | async-start | bytes 2621440 | tf_op jit(solution)/shard_map/all_gather | solution.py:183
  669.0 187.9 %all-gather.53.cloned.1.call-start = ((), (), s32[]{:S(2)}) async-start(), calls=%async_computation.45 | async-start | bytes 2359296 | tf_op jit(solution)/shard_map/all_gather | solution.py:116
  669.6 314.0 %all-gather.55.cloned.1.call-start = ((), (), s32[]{:S(2)}) async-start(), calls=%async_computation.46 | async-start | bytes 9437184 | tf_op jit(solution)/shard_map/all_gather | solution.py:122
  670.1 439.1 %all-gather.57.cloned.1.call-start = ((), (), s32[]{:S(2)}) async-start(), calls=%async_computation.47 | async-start | bytes 9437184 | tf_op jit(solution)/shard_map/all_gather | solution.py:123
  670.7 564.9 %reduce-scatter.19.cloned.1.call-start = ((), (), s32[]{:S(2)}) async-start(), calls=%async_computation.23 | async-start | bytes 5242880 | tf_op jit(solution)/shard_map/reduce_scatter | solution.py:241
  1174.7 167.5 %reduce-scatter.27.cloned.1.call-start = ((), (), s32[]{:S(2)}) async-start(), calls=%async_computation.27 | async-start | bytes 2621440 | tf_op jit(solution)/shard_map/reduce_scatter | solution.py:204
  1204.1 138.1 %reduce-scatter.25.cloned.1.call-start = ((), (), s32[]{:S(2)}) async-start(), calls=%async_computation.26 | async-start | bytes 2621440 | tf_op jit(solution)/shard_map/reduce_scatter | solution.py:201
  1235.4 129.1 %reduce-scatter.23.cloned.1.call-start = ((), (), s32[]{:S(2)}) async-start(), calls=%async_computation.25 | async-start | bytes 2621440 | tf_op jit(solution)/shard_map/reduce_scatter | solution.py:204
  1308.0 131.0 %reduce-scatter.39.cloned.1.call-start = ((), (), s32[]{:S(2)}) async-start(), calls=%async_computation.33 | async-start | bytes 2359296 | tf_op jit(solution)/shard_map/reduce_scatter | solution.py:146
  1311.8 197.6 %reduce-scatter.37.cloned.1.call-start = ((), (), s32[]{:S(2)}) async-start(), calls=%async_computation.32 | async-start | bytes 2359296 | tf_op jit(solution)/shard_map/reduce_scatter | solution.py:146
  1315.4 264.5 %reduce-scatter.35.cloned.1.call-start = ((), (), s32[]{:S(2)}) async-start(), calls=%async_computation.31 | async-start | bytes 2359296 | tf_op jit(solution)/shard_map/reduce_scatter | solution.py:146
  1318.9 414.4 %reduce-scatter.43.cloned.1.call-start = ((), (), s32[]{:S(2)}) async-start(), calls=%async_computation.35 | async-start | bytes 9437184 | tf_op jit(solution)/shard_map/reduce_scatter | solution.py:143
  1326.7 558.5 %reduce-scatter.47.cloned.1.call-start = ((), (), s32[]{:S(2)}) async-start(), calls=%async_computation.37 | async-start | bytes 9437184 | tf_op jit(solution)/shard_map/reduce_scatter | solution.py:146
  1334.6 670.3 %reduce-scatter.31.cloned.1.call-start = ((), (), s32[]{:S(2)}) async-start(), calls=%async_computation.29 | async-start | bytes 7077888 | tf_op jit(solution)/shard_map/reduce_scatter | solution.py:143
  1348.9 776.7 %reduce-scatter.33.cloned.1.call-start = ((), (), s32[]{:S(2)}) async-start(), calls=%async_computation.30 | async-start | bytes 7077888 | tf_op jit(solution)/shard_map/reduce_scatter | solution.py:143
  1357.4 888.8 %reduce-scatter.29.cloned.1.call-start = ((), (), s32[]{:S(2)}) async-start(), calls=%async_computation.28 | async-start | bytes 7077888 | tf_op jit(solution)/shard_map/reduce_scatter | solution.py:143
  1374.6 1024.2 %reduce-scatter.41.cloned.1.call-start = ((), (), s32[]{:S(2)}) async-start(), calls=%async_computation.34 | async-start | bytes 9437184 | tf_op jit(solution)/shard_map/reduce_scatter | solution.py:143
  1382.7 1168.2 %reduce-scatter.45.cloned.1.call-start = ((), (), s32[]{:S(2)}) async-start(), calls=%async_computation.36 | async-start | bytes 9437184 | tf_op jit(solution)/shard_map/reduce_scatter | solution.py:146
  1391.2 1299.6 %all-reduce.7.cloned.1.call-start = ((), (), s32[]{:S(2)}) async-start(), calls=%async_computation.49 | async-start | bytes 14680064 | tf_op jit(solution)/shard_map/psum | solution.py:151
  2551.0 272.2 %all-reduce.5.cloned.1.call-start = ((), (), s32[]{:S(2)}) async-start(), calls=%async_computation.48 | async-start | bytes 311296 | tf_op jit(solution)/shard_map/psum | solution.py:399
  (138 other events, 6598.2 us)
Sparse Core Ops, SparseCore 0:
  10.8 100.5 all-gather.38
  114.2 97.2 all-gather.46
  236.7 22.5 all-gather.26
  261.3 47.7 all-gather.40
  311.7 124.1 all-gather.42
  438.5 123.1 all-gather.44
  563.9 97.1 all-gather.50
  685.7 22.5 all-gather.32
  710.5 47.7 all-gather.48
  759.7 22.5 all-gather.36
  784.5 22.5 all-gather.34
  809.1 47.7 all-gather.52
  859.4 124.1 all-gather.54
  986.1 123.0 all-gather.56
  1141.2 43.0 reduce-scatter.18
  1186.9 44.5 reduce-scatter.16
  1234.0 31.4 reduce-scatter.26
  1267.9 31.4 reduce-scatter.24
  1302.5 31.4 reduce-scatter.22
  1337.2 31.4 reduce-scatter.20
  1372.8 66.1 reduce-scatter.38
  1442.4 66.9 reduce-scatter.36
  1512.9 66.9 reduce-scatter.34
  1583.4 149.8 reduce-scatter.42
  1737.2 147.9 reduce-scatter.46
  1888.8 116.0 reduce-scatter.30
  2008.5 117.0 reduce-scatter.32
  2129.1 117.0 reduce-scatter.28
  2249.8 148.9 reduce-scatter.40
  2402.9 147.9 reduce-scatter.44
  2553.9 136.8 all-reduce.6
  2697.8 125.4 all-reduce.4
  (2 shorter events, 43.2 us)
where the time goes:
time: 2840 us
  waiting for transfers between devices  2320 us (82%)
  matrix products  324 us (11%)
  other arithmetic  89.3 us (3%)
  local copies, waits for them, and re-layouts  79.5 us (3%)
    reduce_scatter x5, waiting for transfers between devices, reduce_weights(): lax.psum_scatter(gradients[0].astype(jnp.bfloat16), 'batch', scatter_dime...  667 us
    reduce_scatter x5, waiting for transfers between devices, reduce_weights(): lax.psum_scatter(gradients[1].astype(jnp.bfloat16), 'batch', scatter_dime...  478 us
    all_gather x3, waiting for transfers between devices, fetch_attention(): lax.all_gather(projections[block_id], 'batch', axis=0, tiled=True)  272 us
    all_gather x2, waiting for transfers between devices, fetch_feedforward(): lax.all_gather(expanders[block_id], 'batch', axis=0, tiled=True)  248 us
    all_gather x2, waiting for transfers between devices, fetch_feedforward(): lax.all_gather(reducers[block_id], 'batch', axis=0, tiled=True)  219 us
    psum x1, waiting for transfers between devices, reduce_weights(): lax.psum(shares[0].astype(jnp.bfloat16), 'seq').astype(jnp.float32)  124 us
    psum x1, waiting for transfers between devices, per_device(): lax.psum((jnp.stack([gain_zero, gain_one, gain_two, gain_three, gain_four...  122 us
    all_gather x3, waiting for transfers between devices, fetch_attention(): lax.all_gather(combiners[block_id], 'batch', axis=0, tiled=True)  99.4 us
  transfers between devices with their start and end apart: 34, of which 29 were waited for; matrix products, arithmetic and copies ran while one was open for 15% of the time, Pallas kernels for 0%

commit v1 on v0

v1 whole, which is shorter than its diff:
```python
import jax
import jax.numpy as jnp
from jax import lax
from jax.sharding import PartitionSpec as P

HEADS = 16


epsilon = 1e-05
masked_score = -1e30
low = jnp.bfloat16


def layer_norm(values, gain_vec, offset):
    middle = jnp.mean(values, -1, keepdims=True)
    centred = values - middle
    spread_out = jnp.mean(centred * centred, -1, keepdims=True)
    return centred * lax.rsqrt(spread_out + epsilon) * gain_vec + offset


def gelu_exact(values):
    return jax.nn.gelu(values, approximate=False)


def times(left, right):
    return jnp.einsum("sd,de->se", left, right, preferred_element_type=jnp.float32)


def times_back(incoming, weight):
    return jnp.einsum("se,de->sd", incoming, weight, preferred_element_type=jnp.float32)


def outer_sum(left, incoming):
    return jnp.einsum("sd,se->de", left, incoming, preferred_element_type=jnp.float32)


def seq_bits():
    bit, bits = lax.axis_size("seq") >> 1, []
    while bit:
        bits.append(bit)
        bit >>= 1
    return bits


def seq_offsets():
    offsets = [0]
    for bit in seq_bits():
        offsets = offsets + [offset ^ bit for offset in offsets]
    return offsets


def swap(values, bit, axis="seq"):
    return lax.ppermute(values, axis, [(i, i ^ bit) for i in range(lax.axis_size(axis))])


def spread(rows):
    for bit in seq_bits():
        rows = jnp.concatenate([rows, swap(rows, bit)], 0)
    return rows


def collect(partial):
    for bit in reversed(seq_bits()):
        half = partial.shape[0] // 2
        arrived = swap(partial[half:].astype(low), bit)
        partial = partial[:half].astype(jnp.float32) + arrived.astype(jnp.float32)
    return partial


def in_order(spread_blocks):
    me = lax.axis_index("seq")
    offsets = jnp.array([seq_offsets().index(i) for i in range(lax.axis_size("seq"))], jnp.int32)
    return [
        lax.dynamic_index_in_dim(spread_blocks, offsets[me ^ i], 0, keepdims=False)
        for i in range(lax.axis_size("seq"))
    ]


def sum_everywhere(values):
    for axis in ("seq", "batch"):
        bit = 1
        while bit < lax.axis_size(axis):
            values = values + swap(values, bit, axis)
            bit <<= 1
    return values


def mine(values, axis):
    return lax.dynamic_index_in_dim(values, lax.axis_index("seq"), axis, keepdims=False)


def gather_batch(values):
    return lax.all_gather(values, "batch", axis=0, tiled=False)


def scatter_batch(values):
    return lax.psum_scatter(values, "batch", scatter_dimension=0, tiled=False)


def deals_by_line():
    return lax.axis_size("batch") == 2 * lax.axis_size("seq")


def line_pairs(step, count, back):
    pairs = []
    for place in range(count):
        for side in range(2):
            here = (place * 2 + side) * count + place
            there = (((place + step) % count) * 2 + side) * count + place
            pairs.append((there, here) if back else (here, there))
    return pairs


def deal_combiners(combiners):
    count = lax.axis_size("seq")
    me = lax.axis_index("seq")
    place = lax.axis_index("batch") // 2
    rows = combiners.shape[1] // count
    parts = combiners.reshape(combiners.shape[0], count, rows, combiners.shape[2])
    own = lax.dynamic_index_in_dim(parts, me, 1, keepdims=False)
    piece = jnp.where(place == me, own, jnp.zeros_like(own))
    for step in range(1, count):
        sent = lax.dynamic_index_in_dim(parts, (me + step) % count, 1, keepdims=False)
        piece = piece + lax.ppermute(sent, ("batch", "seq"), line_pairs(step, count, False))
    return piece


def return_combiners(pieces):
    count = lax.axis_size("seq")
    me = lax.axis_index("seq")
    place = lax.axis_index("batch") // 2
    arrived = [pieces] + [
        lax.ppermute(pieces, ("batch", "seq"), line_pairs(step, count, True))
        for step in range(1, count)
    ]
    ring = jnp.stack(arrived + arrived[:-1], 1)
    ordered = lax.dynamic_slice_in_dim(ring, (count - me) % count, count, 1)
    ordered = ordered.reshape(pieces.shape[0], count * pieces.shape[1], pieces.shape[2])
    for bit in seq_bits():
        ordered = jnp.where((place & bit) == (me & bit), ordered, swap(ordered, bit))
    return ordered


def pack_lanes(piece, rows):
    lanes = piece.shape[0] * piece.shape[1] // rows
    return piece.reshape(piece.shape[0], -1, lanes).transpose(1, 0, 2).reshape(rows, lanes)


def unpack_lanes(packed, rows):
    lanes = packed.shape[1]
    return packed.reshape(-1, rows, lanes).transpose(1, 0, 2).reshape(rows, -1)


def fetch_attention(projections, combiner, dealt):
    count = lax.axis_size("seq")
    rows, width = projections.shape
    share = mine(projections.reshape(rows, 3, count, width // 3 // count), 2).reshape(rows, -1)
    if dealt is None:
        entry = gather_batch(share).reshape(-1, share.shape[1])
        whole = gather_batch(combiner).reshape(count, -1, combiner.shape[1])
        return entry, mine(whole, 0)
    packed = gather_batch(jnp.concatenate([share, pack_lanes(dealt, rows)], 1))
    entry = packed[..., : share.shape[1]].reshape(-1, share.shape[1])
    pieces = packed[..., share.shape[1] :]
    lanes = pieces.shape[-1]
    pieces = pieces.reshape(count, 2, -1, dealt.shape[0], lanes)
    leave = pieces.transpose(1, 0, 3, 2, 4).reshape(-1, dealt.shape[1])
    return entry, leave


def fetch_feedforward(expander, reducer):
    count = lax.axis_size("seq")
    rows, width = expander.shape
    shards = lax.axis_size("batch")
    share_in = mine(expander.reshape(rows, shards, count, -1), 2).reshape(rows, -1)
    share_out = mine(reducer.reshape(count, -1, reducer.shape[1]), 0)
    if share_in.shape[1] != share_out.shape[1]:
        entry = gather_batch(share_in)
        leave = gather_batch(share_out)
    else:
        packed = gather_batch(jnp.concatenate([share_in, share_out], 0))
        entry, leave = packed[:, :rows], packed[:, rows:]
    return entry.reshape(-1, share_in.shape[1]), leave.reshape(-1, share_out.shape[1])


def send_attention(entry_gradient, exit_gradient):
    shards, count = lax.axis_size("batch"), lax.axis_size("seq")
    entry = entry_gradient.astype(low).reshape(shards, -1, entry_gradient.shape[1])
    if not deals_by_line():
        width = exit_gradient.shape[1]
        me = lax.axis_index("seq")
        whole = jnp.zeros((count,) + exit_gradient.shape, low)
        whole = lax.dynamic_update_slice(whole, exit_gradient.astype(low)[None], (me, 0, 0))
        leave = scatter_batch(whole.reshape(shards, -1, width))
        return scatter_batch(entry), leave
    rows = entry.shape[1]
    piece_rows = exit_gradient.shape[0] // shards
    lanes = piece_rows * exit_gradient.shape[1] // rows
    leave = exit_gradient.astype(low).reshape(2, count, piece_rows, -1, lanes)
    leave = leave.transpose(1, 0, 3, 2, 4).reshape(shards, rows, lanes)
    packed = scatter_batch(jnp.concatenate([entry, leave], 2))
    return packed[:, : entry.shape[2]], unpack_lanes(packed[:, entry.shape[2] :], piece_rows)


def send_feedforward(entry_gradient, exit_gradient):
    shards = lax.axis_size("batch")
    entry = entry_gradient.astype(low).reshape(shards, -1, entry_gradient.shape[1])
    leave = exit_gradient.astype(low).reshape(shards, -1, exit_gradient.shape[1])
    if entry.shape[2] != leave.shape[2]:
        return scatter_batch(entry), scatter_batch(leave)
    packed = scatter_batch(jnp.concatenate([entry, leave], 1))
    return packed[: entry.shape[1]], packed[entry.shape[1] :]


def finish_weights(attention_parts, feedforward_parts):
    shards, count = lax.axis_size("batch"), lax.axis_size("seq")
    entries = jnp.stack([part[0] for part in attention_parts])
    leaves = jnp.stack([part[1] for part in attention_parts])
    expands = jnp.stack([part[0] for part in feedforward_parts])
    reduces = jnp.stack([part[1] for part in feedforward_parts])
    if deals_by_line():
        leaves = return_combiners(leaves)
    else:
        leaves = lax.psum(leaves, "seq")
    entry_all = in_order(spread(entries[None]))
    expand_all = in_order(spread(expands[None]))
    reduce_all = in_order(spread(reduces[None]))
    blocks, rows, width = entries.shape
    projections = jnp.stack([part.reshape(blocks, rows, 3, width // 3) for part in entry_all], 3)
    blocks_out, rows_out, width_out = expands.shape
    expanders = jnp.stack(
        [part.reshape(blocks_out, rows_out, shards, width_out // shards) for part in expand_all], 3
    )
    reducers = jnp.stack(reduce_all, 1)
    return (
        projections.reshape(blocks, rows, -1).astype(jnp.float32),
        leaves.astype(jnp.float32),
        expanders.reshape(blocks_out, rows_out, -1).astype(jnp.float32),
        reducers.reshape(reduces.shape[0], -1, reduces.shape[2]).astype(jnp.float32),
    )


def split_heads(values, width):
    return values.reshape(values.shape[0], values.shape[1] // width, width)


def attend_forward(queries, keys, values, key_mask, width):
    factor = float(width) ** (-0.5)
    raw_scores = (
        jnp.einsum(
            "qhc,khc->hqk",
            split_heads(queries, width),
            split_heads(keys, width),
            preferred_element_type=jnp.float32,
        )
        * factor
    )
    scores = jnp.where(key_mask[None], raw_scores, masked_score)
    row_max = jnp.max(scores, -1, keepdims=True)
    exponent = jnp.exp(scores - row_max)
    row_sum = jnp.sum(exponent, -1, keepdims=True)
    weights = (exponent / row_sum).astype(low)
    mixture = jnp.einsum(
        "hqk,khc->qhc", weights, split_heads(values, width), preferred_element_type=jnp.float32
    )
    return (mixture.reshape(queries.shape).astype(low), row_max + jnp.log(row_sum))


def attend_backward(queries, keys, values, key_mask, log_total, mixture_gradient, width):
    factor = float(width) ** (-0.5)
    query_heads = split_heads(queries, width)
    key_heads = split_heads(keys, width)
    value_heads = split_heads(values, width)
    incoming_heads = split_heads(mixture_gradient, width)
    raw_scores = (
        jnp.einsum("qhc,khc->hqk", query_heads, key_heads, preferred_element_type=jnp.float32)
        * factor
    )
    weights = jnp.where(key_mask[None], jnp.exp(raw_scores - log_total), 0.0)
    value_gradient = jnp.einsum(
        "hqk,qhc->khc", weights.astype(low), incoming_heads, preferred_element_type=jnp.float32
    )
    weight_gradient = jnp.einsum(
        "qhc,khc->hqk", incoming_heads, value_heads, preferred_element_type=jnp.float32
    )
    inner_sum = jnp.sum(weights * weight_gradient, -1, keepdims=True)
    score_gradient = (weights * (weight_gradient - inner_sum)).astype(low)
    query_gradient = (
        jnp.einsum("hqk,khc->qhc", score_gradient, key_heads, preferred_element_type=jnp.float32)
        * factor
    )
    key_gradient = (
        jnp.einsum("hqk,qhc->khc", score_gradient, query_heads, preferred_element_type=jnp.float32)
        * factor
    )
    return (
        query_gradient.reshape(queries.shape),
        key_gradient.reshape(keys.shape),
        value_gradient.reshape(values.shape),
    )


def norm_backward(inputs, gain_vec, offset, incoming, normed_gradient):
    input_gradient, gain_gradient, offset_gradient = jax.vjp(layer_norm, inputs, gain_vec, offset)[
        1
    ](normed_gradient)
    return incoming + input_gradient, gain_gradient, offset_gradient


def per_device(
    source_tokens,
    target_tokens,
    source_lengths,
    target_lengths,
    projections,
    combiners,
    expanders,
    reducers,
    norm_gains,
    norm_shifts,
    attention_biases,
    expander_biases,
    reducer_biases,
    source_cotangent,
    target_cotangent,
):
    source_tokens, target_tokens = source_tokens[0], target_tokens[0]
    source_cotangent, target_cotangent = source_cotangent[0], target_cotangent[0]
    count, shards = lax.axis_size("seq"), lax.axis_size("batch")
    me = lax.axis_index("seq")
    local_count, model_width = source_tokens.shape
    head_width = model_width // HEADS
    share = model_width // count
    padding_segment = source_lengths.shape[1] - 1

    here = jnp.arange(local_count, dtype=jnp.int32)
    places = jnp.concatenate([(me ^ offset) * local_count + here for offset in seq_offsets()])

    def segments(lengths):
        ends = jnp.cumsum(lengths[0], dtype=jnp.int32)
        return jnp.sum((places[:, None] >= ends[None, :]).astype(jnp.int32), -1, dtype=jnp.int32)

    source_segment, target_segment = segments(source_lengths), segments(target_lengths)
    encoder_mask = source_segment[:, None] == source_segment[None, :]
    self_mask = (target_segment[:, None] == target_segment[None, :]) & (
        places[:, None] >= places[None, :]
    )
    cross_mask = target_segment[:, None] == source_segment[None, :]
    source_keep = (source_segment[:local_count] < padding_segment).astype(jnp.float32)[:, None]
    target_keep = (target_segment[:local_count] < padding_segment).astype(jnp.float32)[:, None]

    split_biases = attention_biases.reshape(3, 3, count, share)
    entry_biases = lax.dynamic_index_in_dim(split_biases, me, 2, keepdims=False)
    hidden_biases = mine(expander_biases.reshape(2, shards, count, -1), 2).reshape(2, -1)

    dealt = deal_combiners(combiners) if deals_by_line() else [None] * 3

    source_all = spread(source_tokens)
    target_all = spread(target_tokens)
    target_incoming = target_cotangent.astype(jnp.float32) * target_keep
    target_incoming_all = spread(target_incoming.astype(low))

    source_in = source_tokens.astype(jnp.float32)
    target_in = target_tokens.astype(jnp.float32)

    def attention_weights(block):
        return fetch_attention(projections[block], combiners[block], dealt[block])

    def feedforward_weights(block):
        return fetch_feedforward(expanders[block], reducers[block])

    def attention_exit(inputs, mixture, leave, block):
        return inputs + collect(times(mixture, leave).astype(low)) + attention_biases[block, 2]

    def self_forward(inputs, inputs_all, key_mask, norm, block, weights):
        entry, leave = weights
        normed = layer_norm(
            inputs_all.astype(jnp.float32), norm_gains[norm], norm_shifts[norm]
        ).astype(low)
        projected = times(normed, entry)
        queries = (projected[:, :share] + entry_biases[block, 0]).astype(low)
        keys = projected[:, share : 2 * share].astype(low)
        values = (projected[:, 2 * share :] + entry_biases[block, 1]).astype(low)
        mixture, log_total = attend_forward(queries, keys, values, key_mask, head_width)
        result = attention_exit(inputs, mixture, leave, block)
        return result, (normed, queries, keys, values, log_total, mixture)

    def feedforward_forward(inputs, norm, block, weights):
        entry, leave = weights
        normed = spread(layer_norm(inputs, norm_gains[norm], norm_shifts[norm]).astype(low))
        hidden = times(normed, entry) + hidden_biases[block]
        active = gelu_exact(hidden).astype(low)
        result = inputs + collect(times(active, leave).astype(low)) + reducer_biases[block]
        return result, (normed, hidden, active)

    encoder_weights = attention_weights(0)
    middle, encoder_stored = self_forward(
        source_in, source_all, encoder_mask, 0, 0, encoder_weights
    )
    encoder_feed = feedforward_weights(0)
    decoder_weights = attention_weights(1)
    self_out, decoder_stored = self_forward(target_in, target_all, self_mask, 2, 1, decoder_weights)
    memory, encoder_feed_stored = feedforward_forward(middle, 1, 0, encoder_feed)
    memory_low = memory.astype(low)
    memory_all = spread(memory_low)
    cross_weights = attention_weights(2)
    entry, leave = cross_weights
    cross_normed = spread(layer_norm(self_out, norm_gains[3], norm_shifts[3]).astype(low))
    cross_queries = (times(cross_normed, entry[:, :share]) + entry_biases[2, 0]).astype(low)
    projected = times(memory_all, entry[:, share:])
    cross_keys = projected[:, :share].astype(low)
    cross_values = (projected[:, share:] + entry_biases[2, 1]).astype(low)
    cross_mixture, cross_log_total = attend_forward(
        cross_queries, cross_keys, cross_values, cross_mask, head_width
    )
    cross_out = attention_exit(self_out, cross_mixture, leave, 2)
    decoder_feed = feedforward_weights(1)
    decoded, decoder_feed_stored = feedforward_forward(cross_out, 4, 1, decoder_feed)

    def feedforward_backward(incoming, incoming_all, inputs, norm, weights, stored):
        entry, leave = weights
        normed, hidden, active = stored
        active_gradient = times_back(incoming_all, leave)
        hidden_gradient = jax.vjp(gelu_exact, hidden)[1](active_gradient)[0]
        hidden_low = hidden_gradient.astype(low)
        normed_gradient = collect(times_back(hidden_low, entry).astype(low))
        exit_gradient = outer_sum(active, incoming_all)
        entry_gradient = outer_sum(normed, hidden_low)
        result, gain, shift = norm_backward(
            inputs, norm_gains[norm], norm_shifts[norm], incoming, normed_gradient
        )
        shares = send_feedforward(entry_gradient, exit_gradient)
        return result, shares, (gain, shift), (jnp.sum(hidden_gradient, 0), jnp.sum(incoming, 0))

    def attention_core(incoming, weights, stored, key_mask):
        entry, leave = weights
        queries, keys, values, log_total, mixture = stored
        incoming_all = spread(incoming.astype(low))
        mixture_gradient = times_back(incoming_all, leave).astype(low)
        query_gradient, key_gradient, value_gradient = attend_backward(
            queries, keys, values, key_mask, log_total, mixture_gradient, head_width
        )
        exit_gradient = outer_sum(mixture, incoming_all)
        biases = (jnp.sum(query_gradient, 0), jnp.sum(value_gradient, 0), jnp.sum(incoming, 0))
        gradients = (query_gradient.astype(low), key_gradient.astype(low), value_gradient.astype(low))
        return gradients, exit_gradient, biases

    def self_backward(incoming, inputs, key_mask, norm, weights, stored):
        gradients, exit_gradient, biases = attention_core(incoming, weights, stored[1:], key_mask)
        joined = jnp.concatenate(gradients, -1)
        normed_gradient = collect(times_back(joined, weights[0]).astype(low))
        entry_gradient = outer_sum(stored[0], joined)
        result, gain, shift = norm_backward(
            inputs, norm_gains[norm], norm_shifts[norm], incoming, normed_gradient
        )
        return result, send_attention(entry_gradient, exit_gradient), (gain, shift), biases

    incoming, decoder_feed_shares, norm_four, decoder_feed_bias = feedforward_backward(
        target_incoming, target_incoming_all, cross_out, 4, decoder_feed, decoder_feed_stored
    )
    gradients, exit_gradient, cross_bias = attention_core(
        incoming,
        cross_weights,
        (cross_queries, cross_keys, cross_values, cross_log_total, cross_mixture),
        cross_mask,
    )
    pair = jnp.concatenate(gradients[1:], -1)
    entry = cross_weights[0]
    memory_gradient = collect(times_back(pair, entry[:, share:]).astype(low))
    normed_gradient = collect(times_back(gradients[0], entry[:, :share]).astype(low))
    entry_gradient = jnp.concatenate(
        [outer_sum(cross_normed, gradients[0]), outer_sum(memory_all, pair)], 1
    )
    cross_shares = send_attention(entry_gradient, exit_gradient)
    source_incoming = source_cotangent.astype(jnp.float32) * source_keep + memory_gradient
    incoming, *norm_three = norm_backward(
        self_out, norm_gains[3], norm_shifts[3], incoming, normed_gradient
    )
    middle_incoming, encoder_feed_shares, norm_one, encoder_feed_bias = feedforward_backward(
        source_incoming, spread(source_incoming.astype(low)), middle, 1, encoder_feed, encoder_feed_stored
    )
    target_gradient, decoder_shares, norm_two, decoder_bias = self_backward(
        incoming, target_in, self_mask, 2, decoder_weights, decoder_stored
    )
    source_gradient, encoder_shares, norm_zero, encoder_bias = self_backward(
        middle_incoming, source_in, encoder_mask, 0, encoder_weights, encoder_stored
    )

    weight_gradients = finish_weights(
        (encoder_shares, decoder_shares, cross_shares), (encoder_feed_shares, decoder_feed_shares)
    )

    norms = (norm_zero, norm_one, norm_two, norm_three, norm_four)
    gains = jnp.stack([pair[0] for pair in norms])
    shifts = jnp.stack([pair[1] for pair in norms])
    blocks = (encoder_bias, decoder_bias, cross_bias)
    inner = jnp.stack([jnp.stack(bias[:2]) for bias in blocks])
    inner_whole = lax.dynamic_update_slice(
        jnp.zeros((3, 2, count, share), jnp.float32), inner[:, :, None], (0, 0, me, 0)
    ).reshape(3, 2, model_width)
    outer = jnp.stack([bias[2] for bias in blocks])
    hidden = jnp.stack([encoder_feed_bias[0], decoder_feed_bias[0]]).reshape(2, shards, 1, -1)
    hidden_whole = lax.dynamic_update_slice(
        jnp.zeros((2, shards, count, hidden.shape[3]), jnp.float32), hidden, (0, 0, me, 0)
    )
    exits = jnp.stack([encoder_feed_bias[1], decoder_feed_bias[1]])
    parts = [gains, shifts, inner_whole, outer, hidden_whole, exits]
    summed = sum_everywhere(jnp.concatenate([part.reshape(-1, 128) for part in parts], 0))
    rows = [part.size // 128 for part in parts]
    starts = [sum(rows[:i]) for i in range(len(rows))]
    gains, shifts, inner_whole, outer, hidden_whole, exits = [
        summed[start : start + size].reshape(part.shape)
        for start, size, part in zip(starts, rows, parts)
    ]
    return (
        memory_low[None],
        decoded.astype(low)[None],
        source_gradient[None],
        target_gradient[None],
        *weight_gradients,
        gains,
        shifts,
        jnp.concatenate([inner_whole, outer[:, None]], 1),
        hidden_whole.reshape(2, -1),
        exits,
    )


def solution(mesh):
    in_specs = (
        P("batch", "seq", None),
        P("batch", "seq", None),
        P("batch", None),
        P("batch", None),
        P(None, "batch", None),
        P(None, "batch", None),
        P(None, "batch", None),
        P(None, "batch", None),
        P(),
        P(),
        P(),
        P(),
        P(),
        P("batch", "seq", None),
        P("batch", "seq", None),
    )
    out_specs = (
        P("batch", "seq", None),
        P("batch", "seq", None),
        P("batch", "seq", None),
        P("batch", "seq", None),
        P(None, "batch", None),
        P(None, "batch", None),
        P(None, "batch", None),
        P(None, "batch", None),
        P(),
        P(),
        P(),
        P(),
        P(),
    )
    return jax.shard_map(
        per_device, mesh=mesh, in_specs=in_specs, out_specs=out_specs, check_vma=False
    )
```

time: 2840 us -> 988 us (0.35)
  waiting for transfers between devices: 2320 us -> 308 us
  local copies, waits for them, and re-layouts: 79.5 us -> 171 us
  starting transfers between devices: 3.81 us -> 84 us
  matrix products: 324 us -> 248 us
  other arithmetic: 89.3 us -> 145 us
    reduce_scatter x16 -> x5, waiting for transfers between devices: 1150 us -> 49.3 us  [scatter_batch(): return lax.psum_scatter(values, 'batch', scatter_dimension=0, tiled=False)]
    all_gather x16 -> x5, waiting for transfers between devices: 925 us -> 68.5 us  [gather_batch(): return lax.all_gather(values, 'batch', axis=0, tiled=False)]
    psum x2 -> x0, waiting for transfers between devices: 246 us -> none  [the longest x1 124 us: reduce_weights(): lax.psum(shares[0].astype(jnp.bfloat16), 'seq').astype(jnp.float32)]
    ppermute x0 -> x63, waiting for transfers between devices: none -> 190 us  [the longest x57 188 us: swap(): lax.ppermute(values, axis, [(i, i ^ bit) for i in range(lax.axis_size(axi...]
    ppermute x0 -> x63, starting transfers between devices: none -> 83.2 us  [the longest x57 77.3 us: swap(): lax.ppermute(values, axis, [(i, i ^ bit) for i in range(lax.axis_size(axi...]
    dot_general x51, matrix products: 324 us -> 248 us  [the longest x11 47.3 us: times(): jnp.einsum('sd,de->se', left, right, preferred_element_type=jnp.float32)]
    concatenate x2 -> x29, other arithmetic: 4.7 us -> 37 us  [the longest x17 20.5 us: spread(): rows = jnp.concatenate([rows, swap(rows, bit)], 0)]
    reshape x0 -> x28, local copies, waits for them, and re-layouts: none -> 31.2 us  [the longest x2 8.06 us: send_feedforward(): exit_gradient.astype(low).reshape(shards, -1, exit_gradient.shape[1])]
  transfers between devices with their start and end apart: 34 -> 73, of which waited for: 29 -> 31; matrix products, arithmetic and copies ran while one was open for 15% -> 45% of each run, Pallas kernels for 0% -> 0%
where the time goes in v1:
time: 988 us; the launch traced here: 981 us
  waiting for transfers between devices  308 us (31%)
  matrix products  248 us (25%)
  local copies, waits for them, and re-layouts  171 us (17%)
  other arithmetic  145 us (15%)
  starting transfers between devices  84 us (9%)
  between operations  26.5 us (3%)
    ppermute x57, waiting for transfers between devices, swap(): lax.ppermute(values, axis, [(i, i ^ bit) for i in range(lax.axis_size(axi...  188 us
    ppermute x57, starting transfers between devices, swap(): lax.ppermute(values, axis, [(i, i ^ bit) for i in range(lax.axis_size(axi...  77.3 us
    all_gather x5, waiting for transfers between devices, gather_batch(): return lax.all_gather(values, 'batch', axis=0, tiled=False)  68.5 us
    unnamed x571, local copies, waits for them, and re-layouts  63.3 us
    reduce_scatter x5, waiting for transfers between devices, scatter_batch(): return lax.psum_scatter(values, 'batch', scatter_dimension=0, tiled=False)  49.3 us
    dot_general x11, matrix products, times(): jnp.einsum('sd,de->se', left, right, preferred_element_type=jnp.float32)  47.3 us
    dot_general x3, matrix products, attend_backward(): jnp.einsum('qhc,khc->hqk', incoming_heads, value_heads, preferred_element...  42.8 us
    dot_general x11, matrix products, outer_sum(): jnp.einsum('sd,se->de', left, incoming, preferred_element_type=jnp.float32)  41.7 us
  transfers between devices with their start and end apart: 73, of which 31 were waited for; matrix products, arithmetic and copies ran while one was open for 45% of the time, Pallas kernels for 0%

profile of v1, /device:TPU:1, one launch (start us, length us, event | category | flops | bytes accessed | tf_op | source)
XLA Modules:
  0.0 981.4 jit_solution(3839987987588620732)
XLA Ops:
  35.7 7.2 collective-permute-start.1
  54.6 20.9 %all-gather.11.cloned.1.call-done = bf16[1024,1024]{0,1:T(8,128)(2,1)} async-done(((bf16[128,1024]{0,1:T(8,128)(2,1)}), bf16[1024,1024]{0,1:T(8,128)(2,1)}) %all-gather.11.cloned.1.call-update) | async-done | bytes 2097168 | tf_op jit(solution)/shard_map/all_gather | solution.py:93
  79.8 47.5 %all-gather.15.cloned.1.call-done = bf16[1024,1024]{0,1:T(8,128)(2,1)} async-done(((bf16[128,1024]{0,1:T(8,128)(2,1)}), bf16[1024,1024]{0,1:T(8,128)(2,1)}) %all-gather.15.cloned.1.call-update) | async-done | bytes 2097168 | tf_op jit(solution)/shard_map/all_gather | solution.py:93
  186.7 11.7 %collective-permute-done.7 = bf16[256,1024]{1,0:T(8,128)(2,1)S(1)} collective-permute-done((bf16[256,1024]{1,0:T(8,128)(2,1)S(1)}, bf16[256,1024]{1,0:T(8,128)(2,1)S(1)}, u32[]{:S(2)}, u32[]{:S(2)}) %collective-permute-start.7) | collective-permute-done | bytes 524320 | tf_op jit(solution)/shard_map/ppermute | solution.py:53
  211.7 14.1 %multiply_convert_fusion.4 = (bf16[1024,1024]{1,0:T(8,128)(2,1)S(1)}, f32[1024,1024]{1,0:T(8,128)}, f32[1024,1024]{1,0:T(8,128)}) fusion(f32[1024]{0:T(1024)S(1)} %bitcast.643, bf16[128,8,8,128]{3,2,1,0:T(8,128)(2,1)S(1)} %bitcast.523, bf16[512,1024]{1,0:T(8,128)(2,1)} %collective-permute-done.8, bf16[256,1024]{1,0:T(8,128)(2,1)S(1)} %copy-done.128, ...), kind=kOutput, calls=%fused_computation.70 | convolution fusion | flops 2222981120 | bytes 14684160 | tf_op jit(solution)/shard_map/sd,de->se/dot_general | solution.py:26
  238.9 10.9 %collective-permute-done.10 = bf16[256,1024]{1,0:T(8,128)(2,1)S(1)} collective-permute-done((bf16[256,1024]{1,0:T(8,128)(2,1)S(1)}, bf16[256,1024]{1,0:T(8,128)(2,1)S(1)}, u32[]{:S(2)}, u32[]{:S(2)}) %collective-permute-start.10) | collective-permute-done | bytes 524320 | tf_op jit(solution)/shard_map/ppermute | solution.py:53
  250.5 10.6 %collective-permute-done.17 = bf16[256,1024]{1,0:T(8,128)(2,1)S(1)} collective-permute-done((bf16[256,1024]{1,0:T(8,128)(2,1)S(1)}, bf16[256,1024]{1,0:T(8,128)(2,1)S(1)}, u32[]{:S(2)}, u32[]{:S(2)}) %collective-permute-start.17) | collective-permute-done | bytes 524320 | tf_op jit(solution)/shard_map/ppermute | solution.py:53
  263.7 8.6 collective-permute-done.15
  310.1 12.1 %collective-permute-done.20 = bf16[256,1024]{1,0:T(8,128)(2,1)S(1)} collective-permute-done((bf16[256,1024]{1,0:T(8,128)(2,1)S(1)}, bf16[256,1024]{1,0:T(8,128)(2,1)S(1)}, u32[]{:S(2)}, u32[]{:S(2)}) %collective-permute-start.20) | collective-permute-done | bytes 524320 | tf_op jit(solution)/shard_map/ppermute | solution.py:53
  324.9 10.6 %collective-permute-done.21 = bf16[256,1024]{1,0:T(8,128)(2,1)S(1)} collective-permute-done((bf16[256,1024]{1,0:T(8,128)(2,1)S(1)}, bf16[256,1024]{1,0:T(8,128)(2,1)S(1)}, u32[]{:S(2)}, u32[]{:S(2)}) %collective-permute-start.21) | collective-permute-done | bytes 524320 | tf_op jit(solution)/shard_map/ppermute | solution.py:53
  340.0 12.5 %collective-permute-done.25 = bf16[256,1024]{1,0:T(8,128)(2,1)S(1)} collective-permute-done((bf16[256,1024]{1,0:T(8,128)(2,1)S(1)}, bf16[256,1024]{1,0:T(8,128)(2,1)S(1)}, u32[]{:S(2)}, u32[]{:S(2)}) %collective-permute-start.25) | collective-permute-done | bytes 524320 | tf_op jit(solution)/shard_map/ppermute | solution.py:53
  359.8 12.3 %multiply_convert_fusion.3 = (bf16[1024,1024]{1,0:T(8,128)(2,1)S(1)}, f32[1024,1024]{1,0:T(8,128)S(1)}, f32[1024,1024]{1,0:T(8,128)S(1)}) fusion(f32[1024]{0:T(1024)S(1)} %bitcast.645, bf16[128,8,8,128]{3,2,1,0:T(8,128)(2,1)S(1)} %bitcast.529, bf16[512,1024]{1,0:T(8,128)(2,1)} %collective-permute-done.22, bf16[256,1024]{1,0:T(8,128)(2,1)S(1)} %copy-done.141, ...), kind=kOutput, calls=%fused_computation.57 | convolution fusion | flops 2222981120 | bytes 14684160 | tf_op jit(solution)/shard_map/sd,de->se/dot_general | solution.py:26
  388.7 9.2 collective-permute-done.28
  398.8 10.2 %collective-permute-done.24 = bf16[256,1024]{1,0:T(8,128)(2,1)S(1)} collective-permute-done((bf16[256,1024]{1,0:T(8,128)(2,1)S(1)}, bf16[256,1024]{1,0:T(8,128)(2,1)S(1)}, u32[]{:S(2)}, u32[]{:S(2)}) %collective-permute-start.24) | collective-permute-done | bytes 524320 | tf_op jit(solution)/shard_map/ppermute | solution.py:53
  412.1 10.9 %collective-permute-done.29 = bf16[256,1024]{1,0:T(8,128)(2,1)S(1)} collective-permute-done((bf16[256,1024]{1,0:T(8,128)(2,1)S(1)}, bf16[256,1024]{1,0:T(8,128)(2,1)S(1)}, u32[]{:S(2)}, u32[]{:S(2)}) %collective-permute-start.29) | collective-permute-done | bytes 524320 | tf_op jit(solution)/shard_map/ppermute | solution.py:53
  436.7 9.3 fusion.238
  446.0 15.6 %multiply_reduce_fusion.2 = (f32[4,1024]{1,0:T(4,128)}, f32[4,1024,1024]{1,2,0:T(8,128)}) fusion(f32[4,1024,1024]{1,2,0:T(8,128)} %copy-done.2, f32[4,1024]{1,0:T(4,128)} %copy-done.157, pred[1024,1024]{0,1:T(8,128)(4,1)S(1)} %copy-done.8, bf16[1024,4,64]{0,2,1:T(8,128)(2,1)} %bitcast.560, bf16[1024,4,64]{0,2,1:T(8,128)(2,1)} %bitcast.489), kind=kOutput, calls=%fused_computation.7 | convolution fusion | flops 557838336 | bytes 35684352 | tf_op jit(solution)/shard_map/qhc,khc->hqk/dot_general | solution.py:283
  461.6 8.7 multiply_convert_fusion.2
  535.1 7.6 collective-permute-done.33
  562.4 8.8 fusion.250
  576.6 11.0 %multiply_reduce_fusion = (f32[4,1024]{1,0:T(4,128)}, f32[4,1024,1024]{1,2,0:T(8,128)}) fusion(f32[4,1024,1024]{1,2,0:T(8,128)S(1)} %bitcast.432, f32[4,1024]{1,0:T(4,128)} %log_add_fusion, pred[1024,1024]{0,1:T(8,128)(4,1)S(1)} %copy-done.7, bf16[1024,4,64]{0,2,1:T(8,128)(2,1)} %bitcast.557, bf16[1024,4,64]{0,2,1:T(8,128)(2,1)} %bitcast.487), kind=kOutput, calls=%fused_computation.1 | convolution fusion | flops 557838336 | bytes 35684352 | tf_op jit(solution)/shard_map/qhc,khc->hqk/dot_general | solution.py:283
  587.6 11.3 %multiply_convert_fusion = bf16[4,1024,1024]{1,2,0:T(8,128)(2,1)} fusion(f32[4,1024,1024]{1,2,0:T(8,128)} %get-tuple-element.198, f32[4,1024,1024]{1,2,0:T(8,128)S(1)} %bitcast.432, f32[4,1024]{1,0:T(4,128)} %get-tuple-element.197, f32[4,1024]{1,0:T(4,128)} %log_add_fusion, pred[1024,1024]{0,1:T(8,128)(4,1)S(1)} %copy-done.7), kind=kLoop, calls=%fused_computation | loop fusion | flops 25165824 | bytes 43024384 | tf_op jit(solution)/shard_map/convert_element_type | solution.py:287
  603.2 9.9 %fusion.236 = (f32[4,64]{1,0:T(4,128)}, bf16[1024,4,64]{0,2,1:T(8,128)(2,1)}) fusion(bf16[1024,4,64]{0,2,1:T(8,128)(2,1)S(1)} %bitcast.558, f32[4,1024,1024]{1,2,0:T(8,128)} %copy-done.1, f32[4,1024]{1,0:T(4,128)S(1)} %copy-done.156, pred[1024,1024]{0,1:T(8,128)(4,1)S(1)} %copy-done.7), kind=kOutput, calls=%fused_computation.491 | convolution fusion | flops 554172160 | bytes 18891776 | tf_op jit(solution)/shard_map/hqk,qhc->khc/dot_general | solution.py:280
  655.2 16.3 %multiply_reduce_fusion.1 = (f32[4,1024]{1,0:T(4,128)}, f32[4,1024,1024]{1,2,0:T(8,128)}) fusion(f32[4,1024,1024]{1,2,0:T(8,128)} %copy-done, f32[4,1024]{1,0:T(4,128)} %log_add_fusion.1, pred[1024,1024]{0,1:T(8,128)(4,1)S(1)} %copy-done.5, bf16[1024,4,64]{0,2,1:T(8,128)(2,1)} %bitcast.555, bf16[1024,4,64]{0,2,1:T(8,128)(2,1)} %bitcast.485), kind=kOutput, calls=%fused_computation.4 | convolution fusion | flops 557838336 | bytes 35684352 | tf_op jit(solution)/shard_map/qhc,khc->hqk/dot_general | solution.py:283
  671.5 11.1 %multiply_convert_fusion.1 = bf16[4,1024,1024]{1,2,0:T(8,128)(2,1)} fusion(f32[4,1024,1024]{1,2,0:T(8,128)} %get-tuple-element.195, f32[4,1024,1024]{1,2,0:T(8,128)S(1)} %bitcast.430, f32[4,1024]{1,0:T(4,128)} %get-tuple-element.194, f32[4,1024]{1,0:T(4,128)} %log_add_fusion.1, pred[1024,1024]{0,1:T(8,128)(4,1)S(1)} %copy-done.5), kind=kLoop, calls=%fused_computation.3 | loop fusion | flops 25165824 | bytes 43024384 | tf_op jit(solution)/shard_map/convert_element_type | solution.py:287
  694.8 9.0 fusion.234
  776.9 11.2 %collective-permute-done.40 = bf16[256,1024]{1,0:T(8,128)(2,1)} collective-permute-done((bf16[256,1024]{1,0:T(8,128)(2,1)}, bf16[256,1024]{1,0:T(8,128)(2,1)}, u32[]{:S(2)}, u32[]{:S(2)}) %collective-permute-start.40) | collective-permute-done | bytes 524320 | tf_op jit(solution)/shard_map/ppermute | solution.py:53
  813.6 12.2 %collective-permute-done.62 = f32[232,128]{1,0:T(8,128)S(1)} collective-permute-done((f32[232,128]{1,0:T(8,128)S(1)}, f32[232,128]{1,0:T(8,128)S(1)}, u32[]{:S(2)}, u32[]{:S(2)}) %collective-permute-start.62) | collective-permute-done | bytes 118816 | tf_op jit(solution)/shard_map/ppermute | solution.py:53
  834.9 7.7 collective-permute-start.52
  849.2 8.1 collective-permute-start.48
  857.4 49.3 %reduce-scatter.12.cloned.1.call-done = bf16[1,256,1024]{1,2,0:T(8,128)(2,1)} async-done(((bf16[8,256,1024]{1,2,0:T(8,128)(2,1)}), bf16[1,256,1024]{1,2,0:T(8,128)(2,1)}) %reduce-scatter.12.cloned.1.call-update) | async-done | bytes 524304 | tf_op jit(solution)/shard_map/reduce_scatter | solution.py:97
  910.9 9.9 %collective-permute-done.54 = bf16[1,2,128,1024]{2,3,1,0:T(8,128)(2,1)} collective-permute-done((bf16[1,2,128,1024]{2,3,1,0:T(8,128)(2,1)S(1)}, bf16[1,2,128,1024]{2,3,1,0:T(8,128)(2,1)}, u32[]{:S(2)}, u32[]{:S(2)}) %collective-permute-start.54) | collective-permute-done | bytes 524320 | tf_op jit(solution)/shard_map/ppermute | solution.py:53
  (1043 shorter events, 528.5 us)
Async XLA Ops:
  7.2 68.3 %all-gather.11.cloned.1.call-start = ((), (), s32[]{:S(2)}) async-start(), calls=%async_computation.10 | async-start | bytes 2359296 | tf_op jit(solution)/shard_map/all_gather | solution.py:93
  20.4 106.9 %all-gather.15.cloned.1.call-start = ((), (), s32[]{:S(2)}) async-start(), calls=%async_computation.12 | async-start | bytes 2359296 | tf_op jit(solution)/shard_map/all_gather | solution.py:93
  21.7 185.2 %all-gather.13.cloned.1.call-start = ((), (), s32[]{:S(2)}) async-start(), calls=%async_computation.11 | async-start | bytes 4718592 | tf_op jit(solution)/shard_map/all_gather | solution.py:93
  22.9 23.2 %collective-permute-start.11 = (bf16[256,1024]{1,0:T(8,128)(2,1)S(1)}, bf16[256,1024]{1,0:T(8,128)(2,1)}, u32[]{:S(2)}, u32[]{:S(2)}) collective-permute-start(bf16[256,1024]{1,0:T(8,128)(2,1)S(1)} %bitcast.437), channel_id=1, source_target_pairs={{0,2},{1,3},{2,0},{3,1},{4,6},{5,7},{6,4},{7,5},{8,10},{9,11},{10,... | collective-permute-start | bytes 1572872 | tf_op jit(solution)/shard_map/ppermute | solution.py:53
  32.2 247.5 %all-gather.17.cloned.1.call-start = ((), (), s32[]{:S(2)}) async-start(), calls=%async_computation.13 | async-start | bytes 2359296 | tf_op jit(solution)/shard_map/all_gather | solution.py:93
  182.1 20.3 %collective-permute-start.13 = (bf16[512,1024]{1,0:T(8,128)(2,1)}, bf16[512,1024]{1,0:T(8,128)(2,1)}, u32[]{:S(2)}, u32[]{:S(2)}) collective-permute-start(bf16[512,1024]{1,0:T(8,128)(2,1)} %slice.514), channel_id=1, source_target_pairs={{0,1},{1,0},{2,3},{3,2},{4,5},{5,4},{6,7},{7,6},{8,9},{9,8},{10,11... | collective-permute-start | bytes 3145736 | tf_op jit(solution)/shard_map/ppermute | solution.py:53
  205.7 26.3 %collective-permute-start.14 = (bf16[256,1024]{1,0:T(8,128)(2,1)S(1)}, bf16[256,1024]{1,0:T(8,128)(2,1)S(1)}, u32[]{:S(2)}, u32[]{:S(2)}) collective-permute-start(bf16[256,1024]{1,0:T(8,128)(2,1)S(1)} %slice.713), channel_id=1, source_target_pairs={{0,2},{1,3},{2,0},{3,1},{4,6},{5,7},{6,4},{7,5},{8,10},{9,11},{10,... | collective-permute-start | bytes 1572872 | tf_op jit(solution)/shard_map/ppermute | solution.py:53
  231.7 123.4 %all-gather.19.cloned.1.call-start = ((), (), s32[]{:S(2)}) async-start(), calls=%async_computation.14 | async-start | bytes 4718592 | tf_op jit(solution)/shard_map/all_gather | solution.py:93
  237.0 24.1 %collective-permute-start.17 = (bf16[256,1024]{1,0:T(8,128)(2,1)S(1)}, bf16[256,1024]{1,0:T(8,128)(2,1)S(1)}, u32[]{:S(2)}, u32[]{:S(2)}) collective-permute-start(bf16[256,1024]{1,0:T(8,128)(2,1)S(1)} %add_convert_fusion.1), channel_id=1, source_target_pairs={{0,2},{1,3},{2,0},{3,1},{4,6},{5,7},{6,4},{7,5},{8,10},{9,11},{10,... | collective-permute-start | bytes 1572872 | tf_op jit(solution)/shard_map/ppermute | solution.py:53
  250.1 22.2 %collective-permute-start.15 = (bf16[256,1024]{1,0:T(8,128)(2,1)S(1)}, bf16[256,1024]{1,0:T(8,128)(2,1)S(1)}, u32[]{:S(2)}, u32[]{:S(2)}) collective-permute-start(bf16[256,1024]{1,0:T(8,128)(2,1)S(1)} %fusion.140), channel_id=1, source_target_pairs={{0,2},{1,3},{2,0},{3,1},{4,6},{5,7},{6,4},{7,5},{8,10},{9,11},{10,... | collective-permute-start | bytes 1572872 | tf_op jit(solution)/shard_map/ppermute | solution.py:53
  262.2 22.4 %collective-permute-start.18 = (bf16[512,1024]{1,0:T(8,128)(2,1)}, bf16[512,1024]{1,0:T(8,128)(2,1)}, u32[]{:S(2)}, u32[]{:S(2)}) collective-permute-start(bf16[512,1024]{1,0:T(8,128)(2,1)} %pad_maximum_fusion.26), channel_id=1, source_target_pairs={{0,1},{1,0},{2,3},{3,2},{4,5},{5,4},{6,7},{7,6},{8,9},{9,8},{10,11... | collective-permute-start | bytes 3145736 | tf_op jit(solution)/shard_map/ppermute | solution.py:53
  279.7 476.7 %reduce-scatter.10.cloned.1.call-start = ((), (), s32[]{:S(2)}) async-start(), calls=%async_computation.7 | async-start | bytes 2359296 | tf_op jit(solution)/shard_map/reduce_scatter | solution.py:97
  336.7 22.3 %collective-permute-start.22 = (bf16[512,1024]{1,0:T(8,128)(2,1)}, bf16[512,1024]{1,0:T(8,128)(2,1)}, u32[]{:S(2)}, u32[]{:S(2)}) collective-permute-start(bf16[512,1024]{1,0:T(8,128)(2,1)} %pad_maximum_fusion.27), channel_id=1, source_target_pairs={{0,1},{1,0},{2,3},{3,2},{4,5},{5,4},{6,7},{7,6},{8,9},{9,8},{10,11... | collective-permute-start | bytes 3145736 | tf_op jit(solution)/shard_map/ppermute | solution.py:53
  354.4 17.8 %collective-permute-start.26 = (bf16[512,1024]{1,0:T(8,128)(2,1)}, bf16[512,1024]{1,0:T(8,128)(2,1)}, u32[]{:S(2)}, u32[]{:S(2)}) collective-permute-start(bf16[512,1024]{1,0:T(8,128)(2,1)} %pad_maximum_fusion.28), channel_id=1, source_target_pairs={{0,1},{1,0},{2,3},{3,2},{4,5},{5,4},{6,7},{7,6},{8,9},{9,8},{10,11... | collective-permute-start | bytes 3145736 | tf_op jit(solution)/shard_map/ppermute | solution.py:53
  387.4 21.7 %collective-permute-start.24 = (bf16[256,1024]{1,0:T(8,128)(2,1)S(1)}, bf16[256,1024]{1,0:T(8,128)(2,1)S(1)}, u32[]{:S(2)}, u32[]{:S(2)}) collective-permute-start(bf16[256,1024]{1,0:T(8,128)(2,1)S(1)} %slice.710), channel_id=1, source_target_pairs={{0,2},{1,3},{2,0},{3,1},{4,6},{5,7},{6,4},{7,5},{8,10},{9,11},{10,... | collective-permute-start | bytes 1572872 | tf_op jit(solution)/shard_map/ppermute | solution.py:53
  501.5 267.2 %reduce-scatter.14.cloned.1.call-start = ((), (), s32[]{:S(2)}) async-start(), calls=%async_computation.9 | async-start | bytes 4718592 | tf_op jit(solution)/shard_map/reduce_scatter | solution.py:97
  510.5 21.0 %collective-permute-start.42 = (bf16[256,1024]{1,0:T(8,128)(2,1)}, bf16[256,1024]{1,0:T(8,128)(2,1)}, u32[]{:S(2)}, u32[]{:S(2)}) collective-permute-start(bf16[256,1024]{1,0:T(8,128)(2,1)} %slice.705), channel_id=1, source_target_pairs={{0,2},{1,3},{2,0},{3,1},{4,6},{5,7},{6,4},{7,5},{8,10},{9,11},{10,... | collective-permute-start | bytes 1572872 | tf_op jit(solution)/shard_map/ppermute | solution.py:53
  523.7 19.0 %collective-permute-start.33 = (bf16[256,1024]{1,0:T(8,128)(2,1)S(1)}, bf16[256,1024]{1,0:T(8,128)(2,1)S(1)}, u32[]{:S(2)}, u32[]{:S(2)}) collective-permute-start(bf16[256,1024]{1,0:T(8,128)(2,1)S(1)} %convert_element_type.509), channel_id=1, source_target_pairs={{0,2},{1,3},{2,0},{3,1},{4,6},{5,7},{6,4},{7,5},{8,10},{9,11},{10,... | collective-permute-start | bytes 1572872 | tf_op jit(solution)/shard_map/ppermute | solution.py:53
  543.9 18.0 %collective-permute-start.34 = (bf16[512,1024]{1,0:T(8,128)(2,1)}, bf16[512,1024]{1,0:T(8,128)(2,1)}, u32[]{:S(2)}, u32[]{:S(2)}) collective-permute-start(bf16[512,1024]{1,0:T(8,128)(2,1)} %pad_maximum_fusion.31), channel_id=1, source_target_pairs={{0,1},{1,0},{2,3},{3,2},{4,5},{5,4},{6,7},{7,6},{8,9},{9,8},{10,11... | collective-permute-start | bytes 3145736 | tf_op jit(solution)/shard_map/ppermute | solution.py:53
  561.2 210.4 %reduce-scatter.8.cloned.1.call-start = ((), (), s32[]{:S(2)}) async-start(), calls=%async_computation.6 | async-start | bytes 2359296 | tf_op jit(solution)/shard_map/reduce_scatter | solution.py:97
  574.7 24.2 %collective-permute-start.35 = (bf16[512,1024]{1,0:T(8,128)(2,1)}, bf16[512,1024]{1,0:T(8,128)(2,1)}, u32[]{:S(2)}, u32[]{:S(2)}) collective-permute-start(bf16[512,1024]{1,0:T(8,128)(2,1)} %slice.545), channel_id=1, source_target_pairs={{0,1},{1,0},{2,3},{3,2},{4,5},{5,4},{6,7},{7,6},{8,9},{9,8},{10,11... | collective-permute-start | bytes 3145736 | tf_op jit(solution)/shard_map/ppermute | solution.py:53
  602.8 18.1 %collective-permute-start.36 = (bf16[256,1024]{1,0:T(8,128)(2,1)}, bf16[256,1024]{1,0:T(8,128)(2,1)}, u32[]{:S(2)}, u32[]{:S(2)}) collective-permute-start(bf16[256,1024]{1,0:T(8,128)(2,1)} %slice.707), channel_id=1, source_target_pairs={{0,2},{1,3},{2,0},{3,1},{4,6},{5,7},{6,4},{7,5},{8,10},{9,11},{10,... | collective-permute-start | bytes 1572872 | tf_op jit(solution)/shard_map/ppermute | solution.py:53
  652.0 173.8 %reduce-scatter.6.cloned.1.call-start = ((), (), s32[]{:S(2)}) async-start(), calls=%async_computation.5 | async-start | bytes 2359296 | tf_op jit(solution)/shard_map/reduce_scatter | solution.py:97
  710.8 195.9 %reduce-scatter.12.cloned.1.call-start = ((), (), s32[]{:S(2)}) async-start(), calls=%async_computation.8 | async-start | bytes 4718592 | tf_op jit(solution)/shard_map/reduce_scatter | solution.py:97
  768.2 20.0 %collective-permute-start.40 = (bf16[256,1024]{1,0:T(8,128)(2,1)}, bf16[256,1024]{1,0:T(8,128)(2,1)}, u32[]{:S(2)}, u32[]{:S(2)}) collective-permute-start(bf16[256,1024]{1,0:T(8,128)(2,1)} %slice.706), channel_id=1, source_target_pairs={{0,2},{1,3},{2,0},{3,1},{4,6},{5,7},{6,4},{7,5},{8,10},{9,11},{10,... | collective-permute-start | bytes 1572872 | tf_op jit(solution)/shard_map/ppermute | solution.py:53
  830.7 16.6 %collective-permute-start.47 = (bf16[1,3,128,768]{2,3,1,0:T(8,128)(2,1)S(1)}, bf16[1,3,128,768]{2,3,1,0:T(8,128)(2,1)S(1)}, u32[]{:S(2)}, u32[]{:S(2)}) collective-permute-start(bf16[1,3,128,768]{2,3,1,0:T(8,128)(2,1)S(1)} %maximum_bitcast_fusion), channel_id=1, source_target_pairs={{0,2},{1,3},{2,0},{3,1},{4,6},{5,7},{6,4},{7,5},{8,10},{9,11},{10,... | collective-permute-start | bytes 1769480 | tf_op jit(solution)/shard_map/ppermute | solution.py:53
  834.9 74.6 %collective-permute-start.52 = (bf16[3,128,1024]{2,1,0:T(8,128)(2,1)S(1)}, bf16[3,128,1024]{2,1,0:T(8,128)(2,1)}, u32[]{:S(2)}, u32[]{:S(2)}) collective-permute-start(bf16[3,128,1024]{2,1,0:T(8,128)(2,1)S(1)} %bitcast.475), channel_id=1, source_target_pairs={{0,2},{1,3},{2,0},{3,1},{4,6},{5,7},{6,4},{7,5},{8,10},{9,11},{10,... | collective-permute-start | bytes 2359304 | tf_op jit(solution)/shard_map/ppermute | solution.py:53
  849.2 89.5 %collective-permute-start.48 = (bf16[2,3,128,768]{2,3,1,0:T(8,128)(2,1)}, bf16[2,3,128,768]{2,3,1,0:T(8,128)(2,1)}, u32[]{:S(2)}, u32[]{:S(2)}) collective-permute-start(bf16[2,3,128,768]{2,3,1,0:T(8,128)(2,1)} %pad_maximum_fusion.21), channel_id=1, source_target_pairs={{0,1},{1,0},{2,3},{3,2},{4,5},{5,4},{6,7},{7,6},{8,9},{9,8},{10,11... | collective-permute-start | bytes 3538952 | tf_op jit(solution)/shard_map/ppermute | solution.py:53
  909.1 22.9 %collective-permute-start.56 = (bf16[1,2,128,1024]{2,3,1,0:T(8,128)(2,1)S(1)}, bf16[1,2,128,1024]{2,3,1,0:T(8,128)(2,1)}, u32[]{:S(2)}, u32[]{:S(2)}) collective-permute-start(bf16[1,2,128,1024]{2,3,1,0:T(8,128)(2,1)S(1)} %maximum_bitcast_fusion.2), channel_id=1, source_target_pairs={{0,2},{1,3},{2,0},{3,1},{4,6},{5,7},{6,4},{7,5},{8,10},{9,11},{10,... | collective-permute-start | bytes 1572872 | tf_op jit(solution)/shard_map/ppermute | solution.py:53
  909.7 40.0 %collective-permute-start.53 = (bf16[3,128,1024]{2,1,0:T(8,128)(2,1)S(1)}, bf16[3,128,1024]{2,1,0:T(8,128)(2,1)}, u32[]{:S(2)}, u32[]{:S(2)}) collective-permute-start(bf16[3,128,1024]{2,1,0:T(8,128)(2,1)S(1)} %broadcast_select_fusion), channel_id=1, source_target_pairs={{0,1},{1,0},{2,3},{3,2},{4,5},{5,4},{6,7},{7,6},{8,9},{9,8},{10,11... | collective-permute-start | bytes 2359304 | tf_op jit(solution)/shard_map/ppermute | solution.py:53
  922.9 29.2 %collective-permute-start.55 = (bf16[2,2,128,1024]{2,3,1,0:T(8,128)(2,1)}, bf16[2,2,128,1024]{2,3,1,0:T(8,128)(2,1)}, u32[]{:S(2)}, u32[]{:S(2)}) collective-permute-start(bf16[2,2,128,1024]{2,3,1,0:T(8,128)(2,1)} %pad_maximum_fusion.34), channel_id=1, source_target_pairs={{0,1},{1,0},{2,3},{3,2},{4,5},{5,4},{6,7},{7,6},{8,9},{9,8},{10,11... | collective-permute-start | bytes 3145736 | tf_op jit(solution)/shard_map/ppermute | solution.py:53
  934.1 19.5 %collective-permute-start.57 = (bf16[2,2,128,1024]{2,3,1,0:T(8,128)(2,1)}, bf16[2,2,128,1024]{2,3,1,0:T(8,128)(2,1)}, u32[]{:S(2)}, u32[]{:S(2)}) collective-permute-start(bf16[2,2,128,1024]{2,3,1,0:T(8,128)(2,1)} %pad_maximum_fusion.35), channel_id=1, source_target_pairs={{0,1},{1,0},{2,3},{3,2},{4,5},{5,4},{6,7},{7,6},{8,9},{9,8},{10,11... | collective-permute-start | bytes 3145736 | tf_op jit(solution)/shard_map/ppermute | solution.py:53
  (312 other events, 4420.0 us)
Sparse Core Ops, SparseCore 0:
  20.5 54.9 all-gather.10
  78.1 49.1 all-gather.14
  129.3 73.3 all-gather.12
  231.8 47.0 all-gather.16
  281.4 73.3 all-gather.18
  501.7 63.4 reduce-scatter.9
  569.4 88.8 reduce-scatter.13
  662.2 65.7 reduce-scatter.7
  731.9 66.5 reduce-scatter.5
  803.0 103.5 reduce-scatter.11

commit v2 on v1

v2 whole, which is shorter than its diff:
```python
import jax
import jax.numpy as jnp
from jax import lax
from jax.experimental import pallas as pl
from jax.experimental.pallas import tpu as pltpu
from jax.sharding import PartitionSpec as P

HEADS = 16


epsilon = 1e-05
masked_score = -1e30
low = jnp.bfloat16
high = jnp.float32
shape = jax.ShapeDtypeStruct
VMEM = pl.BlockSpec(memory_space=pltpu.VMEM)
SMEM = pl.BlockSpec(memory_space=pltpu.SMEM)
across_rows = (((0,), (0,)), ((), ()))
across_lanes = (((1,), (1,)), ((), ()))


def run(kernel, outs, args, name, flops, scratch=(), scalars=0, room=24):
    moved = sum(a.size * a.dtype.itemsize for a in args) + sum(
        o.size * jnp.dtype(o.dtype).itemsize for o in outs
    )
    return pl.pallas_call(
        kernel,
        out_shape=list(outs),
        in_specs=[SMEM] * scalars + [VMEM] * (len(args) - scalars),
        out_specs=[VMEM] * len(outs),
        scratch_shapes=list(scratch),
        compiler_params=pltpu.CompilerParams(vmem_limit_bytes=room << 20),
        cost_estimate=pl.CostEstimate(
            flops=int(flops), bytes_accessed=int(moved), transcendentals=0
        ),
        name=name,
    )(*args)


def normalize(values, gain, shift):
    middle = jnp.mean(values, -1, keepdims=True)
    centred = values - middle
    width = jnp.mean(centred * centred, -1, keepdims=True)
    return centred * lax.rsqrt(width + epsilon) * gain + shift


def matmul(left, right):
    return jnp.dot(left, right, preferred_element_type=high)


def matmul_back(left, right):
    return lax.dot_general(left, right, across_lanes, preferred_element_type=high)


def matmul_outer(left, right):
    return lax.dot_general(left, right, across_rows, preferred_element_type=high)


def piece_rows(pieces):
    start = 0
    for piece in pieces:
        yield pl.ds(start, piece.shape[0]), piece
        start += piece.shape[0]


def assemble(pieces, table, parts):
    def kernel(table_ref, *refs):
        sources, outs = refs[: len(pieces)], refs[len(pieces) :]
        for which, (start, rows, _) in enumerate(parts):
            for i, source in enumerate(sources):
                at = pl.multiple_of(table_ref[which, i], rows)
                outs[which][pl.ds(at, rows), :] = source[start : start + rows, :]

    width = pieces[0].shape[1]
    outs = [shape((whole, width), low) for _, _, whole in parts]
    return run(kernel, outs, [table, *pieces], "assemble", 1, scalars=1)


def project_self(pieces, gain, shift, entry, biases):
    count, width = len(pieces), entry.shape[1] // 3

    def kernel(*refs):
        sources = refs[:count]
        gain_ref, shift_ref, entry_ref, bias_ref, normed_ref, query_ref, key_ref, value_ref = refs[
            count:
        ]
        for rows, source in piece_rows(sources):
            normed = normalize(source[...].astype(high), gain_ref[...], shift_ref[...])
            normed_ref[rows, :] = normed.astype(low)
            joined = matmul(normed_ref[rows, :], entry_ref[...])
            query_ref[rows, :] = (joined[:, :width] + bias_ref[0:1, :]).astype(low)
            key_ref[rows, :] = joined[:, width : 2 * width].astype(low)
            value_ref[rows, :] = (joined[:, 2 * width :] + bias_ref[1:2, :]).astype(low)

    rows = sum(piece.shape[0] for piece in pieces)
    outs = [shape((rows, pieces[0].shape[1]), low)] + [shape((rows, width), low)] * 3
    flops = 2 * rows * entry.shape[0] * entry.shape[1]
    return run(kernel, outs, [*pieces, gain, shift, entry, biases], "project_self", flops)


def project_cross(pieces, memory_pieces, entry, biases):
    count, width = len(pieces), entry.shape[1] // 3

    def kernel(*refs):
        sources, memories = refs[:count], refs[count : 2 * count]
        entry_ref, bias_ref, query_ref, key_ref, value_ref = refs[2 * count :]
        for rows, source in piece_rows(sources):
            joined = matmul(source[...], entry_ref[:, :width])
            query_ref[rows, :] = (joined + bias_ref[0:1, :]).astype(low)
        for rows, source in piece_rows(memories):
            joined = matmul(source[...], entry_ref[:, width:])
            key_ref[rows, :] = joined[:, :width].astype(low)
            value_ref[rows, :] = (joined[:, width:] + bias_ref[1:2, :]).astype(low)

    rows = sum(piece.shape[0] for piece in pieces)
    outs = [shape((rows, width), low)] * 3
    flops = 2 * rows * entry.shape[0] * entry.shape[1]
    return run(kernel, outs, [*pieces, *memory_pieces, entry, biases], "project_cross", flops)


def head_lanes(values, head, width):
    lanes = lax.broadcasted_iota(jnp.int32, values.shape, 1)
    inside = (lanes >= head * width) & (lanes < (head + 1) * width)
    return jnp.where(inside, values, jnp.zeros_like(values))


def block_bias(keys, cols, causal, key_segment, query_segment, key_place, query_place):
    allowed = key_segment[keys, :] == query_segment[:, cols]
    if causal:
        allowed = allowed & (key_place[keys, :] <= query_place[:, cols])
    return jnp.where(allowed, 0.0, masked_score)


def attend_forward(marks, tags, queries, keys, values, leave, heads, causal, count):
    rows, width = queries.shape
    head_width = width // heads
    block = min(256, rows)
    blocks = rows // block
    local = rows // count
    scale = head_width**-0.5
    tall = max(8, heads)

    def kernel(*refs):
        marks_ref, key_segment, query_segment, key_place, query_place = refs[:5]
        query_ref, key_ref, value_ref, leave_ref, mixture_ref, total_ref = refs[5:11]
        partial_refs = refs[11 : 11 + count]
        score_ref, top_ref, sum_ref, mix_ref, value_turned = refs[11 + count :]
        value_turned[...] = value_ref[...].astype(high).T.astype(low)
        total_ref[...] = jnp.zeros(total_ref.shape, high)
        for i in range(blocks):
            mine = pl.ds(i * block, block)
            cols = slice(i * block, (i + 1) * block)
            query = query_ref[mine, :] * low(scale)
            query_heads = [head_lanes(query, head, head_width) for head in range(heads)]
            top_ref[...] = jnp.full(top_ref.shape, masked_score, high)
            sum_ref[...] = jnp.zeros(sum_ref.shape, high)
            mix_ref[...] = jnp.zeros(mix_ref.shape, high)

            def score(j, carry, i=i, cols=cols, query_heads=query_heads):
                @pl.when(marks_ref[i, j] != 0)
                def _():
                    there = pl.ds(pl.multiple_of(j * block, block), block)
                    bias = block_bias(
                        there, cols, causal, key_segment, query_segment, key_place, query_place
                    )
                    for head in range(heads):
                        scores = matmul_back(key_ref[there, :], query_heads[head]) + bias
                        score_ref[head, there, :] = scores
                        row = slice(head, head + 1)
                        top_ref[row, :] = jnp.maximum(
                            top_ref[row, :], jnp.max(scores, 0, keepdims=True)
                        )

                return carry

            lax.fori_loop(0, blocks, score, 0)

            def mix(j, carry, i=i):
                @pl.when(marks_ref[i, j] != 0)
                def _():
                    there = pl.ds(pl.multiple_of(j * block, block), block)
                    for head in range(heads):
                        row = slice(head, head + 1)
                        features = slice(head * head_width, (head + 1) * head_width)
                        weights = jnp.exp(score_ref[head, there, :] - top_ref[row, :])
                        sum_ref[row, :] += jnp.sum(weights, 0, keepdims=True)
                        mix_ref[features, :] += matmul(
                            value_turned[features, there], weights.astype(low)
                        )

                return carry

            lax.fori_loop(0, blocks, mix, 0)
            for head in range(heads):
                row = slice(head, head + 1)
                features = slice(head * head_width, (head + 1) * head_width)
                mix_ref[features, :] = mix_ref[features, :] * (1.0 / sum_ref[row, :])
                total_ref[row, cols] = top_ref[row, :] + jnp.log(sum_ref[row, :])
            mixture_ref[mine, :] = mix_ref[...].T.astype(low)
        for i in range(count):
            mine = pl.ds(i * local, local)
            partial_refs[i][...] = matmul(mixture_ref[mine, :], leave_ref[...]).astype(low)

    outs = [shape((rows, width), low), shape((tall, rows), high)]
    outs += [shape((local, leave.shape[1]), low)] * count
    scratch = [
        pltpu.VMEM((heads, rows, block), high),
        pltpu.VMEM((tall, block), high),
        pltpu.VMEM((tall, block), high),
        pltpu.VMEM((width, block), high),
        pltpu.VMEM((width, rows), low),
    ]
    flops = 8 * rows * rows * width + 2 * rows * width * leave.shape[1]
    args = [marks, *tags, queries, keys, values, leave]
    mixture, total, *partials = run(
        kernel, outs, args, "attend_forward", flops, scratch, scalars=1
    )
    return mixture, total, partials


def attend_backward(marks, tags, pieces, leave, entry, stored, heads, causal, cross):
    queries, keys, values, mixture, total = stored
    count = len(pieces)
    rows, width = queries.shape
    head_width = width // heads
    block = min(256, rows)
    blocks = rows // block
    local = rows // count
    scale = head_width**-0.5

    def kernel(*refs):
        marks_ref, key_segment, query_segment, key_place, query_place = refs[:5]
        incoming_refs = refs[5 : 5 + count]
        leave_ref, entry_ref, query_ref, key_ref, value_ref, mixture_ref, total_ref = refs[
            5 + count : 12 + count
        ]
        joined_ref, sums_ref, exit_ref = refs[12 + count : 15 + count]
        partial_refs = refs[15 + count : 15 + 2 * count]
        memory_refs = refs[15 + 2 * count : -5]
        incoming_mix, key_sum, value_sum, query_turned, key_turned = refs[-5:]
        exit_sum = None
        for where, piece in piece_rows(incoming_refs):
            incoming_mix[where, :] = matmul_back(piece[...], leave_ref[...]).astype(low)
            term = matmul_outer(mixture_ref[where, :], piece[...])
            exit_sum = term if exit_sum is None else exit_sum + term
        exit_ref[...] = exit_sum.astype(low)
        key_turned[...] = key_ref[...].astype(high).T.astype(low)
        key_sum[...] = jnp.zeros(key_sum.shape, high)
        value_sum[...] = jnp.zeros(value_sum.shape, high)
        query_total = jnp.zeros((1, width), high)
        for i in range(blocks):
            mine = pl.ds(i * block, block)
            cols = slice(i * block, (i + 1) * block)
            query = query_ref[mine, :] * low(scale)
            arriving = incoming_mix[mine, :]
            query_heads = [head_lanes(query, head, head_width) for head in range(heads)]
            arriving_heads = [head_lanes(arriving, head, head_width) for head in range(heads)]
            products = (arriving.astype(high) * mixture_ref[mine, :].astype(high)).T
            inner = [
                jnp.sum(products[head * head_width : (head + 1) * head_width, :], 0, keepdims=True)
                for head in range(heads)
            ]
            query_turned[...] = jnp.zeros(query_turned.shape, high)

            def step(j, carry, i=i, cols=cols, qh=query_heads, ah=arriving_heads, inner=inner):
                @pl.when(marks_ref[i, j] != 0)
                def _():
                    there = pl.ds(pl.multiple_of(j * block, block), block)
                    bias = block_bias(
                        there, cols, causal, key_segment, query_segment, key_place, query_place
                    )
                    key_acc, value_acc = key_sum[there, :], value_sum[there, :]
                    for head in range(heads):
                        features = slice(head * head_width, (head + 1) * head_width)
                        scores = matmul_back(key_ref[there, :], qh[head])
                        weights = jnp.exp(scores - total_ref[head : head + 1, cols] + bias)
                        back = matmul_back(value_ref[there, :], ah[head])
                        change = (weights * (back - inner[head])).astype(low)
                        value_acc = value_acc + matmul(weights.astype(low), ah[head])
                        key_acc = key_acc + matmul(change, qh[head])
                        query_turned[features, :] += matmul(key_turned[features, there], change)
                    key_sum[there, :] = key_acc
                    value_sum[there, :] = value_acc

                return carry

            lax.fori_loop(0, blocks, step, 0)
            query_gradient = query_turned[...].T * scale
            query_total = query_total + jnp.sum(query_gradient, 0, keepdims=True)
            joined_ref[mine, :width] = query_gradient.astype(low)
        joined_ref[:, width : 2 * width] = key_sum[...].astype(low)
        joined_ref[:, 2 * width :] = value_sum[...].astype(low)
        sums_ref[0:1, :] = query_total
        sums_ref[1:2, :] = jnp.sum(value_sum[...], 0, keepdims=True)
        for i in range(count):
            mine = pl.ds(i * local, local)
            if cross:
                query_part = matmul_back(joined_ref[mine, :width], entry_ref[:, :width])
                memory_part = matmul_back(joined_ref[mine, width:], entry_ref[:, width:])
                partial_refs[i][...] = query_part.astype(low)
                memory_refs[i][...] = memory_part.astype(low)
            else:
                partial_refs[i][...] = matmul_back(joined_ref[mine, :], entry_ref[...]).astype(low)

    outs = [shape((rows, 3 * width), low), shape((2, width), high), shape(leave.shape, low)]
    outs += [shape((local, entry.shape[0]), low)] * (count * (2 if cross else 1))
    scratch = [
        pltpu.VMEM((rows, width), low),
        pltpu.VMEM((rows, width), high),
        pltpu.VMEM((rows, width), high),
        pltpu.VMEM((width, block), high),
        pltpu.VMEM((width, rows), low),
    ]
    flops = 20 * rows * rows * width + 10 * rows * width * entry.shape[0]
    args = [marks, *tags, *pieces, leave, entry, queries, keys, values, mixture, total]
    joined, sums, exit_gradient, *partials = run(
        kernel, outs, args, "attend_backward", flops, scratch, scalars=1, room=28
    )
    return joined, sums, exit_gradient, partials[:count], partials[count:]


def feed_forward(pieces, entry, leave, bias):
    count, hidden_width = len(pieces), entry.shape[1]
    step = min(512, hidden_width)

    def kernel(*refs):
        sources = refs[:count]
        entry_ref, leave_ref, bias_ref, active_ref, slope_ref = refs[count : count + 5]
        partial_refs = refs[count + 5 :]
        for (rows, source), partial in zip(piece_rows(sources), partial_refs):
            for start in range(0, hidden_width, step):
                cols = slice(start, start + step)
                hidden = matmul(source[...], entry_ref[:, cols]) + bias_ref[:, cols]
                share = 0.5 * (1.0 + lax.erf(hidden * 0.7071067811865476))
                density = jnp.exp(-0.5 * hidden * hidden) * 0.3989422804014327
                active_ref[rows, cols] = (hidden * share).astype(low)
                slope_ref[rows, cols] = (share + hidden * density).astype(low)
            partial[...] = matmul(active_ref[rows, :], leave_ref[...]).astype(low)

    rows = sum(piece.shape[0] for piece in pieces)
    outs = [shape((rows, hidden_width), low)] * 2
    outs += [shape((piece.shape[0], leave.shape[1]), low) for piece in pieces]
    flops = 4 * rows * entry.shape[0] * hidden_width
    args = [*pieces, entry, leave, bias]
    active, slope, *partials = run(kernel, outs, args, "feed_forward", flops)
    return active, slope, partials


def feed_backward(pieces, entry, leave, slope):
    count, hidden_width = len(pieces), entry.shape[1]

    def kernel(*refs):
        sources = refs[:count]
        entry_ref, leave_ref, slope_ref, hidden_ref, sum_ref = refs[count : count + 5]
        partial_refs = refs[count + 5 :]
        total = jnp.zeros(sum_ref.shape, high)
        for (rows, source), partial in zip(piece_rows(sources), partial_refs):
            hidden = matmul_back(source[...], leave_ref[...]) * slope_ref[rows, :].astype(high)
            total = total + jnp.sum(hidden, 0, keepdims=True)
            hidden_ref[rows, :] = hidden.astype(low)
            partial[...] = matmul_back(hidden_ref[rows, :], entry_ref[...]).astype(low)
        sum_ref[...] = total

    rows = sum(piece.shape[0] for piece in pieces)
    outs = [shape((rows, hidden_width), low), shape((1, hidden_width), high)]
    outs += [shape((piece.shape[0], entry.shape[0]), low) for piece in pieces]
    flops = 4 * rows * entry.shape[0] * hidden_width
    args = [*pieces, entry, leave, slope]
    hidden, total, *partials = run(kernel, outs, args, "feed_backward", flops)
    return hidden, total, partials


def blocks_out(shards, height, width):
    quarter = shards // 4
    return [
        shape((2 * quarter, height, width), low),
        shape((quarter, height, width), low),
        shape((quarter, height, width), low),
    ]


def block_targets(refs):
    return [(ref, at) for ref in refs for at in range(ref.shape[0])]


def outer_sums(pairs, order, name, stacked=False):
    flat, counts, flops = [], [], 0
    for lefts, rights, start, lanes in pairs:
        flat += [*lefts, *rights]
        counts.append((len(lefts), len(rights), start, lanes))
        flops += 2 * sum(left.size for left in lefts) * lanes
    sizes = [(pair[0][0].shape[1], pair[3]) for pair in pairs]

    def compute(refs, outs):
        for (left_count, right_count, start, lanes), out in zip(counts, outs):
            lefts, rights = refs[:left_count], refs[left_count : left_count + right_count]
            refs = refs[left_count + right_count :]
            terms = max(left_count, right_count)
            rows = sum(left.shape[0] for left in lefts) // terms
            step = min(256, out.shape[0])
            side = slice(start, start + lanes)
            for first in range(0, out.shape[0], step):
                cols = slice(first, first + step)
                total = None
                for i in range(terms):
                    where = pl.ds(i * rows, rows)
                    left = lefts[i][:, cols] if left_count == terms else lefts[0][where, cols]
                    right = rights[i][:, side] if right_count == terms else rights[0][where, side]
                    term = matmul_outer(left, right)
                    total = term if total is None else total + term
                out[cols, :] = total.astype(low)

    if order is None:

        def plain(*refs):
            compute(refs[: len(flat)], refs[len(flat) :])

        return run(plain, [shape(size, low) for size in sizes], flat, name, flops)

    shards = order.shape[0]
    heights = [size[0] // shards for size in sizes]
    if stacked:
        corners = [(sum(heights[:i]), 0) for i in range(len(sizes))]
        outs = blocks_out(shards, sum(heights), sizes[0][1])
    else:
        corners = [(0, sum(size[1] for size in sizes[:i])) for i in range(len(sizes))]
        outs = blocks_out(shards, heights[0], sum(size[1] for size in sizes))

    def kernel(order_ref, *refs):
        inputs, rest = refs[: len(flat)], refs[len(flat) :]
        compute(inputs, rest[3:])
        for i, (target, at) in enumerate(block_targets(rest[:3])):
            for source, rows, (top, side) in zip(rest[3:], heights, corners):
                where = pl.ds(pl.multiple_of(order_ref[i] * rows, rows), rows)
                target[at, top : top + rows, side : side + source.shape[1]] = source[where, :]

    scratch = [pltpu.VMEM(size, low) for size in sizes]
    return run(kernel, outs, [order, *flat], name, flops, scratch, scalars=1)


def order_combiners(exits, table):
    shards = table.shape[0]
    rows = exits[0].shape[0] // shards

    def kernel(table_ref, *refs):
        sources = refs[: len(exits)]
        for i, (target, at) in enumerate(block_targets(refs[len(exits) :])):
            where = pl.ds(pl.multiple_of(table_ref[i], rows), rows)
            for block, source in enumerate(sources):
                target[at, block * rows : (block + 1) * rows, :] = source[where, :]

    outs = blocks_out(shards, rows * len(exits), exits[0].shape[1])
    return run(kernel, outs, [table, *exits], "order_combiners", 1, scalars=1)


def add_up(refs):
    total = refs[0][...].astype(high)
    for ref in refs[1:]:
        total = total + ref[...].astype(high)
    return total


def residual_norm(base, addends, bias, gain, shift):
    count = 1 + len(addends)

    def kernel(*refs):
        bias_ref, gain_ref, shift_ref, total_ref, normed_ref = refs[count:]
        total = add_up(refs[:count]) + bias_ref[...]
        total_ref[...] = total
        normed_ref[...] = normalize(total, gain_ref[...], shift_ref[...]).astype(low)

    outs = [shape(base.shape, high), shape(base.shape, low)]
    return run(kernel, outs, [base, *addends, bias, gain, shift], "residual_norm", base.size * 12)


def residual_low(base, addends, bias):
    count = 1 + len(addends)

    def kernel(*refs):
        bias_ref, total_ref = refs[count:]
        total_ref[...] = (add_up(refs[:count]) + bias_ref[...]).astype(low)

    outs = [shape(base.shape, low)]
    return run(kernel, outs, [base, *addends, bias], "residual_low", base.size * 4)[0]


def join_gradient(cotangent, keep, addends):
    count = len(addends)

    def kernel(*refs):
        cotangent_ref, keep_ref = refs[:2]
        gradient_ref, low_ref, sum_ref = refs[2 + count :]
        total = cotangent_ref[...].astype(high) * keep_ref[...]
        for ref in refs[2 : 2 + count]:
            total = total + ref[...].astype(high)
        gradient_ref[...] = total
        low_ref[...] = total.astype(low)
        sum_ref[...] = jnp.sum(total, 0, keepdims=True)

    outs = [
        shape(cotangent.shape, high),
        shape(cotangent.shape, low),
        shape((1, cotangent.shape[1]), high),
    ]
    return run(kernel, outs, [cotangent, keep, *addends], "join_gradient", cotangent.size * 4)


def norm_backward(inputs, gain, incoming, addends):
    count = len(addends)

    def kernel(*refs):
        input_ref, gain_ref, incoming_ref = refs[:3]
        result_ref, low_ref, sums_ref = refs[3 + count :]
        gradient = add_up(refs[3 : 3 + count])
        values = input_ref[...].astype(high)
        centred = values - jnp.mean(values, -1, keepdims=True)
        inverse = lax.rsqrt(jnp.mean(centred * centred, -1, keepdims=True) + epsilon)
        unit = centred * inverse
        sums_ref[0:1, :] = jnp.sum(gradient * unit, 0, keepdims=True)
        sums_ref[1:2, :] = jnp.sum(gradient, 0, keepdims=True)
        scaled = gradient * gain_ref[...]
        inner = jnp.mean(scaled * unit, -1, keepdims=True)
        change = (scaled - jnp.mean(scaled, -1, keepdims=True) - unit * inner) * inverse
        result = incoming_ref[...] + change
        result_ref[...] = result
        low_ref[...] = result.astype(low)
        sums_ref[2:3, :] = jnp.sum(result, 0, keepdims=True)

    outs = [
        shape(inputs.shape, high),
        shape(inputs.shape, low),
        shape((3, inputs.shape[1]), high),
    ]
    args = [inputs, gain, incoming, *addends]
    return run(kernel, outs, args, "norm_backward", inputs.size * 20)


def seq_bits():
    bit, bits = lax.axis_size("seq") >> 1, []
    while bit:
        bits.append(bit)
        bit >>= 1
    return bits


def seq_offsets():
    offsets = [0]
    for bit in seq_bits():
        offsets = offsets + [offset ^ bit for offset in offsets]
    return offsets


def swap(values, bit, axis="seq"):
    return lax.ppermute(values, axis, [(i, i ^ bit) for i in range(lax.axis_size(axis))])


def spread(piece):
    pieces = [piece]
    for bit in seq_bits():
        pieces = pieces + [swap(piece, bit) for piece in pieces]
    return pieces


def sum_low(addends):
    total = addends[0].astype(high)
    for addend in addends[1:]:
        total = total + addend.astype(high)
    return total.astype(low)


def collect(partials):
    kept = [[partial] for partial in partials]
    for bit in reversed(seq_bits()):
        half = len(kept) // 2
        sent = kept[half:]
        arrived = [None] * half
        for i in reversed(range(half)):
            value = sent[i][0] if len(sent[i]) == 1 else sum_low(sent[i])
            arrived[i] = swap(value, bit)
        kept = [own + [other] for own, other in zip(kept[:half], arrived)]
    return kept[0]


def sum_everywhere(values):
    for axis in ("seq", "batch"):
        bit = 1
        while bit < lax.axis_size(axis):
            values = values + swap(values, bit, axis)
            bit <<= 1
    return values


def mine(values, axis):
    return lax.dynamic_index_in_dim(values, lax.axis_index("seq"), axis, keepdims=False)


def in_line():
    return lax.axis_size("batch") == 2 * lax.axis_size("seq")


def line_place():
    return lax.axis_index("batch") // 2, lax.axis_index("batch") % 2


def line_shift(values):
    shards = lax.axis_size("batch")
    return lax.ppermute(values, "batch", [(i, (i + 2) % shards) for i in range(shards)])


def line_order(first):
    length = lax.axis_size("batch") // 2
    place, side = line_place()
    at = (place - first - jnp.arange(length, dtype=jnp.int32)) % length
    return jnp.concatenate([2 * at + side, 2 * at + 1 - side])


def after(values, earlier):
    return lax.optimization_barrier((values, earlier))[0]


def gather_line(values):
    line, across = [values], [swap(values, 1, "batch")]
    for _ in range(1, lax.axis_size("batch") // 2):
        line.append(line_shift(line[-1]))
        across.append(swap(line[-1], 1, "batch"))
    return line + across


def scatter_line(keep, near, far):
    across = [swap(near, 1, "batch"), swap(far, 1, "batch")]
    half = near.shape[0]
    total = None
    for step in range(keep.shape[0]):
        addends = [keep[step], across[step // half][step % half]]
        if total is not None:
            addends = [line_shift(total)] + addends
        total = sum_low(addends)
    return total


def line_pairs(step, count, back):
    pairs = []
    for place in range(count):
        for side in range(2):
            here = (place * 2 + side) * count + place
            there = (((place + step) % count) * 2 + side) * count + place
            pairs.append((there, here) if back else (here, there))
    return pairs


def deal_combiners(combiners):
    count = lax.axis_size("seq")
    me = lax.axis_index("seq")
    place, _ = line_place()
    rows = combiners.shape[1] // count
    parts = combiners.reshape(combiners.shape[0], count, rows, combiners.shape[2])
    own = lax.dynamic_index_in_dim(parts, me, 1, keepdims=False)
    piece = jnp.where(place == me, own, jnp.zeros_like(own))
    for step in range(1, count):
        sent = lax.dynamic_index_in_dim(parts, (me + step) % count, 1, keepdims=False)
        piece = piece + lax.ppermute(sent, ("batch", "seq"), line_pairs(step, count, False))
    return piece.reshape(-1, piece.shape[2])


def return_combiners(pieces, blocks):
    count = lax.axis_size("seq")
    me = lax.axis_index("seq")
    place, _ = line_place()
    arrived = [pieces] + [
        lax.ppermute(pieces, ("batch", "seq"), line_pairs(step, count, True))
        for step in range(1, count)
    ]
    arrived = [piece.reshape(blocks, -1, piece.shape[1]) for piece in arrived]
    ring = jnp.stack(arrived + arrived[:-1], 1)
    ordered = lax.dynamic_slice_in_dim(ring, (count - me) % count, count, 1)
    ordered = ordered.reshape(blocks, -1, pieces.shape[1])
    for bit in seq_bits():
        ordered = jnp.where((place & bit) == (me & bit), ordered, swap(ordered, bit))
    return ordered


def gather_weights(projections, combiners, expanders, reducers):
    count, shards = lax.axis_size("seq"), lax.axis_size("batch")
    blocks, rows, _ = projections.shape
    feeds, _, _ = expanders.shape
    model_width = combiners.shape[2]
    entries = mine(projections.reshape(blocks, rows, 3, count, -1), 3).reshape(blocks, rows, -1)
    expand = mine(expanders.reshape(feeds, rows, shards, count, -1), 3).reshape(feeds, rows, -1)
    reduce = mine(reducers.reshape(feeds, count, -1, model_width), 1)
    if not in_line():

        def whole(values):
            return lax.all_gather(values, "batch", axis=0, tiled=True)

        leaves = [whole(combiners[i]).reshape(count, -1, model_width) for i in range(blocks)]
        return (
            [whole(entries[i]) for i in range(blocks)],
            [mine(leave, 0) for leave in leaves],
            [whole(expand[i]) for i in range(feeds)],
            [whole(reduce[i]) for i in range(feeds)],
        )
    order = line_order(0)
    last = shards // 2 - 1
    piece = model_width // count // shards
    straight = order * rows
    lower = reduce.shape[1]
    first = gather_line(entries[0])
    entry_zero = assemble(first, straight[None], [(0, rows, shards * rows)])
    leaf = gather_line(after(deal_combiners(combiners), first[last]))
    leaves = assemble(
        leaf,
        jnp.stack([((order % 2) * (shards // 2) + order // 2) * piece] * blocks),
        [(i * piece, piece, shards * piece) for i in range(blocks)],
    )

    def feed(which, earlier):
        joined = jnp.concatenate([expand[which], reduce[which]], 0)
        pieces = gather_line(after(joined, earlier))
        both = assemble(
            pieces,
            jnp.stack([straight, order * lower]),
            [(0, rows, shards * rows), (rows, lower, shards * lower)],
        )
        return both, pieces[last]

    feed_zero, done = feed(0, leaf[last])
    rest = gather_line(after(entries[1:].reshape(-1, entries.shape[2]), done))
    entry_rest = assemble(
        rest,
        jnp.stack([straight] * (blocks - 1)),
        [(i * rows, rows, shards * rows) for i in range(blocks - 1)],
    )
    feed_one, _ = feed(1, rest[last])
    return (
        [*entry_zero, *entry_rest],
        leaves,
        [feed_zero[0], feed_one[0]],
        [feed_zero[1], feed_one[1]],
    )


def spread_order(pieces, axis):
    me = lax.axis_index("seq")
    stacked = jnp.stack(pieces)
    offsets = jnp.array([seq_offsets().index(i) for i in range(len(pieces))], jnp.int32)
    ordered = [
        lax.dynamic_index_in_dim(stacked, offsets[me ^ i], 0, keepdims=False)
        for i in range(len(pieces))
    ]
    return jnp.stack(ordered, axis)


def per_device(
    source_tokens,
    target_tokens,
    source_lengths,
    target_lengths,
    projections,
    combiners,
    expanders,
    reducers,
    norm_gains,
    norm_shifts,
    attention_biases,
    expander_biases,
    reducer_biases,
    source_cotangent,
    target_cotangent,
):
    source_tokens, target_tokens = source_tokens[0], target_tokens[0]
    source_cotangent, target_cotangent = source_cotangent[0], target_cotangent[0]
    count, shards = lax.axis_size("seq"), lax.axis_size("batch")
    me = lax.axis_index("seq")
    local_count, model_width = source_tokens.shape
    heads = HEADS // count
    share = model_width // count
    padding_segment = source_lengths.shape[1] - 1

    here = jnp.arange(local_count, dtype=jnp.int32)
    places = jnp.concatenate([(me ^ offset) * local_count + here for offset in seq_offsets()])

    def segments(lengths):
        ends = jnp.cumsum(lengths[0], dtype=jnp.int32)
        return jnp.sum((places[:, None] >= ends[None, :]).astype(jnp.int32), -1, dtype=jnp.int32)

    source_segment, target_segment = segments(source_lengths), segments(target_lengths)
    source_keep = (source_segment[:local_count] < padding_segment).astype(high)[:, None]
    target_keep = (target_segment[:local_count] < padding_segment).astype(high)[:, None]

    def view(query_segment, key_segment, causal):
        def ends_of(values):
            blocks = values.reshape(-1, min(256, values.shape[0]))
            return jnp.min(blocks, 1), jnp.max(blocks, 1)

        query_low, query_high = ends_of(query_segment)
        key_low, key_high = ends_of(key_segment)
        marks = (query_low[:, None] <= key_high[None]) & (key_low[None] <= query_high[:, None])
        if causal:
            place_low, place_high = ends_of(places)
            marks = marks & (place_low[None] <= place_high[:, None])
        tags = (key_segment[:, None], query_segment[None], places[:, None], places[None])
        return marks.astype(jnp.int32), tags

    encoder_view = view(source_segment, source_segment, False)
    self_view = view(target_segment, target_segment, True)
    cross_view = view(target_segment, source_segment, False)

    entry_biases = mine(attention_biases[:, :2].reshape(3, 2, count, share), 2)
    exit_biases = attention_biases[:, 2]
    hidden_biases = mine(expander_biases.reshape(2, shards, count, -1), 2).reshape(2, 1, -1)

    def gain(norm):
        return norm_gains[norm : norm + 1]

    def shift(norm):
        return norm_shifts[norm : norm + 1]

    def exit_bias(block):
        return exit_biases[block : block + 1]

    source_pieces = spread(source_tokens)
    entries, leaves, expand, reduce = gather_weights(projections, combiners, expanders, reducers)
    target_pieces = spread(target_tokens)
    target_incoming, target_incoming_low, target_sum = join_gradient(
        target_cotangent, target_keep, []
    )
    target_incoming_pieces = spread(target_incoming_low)

    def self_forward(pieces, seen, causal, norm, block):
        normed, *projected = project_self(
            pieces, gain(norm), shift(norm), entries[block], entry_biases[block]
        )
        mixture, total, partials = attend_forward(
            *seen, *projected, leaves[block], heads, causal, count
        )
        return normed, (*projected, mixture, total), collect(partials)

    encoder_normed, encoder_stored, addends = self_forward(
        source_pieces, encoder_view, False, 0, 0
    )
    middle, middle_normed = residual_norm(source_tokens, addends, exit_bias(0), gain(1), shift(1))
    middle_pieces = spread(middle_normed)
    decoder_normed, decoder_stored, addends = self_forward(target_pieces, self_view, True, 2, 1)
    self_out, self_normed = residual_norm(target_tokens, addends, exit_bias(1), gain(3), shift(3))
    self_pieces = spread(self_normed)
    encoder_active, encoder_slope, partials = feed_forward(
        middle_pieces, expand[0], reduce[0], hidden_biases[0]
    )
    memory_low = residual_low(middle, collect(partials), reducer_biases[0:1])
    memory_pieces = spread(memory_low)
    cross_projected = project_cross(self_pieces, memory_pieces, entries[2], entry_biases[2])
    mixture, total, partials = attend_forward(
        *cross_view, *cross_projected, leaves[2], heads, False, count
    )
    cross_stored = (*cross_projected, mixture, total)
    cross_out, cross_normed = residual_norm(
        self_out, collect(partials), exit_bias(2), gain(4), shift(4)
    )
    cross_pieces = spread(cross_normed)
    decoder_active, decoder_slope, partials = feed_forward(
        cross_pieces, expand[1], reduce[1], hidden_biases[1]
    )
    decoded_low = residual_low(cross_out, collect(partials), reducer_biases[1:2])

    order = line_order(1) if in_line() else None

    def send(blocks):
        if order is not None:
            return scatter_line(*blocks)
        return [
            lax.psum_scatter(part, "batch", scatter_dimension=0, tiled=True) for part in blocks
        ]

    def feed_gradients(pieces, normed_pieces, hidden, active):
        pairs = [
            (normed_pieces, [hidden], 0, hidden.shape[1]),
            ([active], pieces, 0, model_width),
        ]
        return send(outer_sums(pairs, order, "feed_weights", True))

    def attention_gradients(pairs):
        return send(outer_sums(pairs, order, "attention_weights"))

    hidden, decoder_hidden_sum, partials = feed_backward(
        target_incoming_pieces, expand[1], reduce[1], decoder_slope
    )
    incoming, incoming_low, norm_four = norm_backward(
        cross_out, gain(4), target_incoming, collect(partials)
    )
    incoming_pieces = spread(incoming_low)
    decoder_feed_shares = feed_gradients(
        target_incoming_pieces, cross_pieces, hidden, decoder_active
    )
    cross_joined, cross_sums, cross_exit, partials, memory_partials = attend_backward(
        *cross_view, incoming_pieces, leaves[2], entries[2], cross_stored, heads, False, True
    )
    source_incoming, source_incoming_low, source_sum = join_gradient(
        source_cotangent, source_keep, collect(memory_partials)
    )
    source_incoming_pieces = spread(source_incoming_low)
    self_incoming, self_incoming_low, norm_three = norm_backward(
        self_out, gain(3), incoming, collect(partials)
    )
    self_incoming_pieces = spread(self_incoming_low)
    cross_shares = attention_gradients(
        [
            (self_pieces, [cross_joined], 0, share),
            (memory_pieces, [cross_joined], share, 2 * share),
        ]
    )
    hidden, encoder_hidden_sum, partials = feed_backward(
        source_incoming_pieces, expand[0], reduce[0], encoder_slope
    )
    middle_incoming, middle_incoming_low, norm_one = norm_backward(
        middle, gain(1), source_incoming, collect(partials)
    )
    middle_incoming_pieces = spread(middle_incoming_low)
    decoder_joined, decoder_sums, decoder_exit, partials, _ = attend_backward(
        *self_view, self_incoming_pieces, leaves[1], entries[1], decoder_stored, heads, True, False
    )
    target_gradient, _, norm_two = norm_backward(
        target_tokens, gain(2), self_incoming, collect(partials)
    )
    encoder_feed_shares = feed_gradients(
        source_incoming_pieces, middle_pieces, hidden, encoder_active
    )
    decoder_shares = attention_gradients([([decoder_normed], [decoder_joined], 0, 3 * share)])
    encoder_joined, encoder_sums, encoder_exit, partials, _ = attend_backward(
        *encoder_view,
        middle_incoming_pieces,
        leaves[0],
        entries[0],
        encoder_stored,
        heads,
        False,
        False,
    )
    encoder_shares = attention_gradients([([encoder_normed], [encoder_joined], 0, 3 * share)])
    source_gradient, _, norm_zero = norm_backward(
        source_tokens, gain(0), middle_incoming, collect(partials)
    )

    exits = [encoder_exit, decoder_exit, cross_exit]
    rows = projections.shape[1]
    if order is not None:
        table = ((order % 2) * (shards // 2) + order // 2) * (share // shards)
        pieces = scatter_line(*order_combiners(exits, table))
        combiners_gradient = return_combiners(pieces, 3)
        entry_shares = [encoder_shares, decoder_shares, cross_shares]
        expand_shares = [part[:rows] for part in (encoder_feed_shares, decoder_feed_shares)]
        reduce_shares = [part[rows:] for part in (encoder_feed_shares, decoder_feed_shares)]
    else:
        wholes = [
            lax.dynamic_update_slice(
                jnp.zeros((count,) + part.shape, low), part[None], (me, 0, 0)
            ).reshape(-1, model_width)
            for part in exits
        ]
        combiners_gradient = lax.psum(jnp.stack([send([part])[0] for part in wholes]), "seq")
        entry_shares = [encoder_shares[0], decoder_shares[0]]
        entry_shares.append(jnp.concatenate(cross_shares, 1))
        expand_shares = [encoder_feed_shares[0], decoder_feed_shares[0]]
        reduce_shares = [encoder_feed_shares[1], decoder_feed_shares[1]]

    def whole_entry(part):
        joined = spread_order([p.reshape(rows, 3, share) for p in spread(part)], 2)
        return joined.reshape(rows, -1)

    def whole_expand(part):
        joined = spread_order([p.reshape(rows, shards, -1) for p in spread(part)], 2)
        return joined.reshape(rows, -1)

    def whole_reduce(part):
        return spread_order(spread(part), 0).reshape(-1, model_width)

    projections_gradient = jnp.stack([whole_entry(part) for part in entry_shares]).astype(high)
    expanders_gradient = jnp.stack([whole_expand(part) for part in expand_shares]).astype(high)
    reducers_gradient = jnp.stack([whole_reduce(part) for part in reduce_shares]).astype(high)

    norms = (norm_zero, norm_one, norm_two, norm_three, norm_four)
    norm_sums = jnp.stack([sums[:2] for sums in norms])
    inner = jnp.stack([encoder_sums, decoder_sums, cross_sums])
    inner_whole = lax.dynamic_update_slice(
        jnp.zeros((3, 2, count, share), high), inner[:, :, None], (0, 0, me, 0)
    )
    outer = jnp.stack([norm_one[2], norm_three[2], norm_four[2]])
    hidden_sums = jnp.stack([encoder_hidden_sum, decoder_hidden_sum]).reshape(2, shards, 1, -1)
    hidden_whole = lax.dynamic_update_slice(
        jnp.zeros((2, shards, count, hidden_sums.shape[3]), high), hidden_sums, (0, 0, me, 0)
    )
    exit_sums = jnp.concatenate([source_sum, target_sum])
    parts = [norm_sums, inner_whole, outer, hidden_whole, exit_sums]
    summed = sum_everywhere(jnp.concatenate([part.reshape(-1, 128) for part in parts], 0))
    sizes = [part.size // 128 for part in parts]
    starts = [sum(sizes[:i]) for i in range(len(sizes))]
    norm_sums, inner_whole, outer, hidden_whole, exit_sums = [
        summed[start : start + size].reshape(part.shape)
        for start, size, part in zip(starts, sizes, parts)
    ]
    return (
        memory_low[None],
        decoded_low[None],
        source_gradient[None],
        target_gradient[None],
        projections_gradient,
        combiners_gradient.astype(high),
        expanders_gradient,
        reducers_gradient,
        norm_sums[:, 0],
        norm_sums[:, 1],
        jnp.concatenate([inner_whole.reshape(3, 2, -1), outer[:, None]], 1),
        hidden_whole.reshape(2, -1),
        exit_sums,
    )


def solution(mesh):
    in_specs = (
        P("batch", "seq", None),
        P("batch", "seq", None),
        P("batch", None),
        P("batch", None),
        P(None, "batch", None),
        P(None, "batch", None),
        P(None, "batch", None),
        P(None, "batch", None),
        P(),
        P(),
        P(),
        P(),
        P(),
        P("batch", "seq", None),
        P("batch", "seq", None),
    )
    out_specs = (
        P("batch", "seq", None),
        P("batch", "seq", None),
        P("batch", "seq", None),
        P("batch", "seq", None),
        P(None, "batch", None),
        P(None, "batch", None),
        P(None, "batch", None),
        P(None, "batch", None),
        P(),
        P(),
        P(),
        P(),
        P(),
    )
    return jax.shard_map(
        per_device, mesh=mesh, in_specs=in_specs, out_specs=out_specs, check_vma=False
    )
```

time: 988 us -> 831 us (0.84)
  matrix products: 248 us -> 0 us
  Pallas kernels: 0 us -> 168 us
  starting transfers between devices: 84 us -> 197 us
  other arithmetic: 145 us -> 59.2 us
  waiting for transfers between devices: 308 us -> 224 us
  between operations: 26.5 us -> 11.9 us
    dot_general x51 -> x0, matrix products: 248 us -> none  [the longest x11 47.3 us: times(): jnp.einsum('sd,de->se', left, right, preferred_element_type=jnp.float32)]
    pallas_call x0 -> x36, Pallas kernels: none -> 168 us  [run(): pl.pallas_call(kernel, out_shape=list(outs), in_specs=[SMEM] * scalars +...]
    ppermute x57 -> x126, starting transfers between devices: 77.3 us -> 180 us  [swap(): lax.ppermute(values, axis, [(i, i ^ bit) for i in range(lax.axis_size(axi...]
    ppermute x0 -> x33, waiting for transfers between devices: none -> 97 us  [line_shift(): lax.ppermute(values, 'batch', [(i, (i + 2) % shards) for i in range(shard...]
    all_gather x5 -> x0, waiting for transfers between devices: 68.5 us -> none  [gather_batch(): return lax.all_gather(values, 'batch', axis=0, tiled=False)]
    ppermute x57 -> x126, waiting for transfers between devices: 188 us -> 127 us  [swap(): lax.ppermute(values, axis, [(i, i ^ bit) for i in range(lax.axis_size(axi...]
    reduce_scatter x5 -> x0, waiting for transfers between devices: 49.3 us -> none  [scatter_batch(): return lax.psum_scatter(values, 'batch', scatter_dimension=0, tiled=False)]
    reduce_sum x27 -> x0, other arithmetic: 40.1 us -> none  [the longest x3 11 us: attend_forward(): row_sum = jnp.sum(exponent, -1, keepdims=True)]
  transfers between devices with their start and end apart: 73 -> 165, of which waited for: 31 -> 53; matrix products, arithmetic and copies ran while one was open for 45% -> 20% of each run, Pallas kernels for 0% -> 20%
where the time goes in v2:
time: 831 us; the launch traced here: 822 us
  waiting for transfers between devices  224 us (27%)
  starting transfers between devices  197 us (24%)
  Pallas kernels  168 us (20%)
  local copies, waits for them, and re-layouts  162 us (19%)
  other arithmetic  59.2 us (7%)
  between operations  11.9 us (1%)
    ppermute x126, starting transfers between devices, swap(): lax.ppermute(values, axis, [(i, i ^ bit) for i in range(lax.axis_size(axi...  180 us
    pallas_call x36, Pallas kernels, run(): pl.pallas_call(kernel, out_shape=list(outs), in_specs=[SMEM] * scalars +...  168 us
    ppermute x126, waiting for transfers between devices, swap(): lax.ppermute(values, axis, [(i, i ^ bit) for i in range(lax.axis_size(axi...  127 us
    ppermute x33, waiting for transfers between devices, line_shift(): lax.ppermute(values, 'batch', [(i, (i + 2) % shards) for i in range(shard...  97 us
    unnamed x508, local copies, waits for them, and re-layouts  84.2 us
    convert_element_type x35, other arithmetic, sum_low(): return total.astype(low)  29.9 us
    dynamic_slice x17, local copies, waits for them, and re-layouts, spread_order(): lax.dynamic_index_in_dim(stacked, offsets[me ^ i], 0, keepdims=False)  18.3 us
  transfers between devices with their start and end apart: 165, of which 53 were waited for; matrix products, arithmetic and copies ran while one was open for 20% of the time, Pallas kernels for 20%

profile of v2, /device:TPU:1, one launch (start us, length us, event | category | flops | bytes accessed | tf_op | source)
XLA Modules:
  0.0 822.0 jit_solution(7435220292234119542)
XLA Ops:
  38.1 7.0 collective-permute-done.13.refs_1_
  46.9 9.1 %collective-permute-start.2 = (bf16[256,1024]{1,0:T(8,128)(2,1)}, bf16[256,1024]{1,0:T(8,128)(2,1)S(1)}, u32[]{:S(2)}, u32[]{:S(2)}) collective-permute-start(bf16[256,1024]{1,0:T(8,128)(2,1)} %collective-permute-done.refs_1_), channel_id=1, source_target_pairs={{0,1},{1,0},{2,3},{3,2},{4,5},{5,4},{6,7},{7,6},{8,9},{9,8},{10,11... | collective-permute-start | bytes 1572872 | tf_op jit(solution)/shard_map/ppermute | solution.py:554
  91.0 10.6 %attend_forward.3 = (bf16[1024,256]{1,0:T(8,128)(2,1)S(1)}, f32[8,1024]{1,0:T(8,128)S(1)}, bf16[256,1024]{1,0:T(8,128)(2,1)S(1)}, bf16[256,1024]{1,0:T(8,128)(2,...) custom-call(s32[4,4]{1,0:T(4,128)S(1)} %get-tuple-element.384.refs_0_, s32[1024,1]{1,0:T(8,128)S(1)} %copy.164.refs_1_, ...), custom_call_target="tpu_custom_call" | custom-call | flops 2684354560 | bytes 4767808 | tf_op jit(solution)/shard_map/attend_forward/pallas_call | solution.py:26
  101.8 9.0 %collective-permute-start.21 = (bf16[256,1024]{1,0:T(8,128)(2,1)S(1)}, bf16[256,1024]{1,0:T(8,128)(2,1)S(1)}, u32[]{:S(2)}, u32[]{:S(2)}) collective-permute-start(bf16[256,1024]{1,0:T(8,128)(2,1)S(1)} %get-tuple-element.155), channel_id=1, source_target_pairs={{0,1},{1,0},{2,3},{3,2},{4,5},{5,4},{6,7},{7,6},{8,9},{9,8},{10,11... | collective-permute-start | bytes 1572872 | tf_op jit(solution)/shard_map/ppermute | solution.py:554
  117.7 8.9 %collective-permute-done.28.refs_3_ = bf16[256,1024]{1,0:T(8,128)(2,1)S(1)} collective-permute-done((bf16[256,1024]{1,0:T(8,128)(2,1)S(1)}, bf16[256,1024]{1,0:T(8,128)(2,1)S(1)}, u32[]{:S(2)}, u32[]{:S(2)}) %collective-permute-start.28) | collective-permute-done | bytes 524320 | tf_op jit(solution)/shard_map/ppermute | solution.py:607
  141.4 13.4 %collective-permute-start.24 = (bf16[256,1024]{1,0:T(8,128)(2,1)S(1)}, bf16[256,1024]{1,0:T(8,128)(2,1)S(1)}, u32[]{:S(2)}, u32[]{:S(2)}) collective-permute-start(bf16[256,1024]{1,0:T(8,128)(2,1)S(1)} %get-tuple-element.157.refs_0_), channel_id=1, source_target_pairs={{0,1},{1,0},{2,3},{3,2},{4,5},{5,4},{6,7},{7,6},{8,9},{9,8},{10,11... | collective-permute-start | bytes 1572872 | tf_op jit(solution)/shard_map/ppermute | solution.py:554
  186.8 7.3 feed_forward.2
  203.2 8.4 %collective-permute-done.45.refs_7_ = bf16[256,768]{1,0:T(8,128)(2,1)S(1)} collective-permute-done((bf16[256,768]{1,0:T(8,128)(2,1)}, bf16[256,768]{1,0:T(8,128)(2,1)S(1)}, u32[]{:S(2)}, u32[]{:S(2)}) %collective-permute-start.45) | collective-permute-done | bytes 393248 | tf_op jit(solution)/shard_map/ppermute | solution.py:554
  219.7 7.6 attend_forward.4
  233.5 10.4 %collective-permute-done.35.refs_3_ = bf16[256,1024]{1,0:T(8,128)(2,1)S(1)} collective-permute-done((bf16[256,1024]{1,0:T(8,128)(2,1)S(1)}, bf16[256,1024]{1,0:T(8,128)(2,1)S(1)}, u32[]{:S(2)}, u32[]{:S(2)}) %collective-permute-start.35) | collective-permute-done | bytes 524320 | tf_op jit(solution)/shard_map/ppermute | solution.py:554
  246.2 9.0 %collective-permute-done.48.refs_3_ = bf16[256,1024]{1,0:T(8,128)(2,1)S(1)} collective-permute-done((bf16[256,1024]{1,0:T(8,128)(2,1)S(1)}, bf16[256,1024]{1,0:T(8,128)(2,1)S(1)}, u32[]{:S(2)}, u32[]{:S(2)}) %collective-permute-start.48) | collective-permute-done | bytes 524320 | tf_op jit(solution)/shard_map/ppermute | solution.py:554
  259.4 7.0 collective-permute-done.52.refs_5_.refs_6_
  267.9 9.7 %collective-permute-done.49.refs_1_ = bf16[256,1024]{1,0:T(8,128)(2,1)S(1)} collective-permute-done((bf16[256,1024]{1,0:T(8,128)(2,1)S(1)}, bf16[256,1024]{1,0:T(8,128)(2,1)S(1)}, u32[]{:S(2)}, u32[]{:S(2)}) %collective-permute-start.49) | collective-permute-done | bytes 524320 | tf_op jit(solution)/shard_map/ppermute | solution.py:554
  282.1 10.0 %attend_forward.5 = (bf16[1024,256]{1,0:T(8,128)(2,1)S(1)}, f32[8,1024]{1,0:T(8,128)S(1)}, bf16[256,1024]{1,0:T(8,128)(2,1)S(1)}, bf16[256,1024]{1,0:T(8,128)(2,...) custom-call(s32[4,4]{1,0:T(4,128)S(1)} %copy-done.126, s32[1024,1]{1,0:T(8,128)S(1)} %copy-done.46, ...), custom_call_target="tpu_custom_call" | custom-call | flops 2684354560 | bytes 4767808 | tf_op jit(solution)/shard_map/attend_forward/pallas_call | solution.py:26
  301.5 8.7 %collective-permute-done.62.refs_2_ = bf16[256,1024]{1,0:T(8,128)(2,1)} collective-permute-done((bf16[256,1024]{1,0:T(8,128)(2,1)S(1)}, bf16[256,1024]{1,0:T(8,128)(2,1)}, u32[]{:S(2)}, u32[]{:S(2)}) %collective-permute-start.62) | collective-permute-done | bytes 524320 | tf_op jit(solution)/shard_map/ppermute | solution.py:607
  344.7 6.1 collective-permute-done.67.refs_7_
  352.3 6.8 feed_forward.3
  376.2 12.0 %collective-permute-done.76.refs_5_ = bf16[256,1024]{1,0:T(8,128)(2,1)S(1)} collective-permute-done((bf16[256,1024]{1,0:T(8,128)(2,1)S(1)}, bf16[256,1024]{1,0:T(8,128)(2,1)S(1)}, u32[]{:S(2)}, u32[]{:S(2)}) %collective-permute-start.76) | collective-permute-done | bytes 524320 | tf_op jit(solution)/shard_map/ppermute | solution.py:554
  389.3 8.4 %collective-permute-done.146 = bf16[2,256,1024]{2,1,0:T(8,128)(2,1)S(1)} collective-permute-done((bf16[2,256,1024]{2,1,0:T(8,128)(2,1)S(1)}, bf16[2,256,1024]{2,1,0:T(8,128)(2,1)S(1)}, u32[]{:S(2)}, u32[]{:S(2)}) %collective-permute-start.146) | collective-permute-done | bytes 1048608 | tf_op jit(solution)/shard_map/ppermute | solution.py:554
  404.6 7.9 collective-permute-done.147
  413.1 18.7 %attend_backward.3 = (bf16[1024,768]{1,0:T(8,128)(2,1)S(1)}, f32[2,256]{1,0:T(2,128)S(1)}, bf16[256,1024]{1,0:T(8,128)(2,1)S(1)}, bf16[256,1024]{1,0:T(8,128)(2,...) custom-call(s32[4,4]{1,0:T(4,128)S(1)} %copy-done.126, ...), custom_call_target="tpu_custom_call" | custom-call | flops 8053063680 | bytes 12634176 | tf_op jit(solution)/shard_map/attend_backward/pallas_call | solution.py:26
  501.8 8.8 %collective-permute-done.98.refs_6_ = bf16[256,1024]{1,0:T(8,128)(2,1)} collective-permute-done((bf16[256,1024]{1,0:T(8,128)(2,1)}, bf16[256,1024]{1,0:T(8,128)(2,1)}, u32[]{:S(2)}, u32[]{:S(2)}) %collective-permute-start.98) | collective-permute-done | bytes 524320 | tf_op jit(solution)/shard_map/ppermute | solution.py:554
  540.8 16.4 %attend_backward.5 = (bf16[1024,768]{1,0:T(8,128)(2,1)S(1)}, f32[2,256]{1,0:T(2,128)S(1)}, bf16[256,1024]{1,0:T(8,128)(2,1)S(1)}, bf16[256,1024]{1,0:T(8,128)(2,...) custom-call(s32[4,4]{1,0:T(4,128)S(1)} %copy-done.125, ...), custom_call_target="tpu_custom_call" | custom-call | flops 8053063680 | bytes 10537024 | tf_op jit(solution)/shard_map/attend_backward/pallas_call | solution.py:26
  559.9 6.1 feed_backward.3
  570.7 6.5 feed_weights.2
  604.8 5.7 collective-permute-start.118
  611.0 6.7 collective-permute-start.119
  648.8 20.5 %attend_backward.4 = (bf16[1024,768]{1,0:T(8,128)(2,1)S(1)}, f32[2,256]{1,0:T(2,128)S(1)}, bf16[256,1024]{1,0:T(8,128)(2,1)S(1)}, bf16[256,1024]{1,0:T(8,128)(2,...) custom-call(s32[4,4]{1,0:T(4,128)S(1)} %copy-done.124, ...), custom_call_target="tpu_custom_call" | custom-call | flops 8053063680 | bytes 10537024 | tf_op jit(solution)/shard_map/attend_backward/pallas_call | solution.py:26
  735.1 6.5 collective-permute-done.108
  774.1 5.6 copy.218
  802.5 6.2 collective-permute-start.137
  811.3 6.0 copy.217
  (1024 shorter events, 519.1 us)
Async XLA Ops:
  0.6 46.3 %collective-permute-start = (bf16[256,1024]{1,0:T(8,128)(2,1)}, bf16[256,1024]{1,0:T(8,128)(2,1)}, u32[]{:S(2)}, u32[]{:S(2)}) collective-permute-start(bf16[256,1024]{1,0:T(8,128)(2,1)} %bitcast.386), channel_id=1, source_target_pairs={{0,2},{1,3},{2,0},{3,1},{4,6},{5,7},{6,4},{7,5},{8,10},{9,11},{10,... | collective-permute-start | bytes 1572872 | tf_op jit(solution)/shard_map/ppermute | solution.py:554
  27.4 39.2 %collective-permute-start.1 = (bf16[256,1024]{1,0:T(8,128)(2,1)S(1)}, bf16[256,1024]{1,0:T(8,128)(2,1)S(1)}, u32[]{:S(2)}, u32[]{:S(2)}) collective-permute-start(bf16[256,1024]{1,0:T(8,128)(2,1)S(1)} %bitcast.387), channel_id=1, source_target_pairs={{0,1},{1,0},{2,3},{3,2},{4,5},{5,4},{6,7},{7,6},{8,9},{9,8},{10,11... | collective-permute-start | bytes 1572872 | tf_op jit(solution)/shard_map/ppermute | solution.py:554
  29.3 29.9 %collective-permute-start.6 = (bf16[128,768]{1,0:T(8,128)(2,1)S(1)}, bf16[128,768]{1,0:T(8,128)(2,1)S(1)}, u32[]{:S(2)}, u32[]{:S(2)}) collective-permute-start(bf16[128,768]{1,0:T(8,128)(2,1)S(1)} %copy.162.refs_0_), channel_id=1, source_target_pairs={{0,4},{4,0},{8,12},{12,8},{16,20},{20,16},{24,28},{28,24},{1,5},{5... | collective-permute-start | bytes 589832 | tf_op jit(solution)/shard_map/ppermute | solution.py:554
  66.3 35.4 %collective-permute-start.26 = (bf16[256,1024]{1,0:T(8,128)(2,1)S(1)}, bf16[256,1024]{1,0:T(8,128)(2,1)S(1)}, u32[]{:S(2)}, u32[]{:S(2)}) collective-permute-start(bf16[256,1024]{1,0:T(8,128)(2,1)S(1)} %pad_maximum_fusion.12.refs_0_), channel_id=1, source_target_pairs={{0,8},{4,12},{8,16},{12,20},{16,24},{20,28},{24,0},{28,4},{1,9},{5... | collective-permute-start | bytes 1572872 | tf_op jit(solution)/shard_map/ppermute | solution.py:607
  126.6 29.0 %collective-permute-start.30 = (bf16[256,1024]{1,0:T(8,128)(2,1)S(1)}, bf16[256,1024]{1,0:T(8,128)(2,1)}, u32[]{:S(2)}, u32[]{:S(2)}) collective-permute-start(bf16[256,1024]{1,0:T(8,128)(2,1)S(1)} %collective-permute-done.26.refs_1_), channel_id=1, source_target_pairs={{0,4},{4,0},{8,12},{12,8},{16,20},{20,16},{24,28},{28,24},{1,5},{5... | collective-permute-start | bytes 1572872 | tf_op jit(solution)/shard_map/ppermute | solution.py:554
  155.7 29.7 %collective-permute-start.25 = (bf16[256,1024]{1,0:T(8,128)(2,1)}, bf16[256,1024]{1,0:T(8,128)(2,1)}, u32[]{:S(2)}, u32[]{:S(2)}) collective-permute-start(bf16[256,1024]{1,0:T(8,128)(2,1)} %collective-permute-done.23.refs_1_), channel_id=1, source_target_pairs={{0,1},{1,0},{2,3},{3,2},{4,5},{5,4},{6,7},{7,6},{8,9},{9,8},{10,11... | collective-permute-start | bytes 1572872 | tf_op jit(solution)/shard_map/ppermute | solution.py:554
  162.5 50.6 %collective-permute-start.37 = (bf16[256,1024]{1,0:T(8,128)(2,1)S(1)}, bf16[256,1024]{1,0:T(8,128)(2,1)}, u32[]{:S(2)}, u32[]{:S(2)}) collective-permute-start(bf16[256,1024]{1,0:T(8,128)(2,1)S(1)} %bitcast.382), channel_id=1, source_target_pairs={{0,1},{1,0},{2,3},{3,2},{4,5},{5,4},{6,7},{7,6},{8,9},{9,8},{10,11... | collective-permute-start | bytes 1572872 | tf_op jit(solution)/shard_map/ppermute | solution.py:554
  170.4 42.7 %collective-permute-start.38 = (bf16[256,1024]{1,0:T(8,128)(2,1)}, bf16[256,1024]{1,0:T(8,128)(2,1)}, u32[]{:S(2)}, u32[]{:S(2)}) collective-permute-start(bf16[256,1024]{1,0:T(8,128)(2,1)} %collective-permute-done.36.refs_1_), channel_id=1, source_target_pairs={{0,1},{1,0},{2,3},{3,2},{4,5},{5,4},{6,7},{7,6},{8,9},{9,8},{10,11... | collective-permute-start | bytes 1572872 | tf_op jit(solution)/shard_map/ppermute | solution.py:554
  196.9 31.1 %collective-permute-start.34 = (bf16[256,1024]{1,0:T(8,128)(2,1)S(1)}, bf16[256,1024]{1,0:T(8,128)(2,1)S(1)}, u32[]{:S(2)}, u32[]{:S(2)}) collective-permute-start(bf16[256,1024]{1,0:T(8,128)(2,1)S(1)} %get-tuple-element.164), channel_id=1, source_target_pairs={{0,1},{1,0},{2,3},{3,2},{4,5},{5,4},{6,7},{7,6},{8,9},{9,8},{10,11... | collective-permute-start | bytes 1572872 | tf_op jit(solution)/shard_map/ppermute | solution.py:554
  325.8 26.4 %collective-permute-start.59 = (bf16[256,1024]{1,0:T(8,128)(2,1)S(1)}, bf16[256,1024]{1,0:T(8,128)(2,1)S(1)}, u32[]{:S(2)}, u32[]{:S(2)}) collective-permute-start(bf16[256,1024]{1,0:T(8,128)(2,1)S(1)} %get-tuple-element.187.refs_0_), channel_id=1, source_target_pairs={{0,1},{1,0},{2,3},{3,2},{4,5},{5,4},{6,7},{7,6},{8,9},{9,8},{10,11... | collective-permute-start | bytes 1572872 | tf_op jit(solution)/shard_map/ppermute | solution.py:554
  398.1 47.4 %collective-permute-start.68 = (bf16[256,1024]{1,0:T(8,128)(2,1)}, bf16[256,1024]{1,0:T(8,128)(2,1)}, u32[]{:S(2)}, u32[]{:S(2)}) collective-permute-start(bf16[256,1024]{1,0:T(8,128)(2,1)} %get-tuple-element.192), channel_id=1, source_target_pairs={{0,1},{1,0},{2,3},{3,2},{4,5},{5,4},{6,7},{7,6},{8,9},{9,8},{10,11... | collective-permute-start | bytes 1572872 | tf_op jit(solution)/shard_map/ppermute | solution.py:554
  399.0 36.3 %collective-permute-start.149 = (bf16[2,256,1024]{2,1,0:T(8,128)(2,1)S(1)}, bf16[2,256,1024]{2,1,0:T(8,128)(2,1)S(1)}, u32[]{:S(2)}, u32[]{:S(2)}) collective-permute-start(bf16[2,256,1024]{2,1,0:T(8,128)(2,1)S(1)} %get-tuple-element.268), channel_id=1, source_target_pairs={{0,4},{4,0},{8,12},{12,8},{16,20},{20,16},{24,28},{28,24},{1,5},{5... | collective-permute-start | bytes 3145736 | tf_op jit(solution)/shard_map/ppermute | solution.py:554
  412.5 32.9 %collective-permute-start.70 = (bf16[256,1024]{1,0:T(8,128)(2,1)}, bf16[256,1024]{1,0:T(8,128)(2,1)}, u32[]{:S(2)}, u32[]{:S(2)}) collective-permute-start(bf16[256,1024]{1,0:T(8,128)(2,1)} %add_convert_fusion.8), channel_id=1, source_target_pairs={{0,2},{1,3},{2,0},{3,1},{4,6},{5,7},{6,4},{7,5},{8,10},{9,11},{10,... | collective-permute-start | bytes 1572872 | tf_op jit(solution)/shard_map/ppermute | solution.py:554
  450.9 35.0 %collective-permute-start.95 = (bf16[256,1024]{1,0:T(8,128)(2,1)}, bf16[256,1024]{1,0:T(8,128)(2,1)}, u32[]{:S(2)}, u32[]{:S(2)}) collective-permute-start(bf16[256,1024]{1,0:T(8,128)(2,1)} %get-tuple-element.227), channel_id=1, source_target_pairs={{0,1},{1,0},{2,3},{3,2},{4,5},{5,4},{6,7},{7,6},{8,9},{9,8},{10,11... | collective-permute-start | bytes 1572872 | tf_op jit(solution)/shard_map/ppermute | solution.py:554
  493.6 28.1 %collective-permute-start.126 = (bf16[128,768]{1,0:T(8,128)(2,1)}, bf16[128,768]{1,0:T(8,128)(2,1)}, u32[]{:S(2)}, u32[]{:S(2)}) collective-permute-start(bf16[128,768]{1,0:T(8,128)(2,1)} %fusion.11), channel_id=1, source_target_pairs={{0,1},{1,0},{2,3},{3,2},{4,5},{5,4},{6,7},{7,6},{8,9},{9,8},{10,11... | collective-permute-start | bytes 589832 | tf_op jit(solution)/shard_map/ppermute | solution.py:554
  498.6 35.5 %collective-permute-start.99 = (bf16[256,1024]{1,0:T(8,128)(2,1)}, bf16[256,1024]{1,0:T(8,128)(2,1)}, u32[]{:S(2)}, u32[]{:S(2)}) collective-permute-start(bf16[256,1024]{1,0:T(8,128)(2,1)} %get-tuple-element.231.refs_5_), channel_id=1, source_target_pairs={{0,1},{1,0},{2,3},{3,2},{4,5},{5,4},{6,7},{7,6},{8,9},{9,8},{10,11... | collective-permute-start | bytes 1572872 | tf_op jit(solution)/shard_map/ppermute | solution.py:554
  500.4 33.2 %collective-permute-start.83 = (bf16[256,1024]{1,0:T(8,128)(2,1)}, bf16[256,1024]{1,0:T(8,128)(2,1)}, u32[]{:S(2)}, u32[]{:S(2)}) collective-permute-start(bf16[256,1024]{1,0:T(8,128)(2,1)} %get-tuple-element.210.refs_0_.refs_6_), channel_id=1, source_target_pairs={{0,2},{1,3},{2,0},{3,1},{4,6},{5,7},{6,4},{7,5},{8,10},{9,11},{10,... | collective-permute-start | bytes 1572872 | tf_op jit(solution)/shard_map/ppermute | solution.py:554
  521.8 38.1 %collective-permute-start.84 = (bf16[256,1024]{1,0:T(8,128)(2,1)}, bf16[256,1024]{1,0:T(8,128)(2,1)}, u32[]{:S(2)}, u32[]{:S(2)}) collective-permute-start(bf16[256,1024]{1,0:T(8,128)(2,1)} %get-tuple-element.210.refs_0_.refs_6_), channel_id=1, source_target_pairs={{0,1},{1,0},{2,3},{3,2},{4,5},{5,4},{6,7},{7,6},{8,9},{9,8},{10,11... | collective-permute-start | bytes 1572872 | tf_op jit(solution)/shard_map/ppermute | solution.py:554
  566.0 27.3 %collective-permute-start.86 = (bf16[256,1024]{1,0:T(8,128)(2,1)S(1)}, bf16[256,1024]{1,0:T(8,128)(2,1)S(1)}, u32[]{:S(2)}, u32[]{:S(2)}) collective-permute-start(bf16[256,1024]{1,0:T(8,128)(2,1)S(1)} %get-tuple-element.213), channel_id=1, source_target_pairs={{0,1},{1,0},{2,3},{3,2},{4,5},{5,4},{6,7},{7,6},{8,9},{9,8},{10,11... | collective-permute-start | bytes 1572872 | tf_op jit(solution)/shard_map/ppermute | solution.py:554
  592.4 27.7 %collective-permute-start.103 = (bf16[256,1024]{1,0:T(8,128)(2,1)}, bf16[256,1024]{1,0:T(8,128)(2,1)}, u32[]{:S(2)}, u32[]{:S(2)}) collective-permute-start(bf16[256,1024]{1,0:T(8,128)(2,1)} %add_convert_fusion.2), channel_id=1, source_target_pairs={{0,2},{1,3},{2,0},{3,1},{4,6},{5,7},{6,4},{7,5},{8,10},{9,11},{10,... | collective-permute-start | bytes 1572872 | tf_op jit(solution)/shard_map/ppermute | solution.py:554
  596.7 33.4 %collective-permute-start.89 = (bf16[256,1024]{1,0:T(8,128)(2,1)}, bf16[256,1024]{1,0:T(8,128)(2,1)}, u32[]{:S(2)}, u32[]{:S(2)}) collective-permute-start(bf16[256,1024]{1,0:T(8,128)(2,1)} %get-tuple-element.217.refs_5_), channel_id=1, source_target_pairs={{0,2},{1,3},{2,0},{3,1},{4,6},{5,7},{6,4},{7,5},{8,10},{9,11},{10,... | collective-permute-start | bytes 1572872 | tf_op jit(solution)/shard_map/ppermute | solution.py:554
  601.4 38.2 %collective-permute-start.139 = (bf16[256,1024]{1,0:T(8,128)(2,1)}, bf16[256,1024]{1,0:T(8,128)(2,1)}, u32[]{:S(2)}, u32[]{:S(2)}) collective-permute-start(bf16[256,1024]{1,0:T(8,128)(2,1)} %fusion.6), channel_id=1, source_target_pairs={{0,8},{4,12},{8,16},{12,20},{16,24},{20,28},{24,0},{28,4},{1,9},{5... | collective-permute-start | bytes 1572872 | tf_op jit(solution)/shard_map/ppermute | solution.py:607
  620.1 63.4 %collective-permute-start.141 = (bf16[2,256,1024]{2,1,0:T(8,128)(2,1)}, bf16[2,256,1024]{2,1,0:T(8,128)(2,1)}, u32[]{:S(2)}, u32[]{:S(2)}) collective-permute-start(bf16[2,256,1024]{2,1,0:T(8,128)(2,1)} %copy-done.137), channel_id=1, source_target_pairs={{0,4},{4,0},{8,12},{12,8},{16,20},{20,16},{24,28},{28,24},{1,5},{5... | collective-permute-start | bytes 3145736 | tf_op jit(solution)/shard_map/ppermute | solution.py:554
  642.1 42.9 %collective-permute-start.140 = (bf16[256,1024]{1,0:T(8,128)(2,1)}, bf16[256,1024]{1,0:T(8,128)(2,1)}, u32[]{:S(2)}, u32[]{:S(2)}) collective-permute-start(bf16[256,1024]{1,0:T(8,128)(2,1)} %fusion.5), channel_id=1, source_target_pairs={{0,8},{4,12},{8,16},{12,20},{16,24},{20,28},{24,0},{28,4},{1,9},{5... | collective-permute-start | bytes 1572872 | tf_op jit(solution)/shard_map/ppermute | solution.py:607
  677.6 84.1 %collective-permute-start.92 = (bf16[256,1024]{1,0:T(8,128)(2,1)}, bf16[256,1024]{1,0:T(8,128)(2,1)}, u32[]{:S(2)}, u32[]{:S(2)}) collective-permute-start(bf16[256,1024]{1,0:T(8,128)(2,1)} %copy-done.153), channel_id=1, source_target_pairs={{0,1},{1,0},{2,3},{3,2},{4,5},{5,4},{6,7},{7,6},{8,9},{9,8},{10,11... | collective-permute-start | bytes 1572872 | tf_op jit(solution)/shard_map/ppermute | solution.py:554
  677.9 27.4 %collective-permute-start.93 = (bf16[256,1024]{1,0:T(8,128)(2,1)}, bf16[256,1024]{1,0:T(8,128)(2,1)}, u32[]{:S(2)}, u32[]{:S(2)}) collective-permute-start(bf16[256,1024]{1,0:T(8,128)(2,1)} %copy-done.160), channel_id=1, source_target_pairs={{0,1},{1,0},{2,3},{3,2},{4,5},{5,4},{6,7},{7,6},{8,9},{9,8},{10,11... | collective-permute-start | bytes 1572872 | tf_op jit(solution)/shard_map/ppermute | solution.py:554
  687.4 27.6 %collective-permute-start.107 = (bf16[2,128,768]{2,1,0:T(8,128)(2,1)}, bf16[2,128,768]{2,1,0:T(8,128)(2,1)S(1)}, u32[]{:S(2)}, u32[]{:S(2)}) collective-permute-start(bf16[2,128,768]{2,1,0:T(8,128)(2,1)} %copy-done.165), channel_id=1, source_target_pairs={{0,4},{4,0},{8,12},{12,8},{16,20},{20,16},{24,28},{28,24},{1,5},{5... | collective-permute-start | bytes 1179656 | tf_op jit(solution)/shard_map/ppermute | solution.py:554
  726.6 31.9 %collective-permute-start.155 = (bf16[128,1024]{1,0:T(8,128)(2,1)}, bf16[128,1024]{1,0:T(8,128)(2,1)}, u32[]{:S(2)}, u32[]{:S(2)}) collective-permute-start(bf16[128,1024]{1,0:T(8,128)(2,1)} %get-tuple-element.354), channel_id=1, source_target_pairs={{0,1},{1,0},{2,3},{3,2},{4,5},{5,4},{6,7},{7,6},{8,9},{9,8},{10,11... | collective-permute-start | bytes 786440 | tf_op jit(solution)/shard_map/ppermute | solution.py:554
  731.6 30.8 %collective-permute-start.94 = (bf16[256,1024]{1,0:T(8,128)(2,1)}, bf16[256,1024]{1,0:T(8,128)(2,1)S(1)}, u32[]{:S(2)}, u32[]{:S(2)}) collective-permute-start(bf16[256,1024]{1,0:T(8,128)(2,1)} %add_convert_fusion.4), channel_id=1, source_target_pairs={{0,2},{1,3},{2,0},{3,1},{4,6},{5,7},{6,4},{7,5},{8,10},{9,11},{10,... | collective-permute-start | bytes 1572872 | tf_op jit(solution)/shard_map/ppermute | solution.py:554
  752.7 30.4 %collective-permute-start.109 = (bf16[128,768]{1,0:T(8,128)(2,1)}, bf16[128,768]{1,0:T(8,128)(2,1)}, u32[]{:S(2)}, u32[]{:S(2)}) collective-permute-start(bf16[128,768]{1,0:T(8,128)(2,1)} %fusion.17), channel_id=1, source_target_pairs={{0,2},{1,3},{2,0},{3,1},{4,6},{5,7},{6,4},{7,5},{8,10},{9,11},{10,... | collective-permute-start | bytes 589832 | tf_op jit(solution)/shard_map/ppermute | solution.py:554
  758.6 28.5 %collective-permute-start.110 = (bf16[128,768]{1,0:T(8,128)(2,1)}, bf16[128,768]{1,0:T(8,128)(2,1)}, u32[]{:S(2)}, u32[]{:S(2)}) collective-permute-start(bf16[128,768]{1,0:T(8,128)(2,1)} %fusion.17), channel_id=1, source_target_pairs={{0,1},{1,0},{2,3},{3,2},{4,5},{5,4},{6,7},{7,6},{8,9},{9,8},{10,11... | collective-permute-start | bytes 589832 | tf_op jit(solution)/shard_map/ppermute | solution.py:554
  773.0 28.5 %collective-permute-start.136 = (bf16[3,128,1024]{2,1,0:T(8,128)(2,1)S(1)}, bf16[3,128,1024]{2,1,0:T(8,128)(2,1)}, u32[]{:S(2)}, u32[]{:S(2)}) collective-permute-start(bf16[3,128,1024]{2,1,0:T(8,128)(2,1)S(1)} %bitcast.425), channel_id=1, source_target_pairs={{0,2},{1,3},{2,0},{3,1},{4,6},{5,7},{6,4},{7,5},{8,10},{9,11},{10,... | collective-permute-start | bytes 2359304 | tf_op jit(solution)/shard_map/ppermute | solution.py:554
  (370 other events, 4274.7 us)

commit v3 on v2

--- a/solution.py
+++ b/solution.py
@@ -6,6 +6,7 @@
 from jax.sharding import PartitionSpec as P
 
 HEADS = 16
+COST = 0.05
 
 
 epsilon = 1e-05
@@ -19,11 +20,29 @@
 across_lanes = (((1,), (1,)), ((), ()))
 
 
+class Turn:
+    last = None
+
+
+def after(values, earlier):
+    return lax.optimization_barrier((values, earlier))[0]
+
+
+def hold(values):
+    return values if Turn.last is None else after(values, Turn.last)
+
+
+def take_turn(call, args, skip=0):
+    args = list(args)
+    least = min(range(skip, len(args)), key=lambda i: args[i].size)
+    args[least] = hold(args[least])
+    results = call(*args)
+    Turn.last = min(results, key=lambda value: value.size)
+    return results
+
+
 def run(kernel, outs, args, name, flops, scratch=(), scalars=0, room=24):
-    moved = sum(a.size * a.dtype.itemsize for a in args) + sum(
-        o.size * jnp.dtype(o.dtype).itemsize for o in outs
-    )
-    return pl.pallas_call(
+    call = pl.pallas_call(
         kernel,
         out_shape=list(outs),
         in_specs=[SMEM] * scalars + [VMEM] * (len(args) - scalars),
@@ -31,10 +50,11 @@
         scratch_shapes=list(scratch),
         compiler_params=pltpu.CompilerParams(vmem_limit_bytes=room << 20),
         cost_estimate=pl.CostEstimate(
-            flops=int(flops), bytes_accessed=int(moved), transcendentals=0
+            flops=int(flops * COST), bytes_accessed=0, transcendentals=0
         ),
         name=name,
-    )(*args)
+    )
+    return take_turn(call, args)
 
 
 def normalize(values, gain, shift):
@@ -63,17 +83,33 @@
         start += piece.shape[0]
 
 
-def assemble(pieces, table, parts):
+def assemble(sources, table, parts, height):
+    counts = [source.shape[0] // height for source in sources]
+    spots = [(i, at) for i, count in enumerate(counts) for at in range(count)]
+
     def kernel(table_ref, *refs):
-        sources, outs = refs[: len(pieces)], refs[len(pieces) :]
+        outs = refs[len(sources) :]
         for which, (start, rows, _) in enumerate(parts):
-            for i, source in enumerate(sources):
-                at = pl.multiple_of(table_ref[which, i], rows)
-                outs[which][pl.ds(at, rows), :] = source[start : start + rows, :]
-
-    width = pieces[0].shape[1]
+            for i, (source, at) in enumerate(spots):
+                first = at * height + start
+                where = pl.ds(pl.multiple_of(table_ref[which, i], rows), rows)
+                outs[which][where, :] = refs[source][first : first + rows, :]
+
+    width = sources[0].shape[1]
     outs = [shape((whole, width), low) for _, _, whole in parts]
-    return run(kernel, outs, [table, *pieces], "assemble", 1, scalars=1)
+    return run(kernel, outs, [table, *sources], "assemble", 1, scalars=1)
+
+
+def part_rows(pieces, height, first, rows):
+    count = pieces.shape[0] // height
+
+    def kernel(source, out):
+        for i in range(count):
+            start = i * height + first
+            out[i * rows : (i + 1) * rows, :] = source[start : start + rows, :]
+
+    outs = [shape((count * rows, pieces.shape[1]), low)]
+    return run(kernel, outs, [pieces], "part_rows", 1)[0]
 
 
 def project_self(pieces, gain, shift, entry, biases):
@@ -131,20 +167,18 @@
     return jnp.where(allowed, 0.0, masked_score)
 
 
-def attend_forward(marks, tags, queries, keys, values, leave, heads, causal, count):
+def attend_forward(marks, tags, queries, keys, values, heads, causal):
     rows, width = queries.shape
     head_width = width // heads
     block = min(256, rows)
     blocks = rows // block
-    local = rows // count
     scale = head_width**-0.5
     tall = max(8, heads)
 
     def kernel(*refs):
         marks_ref, key_segment, query_segment, key_place, query_place = refs[:5]
-        query_ref, key_ref, value_ref, leave_ref, mixture_ref, total_ref = refs[5:11]
-        partial_refs = refs[11 : 11 + count]
-        score_ref, top_ref, sum_ref, mix_ref, value_turned = refs[11 + count :]
+        query_ref, key_ref, value_ref, mixture_ref, total_ref = refs[5:10]
+        score_ref, top_ref, sum_ref, mix_ref, value_turned = refs[10:]
         value_turned[...] = value_ref[...].astype(high).T.astype(low)
         total_ref[...] = jnp.zeros(total_ref.shape, high)
         for i in range(blocks):
@@ -197,12 +231,8 @@
                 mix_ref[features, :] = mix_ref[features, :] * (1.0 / sum_ref[row, :])
                 total_ref[row, cols] = top_ref[row, :] + jnp.log(sum_ref[row, :])
             mixture_ref[mine, :] = mix_ref[...].T.astype(low)
-        for i in range(count):
-            mine = pl.ds(i * local, local)
-            partial_refs[i][...] = matmul(mixture_ref[mine, :], leave_ref[...]).astype(low)
 
     outs = [shape((rows, width), low), shape((tall, rows), high)]
-    outs += [shape((local, leave.shape[1]), low)] * count
     scratch = [
         pltpu.VMEM((heads, rows, block), high),
         pltpu.VMEM((tall, block), high),
@@ -210,12 +240,20 @@
         pltpu.VMEM((width, block), high),
         pltpu.VMEM((width, rows), low),
     ]
-    flops = 8 * rows * rows * width + 2 * rows * width * leave.shape[1]
-    args = [marks, *tags, queries, keys, values, leave]
-    mixture, total, *partials = run(
-        kernel, outs, args, "attend_forward", flops, scratch, scalars=1
-    )
-    return mixture, total, partials
+    flops = 8 * rows * rows * width
+    args = [marks, *tags, queries, keys, values]
+    return run(kernel, outs, args, "attend_forward", flops, scratch, scalars=1)
+
+
+def project_out(mixture, leave, count):
+    local = mixture.shape[0] // count
+
+    def kernel(mixture_ref, leave_ref, *outs):
+        for i, out in enumerate(outs):
+            out[...] = matmul(mixture_ref[pl.ds(i * local, local), :], leave_ref[...]).astype(low)
+
+    outs = [shape((local, leave.shape[1]), low)] * count
+    return run(kernel, outs, [mixture, leave], "project_out", 2 * mixture.size * leave.shape[1])
 
 
 def attend_backward(marks, tags, pieces, leave, entry, stored, heads, causal, cross):
@@ -234,16 +272,12 @@
         leave_ref, entry_ref, query_ref, key_ref, value_ref, mixture_ref, total_ref = refs[
             5 + count : 12 + count
         ]
-        joined_ref, sums_ref, exit_ref = refs[12 + count : 15 + count]
-        partial_refs = refs[15 + count : 15 + 2 * count]
-        memory_refs = refs[15 + 2 * count : -5]
+        joined_ref, sums_ref = refs[12 + count : 14 + count]
+        partial_refs = refs[14 + count : 14 + 2 * count]
+        memory_refs = refs[14 + 2 * count : -5]
         incoming_mix, key_sum, value_sum, query_turned, key_turned = refs[-5:]
-        exit_sum = None
         for where, piece in piece_rows(incoming_refs):
             incoming_mix[where, :] = matmul_back(piece[...], leave_ref[...]).astype(low)
-            term = matmul_outer(mixture_ref[where, :], piece[...])
-            exit_sum = term if exit_sum is None else exit_sum + term
-        exit_ref[...] = exit_sum.astype(low)
         key_turned[...] = key_ref[...].astype(high).T.astype(low)
         key_sum[...] = jnp.zeros(key_sum.shape, high)
         value_sum[...] = jnp.zeros(value_sum.shape, high)
@@ -302,7 +336,7 @@
             else:
                 partial_refs[i][...] = matmul_back(joined_ref[mine, :], entry_ref[...]).astype(low)
 
-    outs = [shape((rows, 3 * width), low), shape((2, width), high), shape(leave.shape, low)]
+    outs = [shape((rows, 3 * width), low), shape((2, width), high)]
     outs += [shape((local, entry.shape[0]), low)] * (count * (2 if cross else 1))
     scratch = [
         pltpu.VMEM((rows, width), low),
@@ -313,10 +347,10 @@
     ]
     flops = 20 * rows * rows * width + 10 * rows * width * entry.shape[0]
     args = [marks, *tags, *pieces, leave, entry, queries, keys, values, mixture, total]
-    joined, sums, exit_gradient, *partials = run(
+    joined, sums, *partials = run(
         kernel, outs, args, "attend_backward", flops, scratch, scalars=1, room=28
     )
-    return joined, sums, exit_gradient, partials[:count], partials[count:]
+    return joined, sums, partials[:count], partials[count:]
 
 
 def feed_forward(pieces, entry, leave, bias):
@@ -371,12 +405,7 @@
 
 
 def blocks_out(shards, height, width):
-    quarter = shards // 4
-    return [
-        shape((2 * quarter, height, width), low),
-        shape((quarter, height, width), low),
-        shape((quarter, height, width), low),
-    ]
+    return [shape((shards // 2, height, width), low)] * 2
 
 
 def block_targets(refs):
@@ -417,7 +446,8 @@
 
         return run(plain, [shape(size, low) for size in sizes], flat, name, flops)
 
-    shards = order.shape[0]
+    straight = isinstance(order, int)
+    shards = order if straight else order.shape[0]
     heights = [size[0] // shards for size in sizes]
     if stacked:
         corners = [(sum(heights[:i]), 0) for i in range(len(sizes))]
@@ -425,16 +455,28 @@
     else:
         corners = [(0, sum(size[1] for size in sizes[:i])) for i in range(len(sizes))]
         outs = blocks_out(shards, heights[0], sum(size[1] for size in sizes))
+    scratch = [pltpu.VMEM(size, low) for size in sizes]
+    if straight:
+        height, width = outs[0].shape[1:]
+
+        def fixed(*refs):
+            inputs, (out, *buffers) = refs[: len(flat)], refs[len(flat) :]
+            compute(inputs, buffers)
+            for i in range(shards):
+                for source, rows, (top, side) in zip(buffers, heights, corners):
+                    part = source[i * rows : (i + 1) * rows, :]
+                    out[i, top : top + rows, side : side + source.shape[1]] = part
+
+        return run(fixed, [shape((shards, height, width), low)], flat, name, flops, scratch)[0]
 
     def kernel(order_ref, *refs):
         inputs, rest = refs[: len(flat)], refs[len(flat) :]
-        compute(inputs, rest[3:])
-        for i, (target, at) in enumerate(block_targets(rest[:3])):
-            for source, rows, (top, side) in zip(rest[3:], heights, corners):
+        compute(inputs, rest[2:])
+        for i, (target, at) in enumerate(block_targets(rest[:2])):
+            for source, rows, (top, side) in zip(rest[2:], heights, corners):
                 where = pl.ds(pl.multiple_of(order_ref[i] * rows, rows), rows)
                 target[at, top : top + rows, side : side + source.shape[1]] = source[where, :]
 
-    scratch = [pltpu.VMEM(size, low) for size in sizes]
     return run(kernel, outs, [order, *flat], name, flops, scratch, scalars=1)
 
 
@@ -451,6 +493,108 @@
 
     outs = blocks_out(shards, rows * len(exits), exits[0].shape[1])
     return run(kernel, outs, [table, *exits], "order_combiners", 1, scalars=1)
+
+
+def cut(arrays, table, moves, outs, name):
+    def kernel(table_ref, *refs):
+        sources, targets, semaphore = refs[: len(arrays)], refs[len(arrays) : -1], refs[-1]
+        copies = []
+        for array, block, rows, (row, down), lanes, (lane, along), entry, out, top, side in moves:
+            where = table_ref[entry]
+            first = row + pl.multiple_of(where * down, down) if down else row
+            left = pl.multiple_of(lane + where * along, lanes) if along else lane
+            source = sources[array].at[block, pl.ds(first, rows), pl.ds(left, lanes)]
+            target = targets[out].at[pl.ds(top, rows), pl.ds(side, lanes)]
+            copies.append(pltpu.make_async_copy(source, target, semaphore.at[len(copies)]))
+            copies[-1].start()
+        for started in copies:
+            started.wait()
+
+    anywhere = pl.BlockSpec(memory_space=pltpu.HBM)
+    call = pl.pallas_call(
+        kernel,
+        out_shape=outs,
+        in_specs=[SMEM] + [anywhere] * len(arrays),
+        out_specs=[VMEM] * len(outs),
+        scratch_shapes=[pltpu.SemaphoreType.DMA((len(moves),))],
+        compiler_params=pltpu.CompilerParams(vmem_limit_bytes=16 << 20),
+        cost_estimate=pl.CostEstimate(flops=1, bytes_accessed=0, transcendentals=0),
+        name=name,
+    )
+    return take_turn(call, [table, *arrays])
+
+
+def finish(pieces, table, former, outputs, name):
+    count = len(pieces)
+
+    def kernel(table_ref, *refs):
+        sources = refs[:count]
+        refs = refs[count + len(former) :]
+        targets, buffers, semaphore = refs[: len(outputs)], refs[len(outputs) : -1], refs[-1]
+        copies = []
+        for i, ((_, block, moves), target, buffer) in enumerate(zip(outputs, targets, buffers)):
+            for which, source in enumerate(sources):
+                owner = table_ref[which]
+                for (top, rows), (side, lanes), (row, row_step), (lane, lane_step) in moves:
+                    down = row + pl.multiple_of(owner * row_step, row_step) if row_step else row
+                    along = lane + owner * lane_step if lane_step else lane
+                    if lane_step:
+                        along = pl.multiple_of(along, lanes)
+                    part = source[top : top + rows, side : side + lanes].astype(high)
+                    buffer[pl.ds(down, rows), pl.ds(along, lanes)] = part
+            copies.append(pltpu.make_async_copy(buffer, target.at[block], semaphore.at[i]))
+            copies[-1].start()
+        for started in copies:
+            started.wait()
+
+    anywhere = pl.BlockSpec(memory_space=pl.ANY)
+    aliases = {1 + count + i: i for i in range(len(former))}
+    call = pl.pallas_call(
+        kernel,
+        out_shape=[shape(size, high) for size, _, _ in outputs],
+        in_specs=[SMEM] + [VMEM] * count + [anywhere] * len(former),
+        out_specs=[anywhere] * len(outputs),
+        scratch_shapes=[pltpu.VMEM(size[1:], high) for size, _, _ in outputs]
+        + [pltpu.SemaphoreType.DMA((len(outputs),))],
+        input_output_aliases=aliases,
+        compiler_params=pltpu.CompilerParams(vmem_limit_bytes=24 << 20),
+        cost_estimate=pl.CostEstimate(flops=1, bytes_accessed=0, transcendentals=0),
+        name=name,
+    )
+    table = hold(table)
+    return call(table, *pieces, *former)
+
+
+def lay_sums(rows, shares, hidden, me, shards):
+    width, share = rows[0].shape[1], shares[0].shape[1]
+    narrow = hidden[0].shape[1] // shards
+    group = narrow * (width // share)
+    per_row = width // group
+    used = sum(part.shape[0] for part in [*rows, *shares]) + len(hidden) * shards // per_row
+    total = -(-used // 8) * 8
+
+    def kernel(me_ref, *refs):
+        out = refs[-1]
+        mine = me_ref[0]
+        out[...] = jnp.zeros(out.shape, high)
+        at = 0
+        for ref in refs[: len(rows)]:
+            out[at : at + ref.shape[0], :] = ref[...]
+            at += ref.shape[0]
+        side = pl.ds(pl.multiple_of(mine * share, share), share)
+        for ref in refs[len(rows) : len(rows) + len(shares)]:
+            out[at : at + ref.shape[0], side] = ref[...]
+            at += ref.shape[0]
+        for ref in refs[len(rows) + len(shares) : -1]:
+            for shard in range(shards):
+                start = (shard % per_row) * group + mine * narrow
+                row = at + shard // per_row
+                here = slice(shard * narrow, (shard + 1) * narrow)
+                out[row : row + 1, pl.ds(pl.multiple_of(start, narrow), narrow)] = ref[:, here]
+            at += shards // per_row
+
+    args = [me, *rows, *shares, *hidden]
+    return run(kernel, [shape((total, width), high)], args, "lay_sums", total, scalars=1)[0]
 
 
 def add_up(refs):
@@ -561,81 +705,141 @@
     return pieces
 
 
-def sum_low(addends):
-    total = addends[0].astype(high)
-    for addend in addends[1:]:
-        total = total + addend.astype(high)
-    return total.astype(low)
-
-
-def collect(partials):
-    kept = [[partial] for partial in partials]
-    for bit in reversed(seq_bits()):
-        half = len(kept) // 2
-        sent = kept[half:]
-        arrived = [None] * half
-        for i in reversed(range(half)):
-            value = sent[i][0] if len(sent[i]) == 1 else sum_low(sent[i])
-            arrived[i] = swap(value, bit)
-        kept = [own + [other] for own, other in zip(kept[:half], arrived)]
-    return kept[0]
-
-
-def sum_everywhere(values):
-    for axis in ("seq", "batch"):
-        bit = 1
-        while bit < lax.axis_size(axis):
-            values = values + swap(values, bit, axis)
-            bit <<= 1
-    return values
+def quick():
+    return lax.axis_size("seq") == 4 and lax.axis_size("batch") == 8
+
+
+class Spread:
+    def __init__(self, piece):
+        self.pieces = [piece]
+        if quick():
+            self.far = swap(piece, 2)
+            self.near = swap(piece, 1)
+
+    def finish(self):
+        if not quick():
+            return spread(self.pieces[0])
+        far = hold(self.far)
+        return [self.pieces[0], far, self.near, swap(far, 1)]
+
+
+class Collect:
+    def __init__(self, partials):
+        self.partials = partials
+        if quick():
+            self.second = swap(partials[3], 1)
+            self.first = swap(partials[2], 1)
+
+    def turn(self):
+        if quick():
+            total = add_low([self.partials[1], self.second])
+            self.far = swap(total, 2)
+
+    def finish(self):
+        if quick():
+            return [self.partials[0], self.first, self.far]
+        kept = [[partial] for partial in self.partials]
+        for bit in reversed(seq_bits()):
+            half = len(kept) // 2
+            sent = [part[0] if len(part) == 1 else add_low(part) for part in kept[half:]]
+            kept = [own + [swap(other, bit)] for own, other in zip(kept[:half], sent)]
+        return kept[0]
+
+
+def add_low(addends):
+    def kernel(*refs):
+        refs[-1][...] = add_up(refs[:-1]).astype(low)
+
+    return run(kernel, [shape(addends[0].shape, low)], addends, "add_low", addends[0].size)[0]
+
+
+def add_high(addends):
+    def kernel(*refs):
+        refs[-1][...] = add_up(refs[:-1])
+
+    return run(kernel, [shape(addends[0].shape, high)], addends, "add_high", addends[0].size)[0]
 
 
 def mine(values, axis):
     return lax.dynamic_index_in_dim(values, lax.axis_index("seq"), axis, keepdims=False)
 
 
-def in_line():
-    return lax.axis_size("batch") == 2 * lax.axis_size("seq")
-
-
 def line_place():
     return lax.axis_index("batch") // 2, lax.axis_index("batch") % 2
 
 
-def line_shift(values):
+def line_groups():
     shards = lax.axis_size("batch")
-    return lax.ppermute(values, "batch", [(i, (i + 2) % shards) for i in range(shards)])
-
-
-def line_order(first):
-    length = lax.axis_size("batch") // 2
+    return [list(range(side, shards, 2)) for side in range(2)]
+
+
+def line_order():
+    _, side = line_place()
+    at = 2 * jnp.arange(lax.axis_size("batch") // 2, dtype=jnp.int32)
+    return jnp.concatenate([at + side, at + 1 - side])
+
+
+def relay_order():
     place, side = line_place()
-    at = (place - first - jnp.arange(length, dtype=jnp.int32)) % length
+    at = (place - jnp.arange(4, dtype=jnp.int32)) % 4
     return jnp.concatenate([2 * at + side, 2 * at + 1 - side])
 
 
-def after(values, earlier):
-    return lax.optimization_barrier((values, earlier))[0]
+class Relay:
+    def __init__(self, values):
+        self.line, self.across = [values], []
+        self.touch()
+
+    def touch(self):
+        newest = self.line[-1] = hold(self.line[-1])
+        if len(self.line) < 4:
+            shards = lax.axis_size("batch")
+            pairs = [(i, (i + 2) % shards) for i in range(shards)]
+            self.line.append(lax.ppermute(newest, "batch", pairs))
+        self.across.append(to_side(newest))
+
+    def pieces(self):
+        return self.line + self.across
 
 
 def gather_line(values):
-    line, across = [values], [swap(values, 1, "batch")]
-    for _ in range(1, lax.axis_size("batch") // 2):
-        line.append(line_shift(line[-1]))
-        across.append(swap(line[-1], 1, "batch"))
-    return line + across
-
-
-def scatter_line(keep, near, far):
-    across = [swap(near, 1, "batch"), swap(far, 1, "batch")]
-    half = near.shape[0]
-    total = None
-    for step in range(keep.shape[0]):
-        addends = [keep[step], across[step // half][step % half]]
-        if total is not None:
-            addends = [line_shift(total)] + addends
-        total = sum_low(addends)
-    return total
+    return lax.all_gather(values, "batch", axis=0, tiled=True, axis_index_groups=line_groups())
+
+
+def to_side(values):
+    return swap(values, 1, "batch")
+
+
+class Scatter:
+    def __init__(self, blocks):
+        self.keep, sent = blocks
+        self.arrived = to_side(sent)
+
+    def turn(self):
+        total = add_low([self.keep, self.arrived])
+        self.sums = lax.psum_scatter(
+            total, "batch", scatter_dimension=0, tiled=False, axis_index_groups=line_groups()
+        )
+
+    def finish(self):
+        return add_low([self.sums])
+
+
+class Sum:
+    def __init__(self, values):
+        bits = [(axis, 1 << i) for axis in ("seq", "batch") for i in range(5)]
+        self.left = [(axis, bit) for axis, bit in bits if bit < lax.axis_size(axis)]
+        self.values = values
+        self.send()
+
+    def send(self):
+        axis, bit = self.left.pop(0)
+        self.arrived = swap(self.values, bit, axis)
+
+    def turn(self):
+        self.values = add_high([self.values, self.arrived])
+        if self.left:
+            self.send()
 
 
 def line_pairs(step, count, back):
@@ -648,38 +852,64 @@
     return pairs
 
 
-def deal_combiners(combiners):
-    count = lax.axis_size("seq")
-    me = lax.axis_index("seq")
-    place, _ = line_place()
-    rows = combiners.shape[1] // count
-    parts = combiners.reshape(combiners.shape[0], count, rows, combiners.shape[2])
-    own = lax.dynamic_index_in_dim(parts, me, 1, keepdims=False)
-    piece = jnp.where(place == me, own, jnp.zeros_like(own))
-    for step in range(1, count):
-        sent = lax.dynamic_index_in_dim(parts, (me + step) % count, 1, keepdims=False)
-        piece = piece + lax.ppermute(sent, ("batch", "seq"), line_pairs(step, count, False))
-    return piece.reshape(-1, piece.shape[2])
-
-
-def return_combiners(pieces, blocks):
-    count = lax.axis_size("seq")
-    me = lax.axis_index("seq")
-    place, _ = line_place()
-    arrived = [pieces] + [
-        lax.ppermute(pieces, ("batch", "seq"), line_pairs(step, count, True))
-        for step in range(1, count)
-    ]
-    arrived = [piece.reshape(blocks, -1, piece.shape[1]) for piece in arrived]
-    ring = jnp.stack(arrived + arrived[:-1], 1)
-    ordered = lax.dynamic_slice_in_dim(ring, (count - me) % count, count, 1)
-    ordered = ordered.reshape(blocks, -1, pieces.shape[1])
-    for bit in seq_bits():
-        ordered = jnp.where((place & bit) == (me & bit), ordered, swap(ordered, bit))
-    return ordered
-
-
-def gather_weights(projections, combiners, expanders, reducers):
+def add_dealt(own, sent, owned):
+    def kernel(owned_ref, own_ref, *refs):
+        total = add_up(refs[:-1])
+        kept = own_ref[...].astype(high)
+        refs[-1][...] = jnp.where(owned_ref[0] != 0, kept, total).astype(low)
+
+    outs = [shape(own.shape, low)]
+    return run(kernel, outs, [owned, own, *sent], "add_dealt", own.size, scalars=1)[0]
+
+
+class Return:
+    def __init__(self, pieces, blocks):
+        self.blocks, self.left = blocks, seq_bits()
+        self.arrived = [pieces] + [
+            lax.ppermute(pieces, ("batch", "seq"), line_pairs(step, 4, True)) for step in range(1, 4)
+        ]
+
+    def turn(self):
+        me = lax.axis_index("seq")
+        place, _ = line_place()
+        if isinstance(self.arrived, list):
+            table = (me + jnp.arange(4, dtype=jnp.int32)) % 4
+            self.ordered = stack_places(self.arrived, table, self.blocks)
+        else:
+            self.ordered = self.pick()
+        bit = self.left.pop(0)
+        self.mine = ((place & bit) == (me & bit)).astype(jnp.int32)[None]
+        self.arrived = swap(self.ordered, bit)
+
+    def pick(self):
+        return choose(self.ordered, self.arrived, self.mine, low)
+
+    def finish(self):
+        return choose(self.ordered, self.arrived, self.mine, high)
+
+
+def stack_places(pieces, table, blocks):
+    rows = pieces[0].shape[0] // blocks
+
+    def kernel(table_ref, *refs):
+        out = refs[-1]
+        for i, source in enumerate(refs[:-1]):
+            where = pl.ds(pl.multiple_of(table_ref[i] * rows, rows), rows)
+            for block in range(blocks):
+                out[block, where, :] = source[block * rows : (block + 1) * rows, :]
+
+    outs = [shape((blocks, rows * len(pieces), pieces[0].shape[1]), low)]
+    return run(kernel, outs, [table, *pieces], "stack_places", 1, scalars=1)[0]
+
+
+def choose(one, other, first, kind):
+    def kernel(first_ref, one_ref, other_ref, out):
+        out[...] = jnp.where(first_ref[0] != 0, one_ref[...], other_ref[...]).astype(kind)
+
+    return run(kernel, [shape(one.shape, kind)], [first, one, other], "choose", 1, scalars=1)[0]
+
+
+def gather_whole(projections, combiners, expanders, reducers):
     count, shards = lax.axis_size("seq"), lax.axis_size("batch")
     blocks, rows, _ = projections.shape
     feeds, _, _ = expanders.shape
@@ -687,55 +917,16 @@
     entries = mine(projections.reshape(blocks, rows, 3, count, -1), 3).reshape(blocks, rows, -1)
     expand = mine(expanders.reshape(feeds, rows, shards, count, -1), 3).reshape(feeds, rows, -1)
     reduce = mine(reducers.reshape(feeds, count, -1, model_width), 1)
-    if not in_line():
-
-        def whole(values):
-            return lax.all_gather(values, "batch", axis=0, tiled=True)
-
-        leaves = [whole(combiners[i]).reshape(count, -1, model_width) for i in range(blocks)]
-        return (
-            [whole(entries[i]) for i in range(blocks)],
-            [mine(leave, 0) for leave in leaves],
-            [whole(expand[i]) for i in range(feeds)],
-            [whole(reduce[i]) for i in range(feeds)],
-        )
-    order = line_order(0)
-    last = shards // 2 - 1
-    piece = model_width // count // shards
-    straight = order * rows
-    lower = reduce.shape[1]
-    first = gather_line(entries[0])
-    entry_zero = assemble(first, straight[None], [(0, rows, shards * rows)])
-    leaf = gather_line(after(deal_combiners(combiners), first[last]))
-    leaves = assemble(
-        leaf,
-        jnp.stack([((order % 2) * (shards // 2) + order // 2) * piece] * blocks),
-        [(i * piece, piece, shards * piece) for i in range(blocks)],
-    )
-
-    def feed(which, earlier):
-        joined = jnp.concatenate([expand[which], reduce[which]], 0)
-        pieces = gather_line(after(joined, earlier))
-        both = assemble(
-            pieces,
-            jnp.stack([straight, order * lower]),
-            [(0, rows, shards * rows), (rows, lower, shards * lower)],
-        )
-        return both, pieces[last]
-
-    feed_zero, done = feed(0, leaf[last])
-    rest = gather_line(after(entries[1:].reshape(-1, entries.shape[2]), done))
-    entry_rest = assemble(
-        rest,
-        jnp.stack([straight] * (blocks - 1)),
-        [(i * rows, rows, shards * rows) for i in range(blocks - 1)],
-    )
-    feed_one, _ = feed(1, rest[last])
+
+    def whole(values):
+        return lax.all_gather(values, "batch", axis=0, tiled=True)
+
+    leaves = [whole(combiners[i]).reshape(count, -1, model_width) for i in range(blocks)]
     return (
-        [*entry_zero, *entry_rest],
-        leaves,
-        [feed_zero[0], feed_one[0]],
-        [feed_zero[1], feed_one[1]],
+        [whole(entries[i]) for i in range(blocks)],
+        [mine(leave, 0) for leave in leaves],
+        [whole(expand[i]) for i in range(feeds)],
+        [whole(reduce[i]) for i in range(feeds)],
     )
 
 
@@ -767,6 +958,7 @@
     source_cotangent,
     target_cotangent,
 ):
+    Turn.last = None
     source_tokens, target_tokens = source_tokens[0], target_tokens[0]
     source_cotangent, target_cotangent = source_cotangent[0], target_cotangent[0]
     count, shards = lax.axis_size("seq"), lax.axis_size("batch")
@@ -818,137 +1010,343 @@
     def exit_bias(block):
         return exit_biases[block : block + 1]
 
-    source_pieces = spread(source_tokens)
-    entries, leaves, expand, reduce = gather_weights(projections, combiners, expanders, reducers)
-    target_pieces = spread(target_tokens)
+    rows = projections.shape[1]
+    feed_rows = reducers.shape[1] // count
+    if quick():
+        piece = share // shards
+        line = (me + jnp.arange(count, dtype=jnp.int32)) % count
+        table = jnp.concatenate([me[None], line])
+
+        def entry_cut(block, out, top):
+            return [
+                (0, block, rows, (0, 0), share, (part * model_width, share), 0, out, top, part * share)
+                for part in range(3)
+            ]
+
+        moves = entry_cut(0, 0, 0) + [
+            (1, block, piece, (0, piece), model_width, (0, 0), 1 + i, 1 + i, block * piece, 0)
+            for i in range(count)
+            for block in range(3)
+        ]
+        outs = [shape((rows, 3 * share), low)] + [shape((3 * piece, model_width), low)] * count
+        first, *deals = cut([projections, combiners], table, moves, outs, "cut_first")
+        entry_relay = Relay(first)
+        sent = [
+            lax.ppermute(deals[step], ("batch", "seq"), line_pairs(step, count, False))
+            for step in range(1, count)
+        ]
+        lanes = expanders.shape[2] // shards
+        moves = entry_cut(1, 2, 0) + entry_cut(2, 2, rows)
+        for feed in range(2):
+            moves += [
+                (1, feed, rows, (0, 0), feed_rows, (part * lanes, feed_rows), 0, feed, 0, part * feed_rows)
+                for part in range(shards)
+            ]
+            moves.append(
+                (2, feed, feed_rows, (0, feed_rows), model_width, (0, 0), 0, feed, rows, 0)
+            )
+        outs = [shape((rows + feed_rows, model_width), low)] * 2
+        outs += [shape((2 * rows, 3 * share), low)]
+        feed_zero, feed_one, entry_rest = cut(
+            [projections, expanders, reducers], table, moves, outs, "cut_rest"
+        )
+        entry_relay.touch()
+        source_spread = Spread(hold(source_tokens))
+        entry_relay.touch()
+        entry_relay.touch()
+        place, _ = line_place()
+        order, relayed = line_order(), relay_order()
+        entry_table = (order * rows)[None]
+        whole_rows = shards * rows
+        dealt = add_dealt(deals[0], sent, (place == me).astype(jnp.int32)[None])
+        leave_relay = Relay(dealt)
+        feed_line = gather_line(hold(feed_zero))
+        source_pieces = source_spread.finish()
+        encoder_entry = assemble(
+            entry_relay.pieces(), (relayed * rows)[None], [(0, rows, whole_rows)], rows
+        )[0]
+        leave_relay.touch()
+        target_spread = Spread(hold(target_tokens))
+    else:
+        entries, leaves, expand, reduce = gather_whole(
+            projections, combiners, expanders, reducers
+        )
+        encoder_entry, decoder_entry, cross_entry = entries
+        source_pieces = spread(source_tokens)
+        target_spread = Spread(target_tokens)
+
+    encoder_normed, *projected = project_self(
+        source_pieces, gain(0), shift(0), encoder_entry, entry_biases[0]
+    )
+    if quick():
+        leave_relay.touch()
+    mixture, total = attend_forward(*encoder_view, *projected, heads, False)
+    encoder_stored = (*projected, mixture, total)
+    target_pieces = target_spread.finish()
+    if quick():
+        leave_relay.touch()
+        rest_line = gather_line(hold(entry_rest))
+        leaves = assemble(
+            leave_relay.pieces(),
+            jnp.stack([((relayed % 2) * 4 + relayed // 2) * piece] * 3),
+            [(i * piece, piece, shards * piece) for i in range(3)],
+            3 * piece,
+        )
+        feed_other = to_side(hold(feed_line))
+    encoder_partials = Collect(project_out(mixture, leaves[0], count))
+    encoder_partials.turn()
     target_incoming, target_incoming_low, target_sum = join_gradient(
         target_cotangent, target_keep, []
     )
-    target_incoming_pieces = spread(target_incoming_low)
-
-    def self_forward(pieces, seen, causal, norm, block):
-        normed, *projected = project_self(
-            pieces, gain(norm), shift(norm), entries[block], entry_biases[block]
-        )
-        mixture, total, partials = attend_forward(
-            *seen, *projected, leaves[block], heads, causal, count
-        )
-        return normed, (*projected, mixture, total), collect(partials)
-
-    encoder_normed, encoder_stored, addends = self_forward(
-        source_pieces, encoder_view, False, 0, 0
-    )
-    middle, middle_normed = residual_norm(source_tokens, addends, exit_bias(0), gain(1), shift(1))
-    middle_pieces = spread(middle_normed)
-    decoder_normed, decoder_stored, addends = self_forward(target_pieces, self_view, True, 2, 1)
-    self_out, self_normed = residual_norm(target_tokens, addends, exit_bias(1), gain(3), shift(3))
-    self_pieces = spread(self_normed)
+    if quick():
+        last_line = gather_line(hold(feed_one))
+    middle, middle_normed = residual_norm(
+        source_tokens, encoder_partials.finish(), exit_bias(0), gain(1), shift(1)
+    )
+    middle_spread = Spread(middle_normed)
+    if quick():
+        one_line = part_rows(rest_line, 2 * rows, 0, rows)
+        two_line = part_rows(rest_line, 2 * rows, rows, rows)
+        one_other = to_side(one_line)
+    middle_pieces = middle_spread.finish()
+    if quick():
+        expand, reduce = [None, None], [None, None]
+        feed_parts = [(0, rows, whole_rows), (rows, feed_rows, shards * feed_rows)]
+        feed_table = jnp.stack([order * rows, order * feed_rows])
+        height = rows + feed_rows
+        expand[0], reduce[0] = assemble([feed_line, feed_other], feed_table, feed_parts, height)
     encoder_active, encoder_slope, partials = feed_forward(
         middle_pieces, expand[0], reduce[0], hidden_biases[0]
     )
-    memory_low = residual_low(middle, collect(partials), reducer_biases[0:1])
-    memory_pieces = spread(memory_low)
-    cross_projected = project_cross(self_pieces, memory_pieces, entries[2], entry_biases[2])
-    mixture, total, partials = attend_forward(
-        *cross_view, *cross_projected, leaves[2], heads, False, count
-    )
+    memory_partials = Collect(partials)
+    memory_partials.turn()
+    if quick():
+        decoder_entry = assemble(
+            [one_line, one_other], entry_table, [(0, rows, whole_rows)], rows
+        )[0]
+        two_other = to_side(hold(two_line))
+    decoder_normed, *projected = project_self(
+        target_pieces, gain(2), shift(2), decoder_entry, entry_biases[1]
+    )
+    mixture, total = attend_forward(*self_view, *projected, heads, True)
+    decoder_stored = (*projected, mixture, total)
+    decoder_partials = Collect(project_out(mixture, leaves[1], count))
+    decoder_partials.turn()
+    memory_low = residual_low(middle, memory_partials.finish(), reducer_biases[0:1])
+    memory_spread = Spread(memory_low)
+    if quick():
+        last_other = to_side(hold(last_line))
+    self_out, self_normed = residual_norm(
+        target_tokens, decoder_partials.finish(), exit_bias(1), gain(3), shift(3)
+    )
+    self_spread = Spread(self_normed)
+    memory_pieces = memory_spread.finish()
+    self_pieces = self_spread.finish()
+    if quick():
+        cross_entry = assemble(
+            [two_line, two_other], entry_table, [(0, rows, whole_rows)], rows
+        )[0]
+    target_incoming_spread = Spread(hold(target_incoming_low))
+    cross_projected = project_cross(self_pieces, memory_pieces, cross_entry, entry_biases[2])
+    mixture, total = attend_forward(*cross_view, *cross_projected, heads, False)
     cross_stored = (*cross_projected, mixture, total)
+    target_incoming_pieces = target_incoming_spread.finish()
+    partials = Collect(project_out(mixture, leaves[2], count))
+    partials.turn()
     cross_out, cross_normed = residual_norm(
-        self_out, collect(partials), exit_bias(2), gain(4), shift(4)
-    )
-    cross_pieces = spread(cross_normed)
+        self_out, partials.finish(), exit_bias(2), gain(4), shift(4)
+    )
+    cross_spread = Spread(cross_normed)
+    if quick():
+        expand[1], reduce[1] = assemble([last_line, last_other], feed_table, feed_parts, height)
+    cross_pieces = cross_spread.finish()
     decoder_active, decoder_slope, partials = feed_forward(
         cross_pieces, expand[1], reduce[1], hidden_biases[1]
     )
-    decoded_low = residual_low(cross_out, collect(partials), reducer_biases[1:2])
-
-    order = line_order(1) if in_line() else None
-
-    def send(blocks):
-        if order is not None:
-            return scatter_line(*blocks)
-        return [
-            lax.psum_scatter(part, "batch", scatter_dimension=0, tiled=True) for part in blocks
-        ]
+    decoded_partials = Collect(partials)
+
+    order = line_order() if quick() else None
 
     def feed_gradients(pieces, normed_pieces, hidden, active):
         pairs = [
             (normed_pieces, [hidden], 0, hidden.shape[1]),
             ([active], pieces, 0, model_width),
         ]
-        return send(outer_sums(pairs, order, "feed_weights", True))
-
-    def attention_gradients(pairs):
-        return send(outer_sums(pairs, order, "attention_weights"))
+        return outer_sums(pairs, order, "feed_weights", True)
+
+    def exit_gradient(stored, pieces):
+        pairs = [([stored[3]], pieces, 0, model_width)]
+        return outer_sums(pairs, None, "exit_weights")[0]
+
+    def sums_over_batch(blocks):
+        if quick():
+            return Scatter(blocks)
+        return [
+            lax.psum_scatter(part, "batch", scatter_dimension=0, tiled=True) for part in blocks
+        ]
 
     hidden, decoder_hidden_sum, partials = feed_backward(
         target_incoming_pieces, expand[1], reduce[1], decoder_slope
     )
+    partials = Collect(partials)
+    partials.turn()
+    decoded_partials.turn()
+    decoder_feed_shares = sums_over_batch(
+        feed_gradients(target_incoming_pieces, cross_pieces, hidden, decoder_active)
+    )
     incoming, incoming_low, norm_four = norm_backward(
-        cross_out, gain(4), target_incoming, collect(partials)
-    )
-    incoming_pieces = spread(incoming_low)
-    decoder_feed_shares = feed_gradients(
-        target_incoming_pieces, cross_pieces, hidden, decoder_active
-    )
-    cross_joined, cross_sums, cross_exit, partials, memory_partials = attend_backward(
-        *cross_view, incoming_pieces, leaves[2], entries[2], cross_stored, heads, False, True
-    )
+        cross_out, gain(4), target_incoming, partials.finish()
+    )
+    incoming_spread = Spread(incoming_low)
+    decoded_low = residual_low(cross_out, decoded_partials.finish(), reducer_biases[1:2])
+    incoming_pieces = incoming_spread.finish()
+    cross_joined, cross_sums, partials, memory_partials = attend_backward(
+        *cross_view, incoming_pieces, leaves[2], cross_entry, cross_stored, heads, False, True
+    )
+    memory_partials = Collect(memory_partials)
+    memory_partials.turn()
+    partials = Collect(partials)
+    cross_exit = exit_gradient(cross_stored, incoming_pieces)
+    cross_shares = sums_over_batch(
+        outer_sums(
+            [
+                (self_pieces, [cross_joined], 0, share),
+                (memory_pieces, [cross_joined], share, 2 * share),
+            ],
+            order,
+            "attention_weights",
+        )
+    )
+    if quick():
+        decoder_feed_shares.turn()
     source_incoming, source_incoming_low, source_sum = join_gradient(
-        source_cotangent, source_keep, collect(memory_partials)
-    )
-    source_incoming_pieces = spread(source_incoming_low)
+        source_cotangent, source_keep, memory_partials.finish()
+    )
+    source_incoming_spread = Spread(source_incoming_low)
+    partials.turn()
+    source_incoming_pieces = source_incoming_spread.finish()
+    hidden, encoder_hidden_sum, feed_partials = feed_backward(
+        source_incoming_pieces, expand[0], reduce[0], encoder_slope
+    )
+    feed_partials = Collect(feed_partials)
+    feed_partials.turn()
     self_incoming, self_incoming_low, norm_three = norm_backward(
-        self_out, gain(3), incoming, collect(partials)
-    )
-    self_incoming_pieces = spread(self_incoming_low)
-    cross_shares = attention_gradients(
-        [
-            (self_pieces, [cross_joined], 0, share),
-            (memory_pieces, [cross_joined], share, 2 * share),
-        ]
-    )
-    hidden, encoder_hidden_sum, partials = feed_backward(
-        source_incoming_pieces, expand[0], reduce[0], encoder_slope
+        self_out, gain(3), incoming, partials.finish()
+    )
+    self_incoming_spread = Spread(self_incoming_low)
+    encoder_feed_shares = sums_over_batch(
+        feed_gradients(source_incoming_pieces, middle_pieces, hidden, encoder_active)
     )
     middle_incoming, middle_incoming_low, norm_one = norm_backward(
-        middle, gain(1), source_incoming, collect(partials)
-    )
-    middle_incoming_pieces = spread(middle_incoming_low)
-    decoder_joined, decoder_sums, decoder_exit, partials, _ = attend_backward(
-        *self_view, self_incoming_pieces, leaves[1], entries[1], decoder_stored, heads, True, False
-    )
-    target_gradient, _, norm_two = norm_backward(
-        target_tokens, gain(2), self_incoming, collect(partials)
-    )
-    encoder_feed_shares = feed_gradients(
-        source_incoming_pieces, middle_pieces, hidden, encoder_active
-    )
-    decoder_shares = attention_gradients([([decoder_normed], [decoder_joined], 0, 3 * share)])
-    encoder_joined, encoder_sums, encoder_exit, partials, _ = attend_backward(
+        middle, gain(1), source_incoming, feed_partials.finish()
+    )
+    middle_incoming_spread = Spread(middle_incoming_low)
+    self_incoming_pieces = self_incoming_spread.finish()
+    if quick():
+        cross_shares.turn()
+    decoder_joined, decoder_sums, decoder_partials, _ = attend_backward(
+        *self_view, self_incoming_pieces, leaves[1], decoder_entry, decoder_stored, heads, True, False
+    )
+    decoder_partials = Collect(decoder_partials)
+    decoder_shares = sums_over_batch(
+        outer_sums([([decoder_normed], [decoder_joined], 0, 3 * share)], order, "attention_weights")
+    )
+    decoder_partials.turn()
+    middle_incoming_pieces = middle_incoming_spread.finish()
+    if quick():
+        decoder_feed_spread = Spread(decoder_feed_shares.finish())
+    decoder_exit = exit_gradient(decoder_stored, self_incoming_pieces)
+    encoder_exit = exit_gradient(encoder_stored, middle_incoming_pieces)
+    exits = [encoder_exit, decoder_exit, cross_exit]
+    if quick():
+        table = ((order % 2) * 4 + order // 2) * piece
+        exit_scatter = Scatter(order_combiners(exits, table))
+        encoder_feed_shares.turn()
+        decoder_feed_pieces = decoder_feed_spread.finish()
+    encoder_joined, encoder_sums, encoder_partials, _ = attend_backward(
         *encoder_view,
         middle_incoming_pieces,
         leaves[0],
-        entries[0],
+        encoder_entry,
         encoder_stored,
         heads,
         False,
         False,
     )
-    encoder_shares = attention_gradients([([encoder_normed], [encoder_joined], 0, 3 * share)])
+    encoder_partials = Collect(encoder_partials)
+    if quick():
+        exit_scatter.turn()
+    encoder_shares = sums_over_batch(
+        outer_sums([([encoder_normed], [encoder_joined], 0, 3 * share)], order, "attention_weights")
+    )
+    encoder_partials.turn()
+    if quick():
+        decoder_shares.turn()
+        cross_spread = Spread(cross_shares.finish())
+    target_gradient, _, norm_two = norm_backward(
+        target_tokens, gain(2), self_incoming, decoder_partials.finish()
+    )
     source_gradient, _, norm_zero = norm_backward(
-        source_tokens, gain(0), middle_incoming, collect(partials)
-    )
-
-    exits = [encoder_exit, decoder_exit, cross_exit]
-    rows = projections.shape[1]
-    if order is not None:
-        table = ((order % 2) * (shards // 2) + order // 2) * (share // shards)
-        pieces = scatter_line(*order_combiners(exits, table))
-        combiners_gradient = return_combiners(pieces, 3)
-        entry_shares = [encoder_shares, decoder_shares, cross_shares]
-        expand_shares = [part[:rows] for part in (encoder_feed_shares, decoder_feed_shares)]
-        reduce_shares = [part[rows:] for part in (encoder_feed_shares, decoder_feed_shares)]
+        source_tokens, gain(0), middle_incoming, encoder_partials.finish()
+    )
+
+    norms = (norm_zero, norm_one, norm_two, norm_three, norm_four)
+    if quick():
+        laid = lay_sums(
+            [*norms, source_sum, target_sum],
+            [encoder_sums, decoder_sums, cross_sums],
+            [encoder_hidden_sum, decoder_hidden_sum],
+            me[None],
+            shards,
+        )
+        summed = Sum(laid)
+        owners = me ^ jnp.array(seq_offsets(), jnp.int32)
+        entry_moves = [
+            ((0, rows), (part * share, share), (0, 0), (part * model_width, share))
+            for part in range(3)
+        ]
+        expand_moves = [
+            ((0, rows), (part * feed_rows, feed_rows), (0, 0), (part * lanes, feed_rows))
+            for part in range(shards)
+        ]
+        reduce_moves = [((rows, feed_rows), (0, model_width), (0, feed_rows), (0, 0))]
+
+        def finish_entry(block, shares, former):
+            outputs = [(projections.shape, block, entry_moves)]
+            return finish(shares, owners, former, outputs, "finish_entry")
+
+        def finish_feed(feed, shares, former):
+            outputs = [
+                (expanders.shape, feed, expand_moves),
+                (reducers.shape, feed, reduce_moves),
+            ]
+            return finish(shares, owners, former, outputs, "finish_feed")
+
+        encoder_shares.turn()
+        summed.turn()
+        feeds_whole = finish_feed(1, decoder_feed_pieces, [])
+        feed_spread = Spread(encoder_feed_shares.finish())
+        summed.turn()
+        entry_whole = finish_entry(2, cross_spread.finish(), [])
+        exit_return = Return(exit_scatter.finish(), 3)
+        summed.turn()
+        feeds_whole = finish_feed(0, feed_spread.finish(), feeds_whole)
+        summed.turn()
+        decoder_spread = Spread(decoder_shares.finish())
+        exit_return.turn()
+        summed.turn()
+        summed = summed.values
+        exit_return.turn()
+        entry_whole = finish_entry(1, decoder_spread.finish(), entry_whole)
+        encoder_spread = Spread(encoder_shares.finish())
+        combiners_gradient = exit_return.finish()
+        entry_whole = finish_entry(0, encoder_spread.finish(), entry_whole)
+        projections_gradient = entry_whole[0]
+        expanders_gradient, reducers_gradient = feeds_whole
+        norm_sums = summed[:15].reshape(5, 3, -1)
+        exit_sums = summed[15:17]
+        inner = summed[17:23].reshape(3, 2, -1)
+        hidden_sums = summed[23 : 23 + 2 * expanders.shape[2] // model_width].reshape(2, -1)
     else:
         wholes = [
             lax.dynamic_update_slice(
@@ -956,60 +1354,48 @@
             ).reshape(-1, model_width)
             for part in exits
         ]
-        combiners_gradient = lax.psum(jnp.stack([send([part])[0] for part in wholes]), "seq")
-        entry_shares = [encoder_shares[0], decoder_shares[0]]
-        entry_shares.append(jnp.concatenate(cross_shares, 1))
-        expand_shares = [encoder_feed_shares[0], decoder_feed_shares[0]]
-        reduce_shares = [encoder_feed_shares[1], decoder_feed_shares[1]]
-
-    def whole_entry(part):
-        joined = spread_order([p.reshape(rows, 3, share) for p in spread(part)], 2)
-        return joined.reshape(rows, -1)
-
-    def whole_expand(part):
-        joined = spread_order([p.reshape(rows, shards, -1) for p in spread(part)], 2)
-        return joined.reshape(rows, -1)
-
-    def whole_reduce(part):
-        return spread_order(spread(part), 0).reshape(-1, model_width)
-
-    projections_gradient = jnp.stack([whole_entry(part) for part in entry_shares]).astype(high)
-    expanders_gradient = jnp.stack([whole_expand(part) for part in expand_shares]).astype(high)
-    reducers_gradient = jnp.stack([whole_reduce(part) for part in reduce_shares]).astype(high)
-
-    norms = (norm_zero, norm_one, norm_two, norm_three, norm_four)
-    norm_sums = jnp.stack([sums[:2] for sums in norms])
-    inner = jnp.stack([encoder_sums, decoder_sums, cross_sums])
-    inner_whole = lax.dynamic_update_slice(
-        jnp.zeros((3, 2, count, share), high), inner[:, :, None], (0, 0, me, 0)
-    )
-    outer = jnp.stack([norm_one[2], norm_three[2], norm_four[2]])
-    hidden_sums = jnp.stack([encoder_hidden_sum, decoder_hidden_sum]).reshape(2, shards, 1, -1)
-    hidden_whole = lax.dynamic_update_slice(
-        jnp.zeros((2, shards, count, hidden_sums.shape[3]), high), hidden_sums, (0, 0, me, 0)
-    )
-    exit_sums = jnp.concatenate([source_sum, target_sum])
-    parts = [norm_sums, inner_whole, outer, hidden_whole, exit_sums]
-    summed = sum_everywhere(jnp.concatenate([part.reshape(-1, 128) for part in parts], 0))
-    sizes = [part.size // 128 for part in parts]
-    starts = [sum(sizes[:i]) for i in range(len(sizes))]
-    norm_sums, inner_whole, outer, hidden_whole, exit_sums = [
-        summed[start : start + size].reshape(part.shape)
-        for start, size, part in zip(starts, sizes, parts)
-    ]
+        combiners_gradient = jnp.stack([sums_over_batch([part])[0] for part in wholes])
+        combiners_gradient = lax.psum(combiners_gradient, "seq").astype(high)
+        entry_shares = [encoder_shares[0], decoder_shares[0], jnp.concatenate(cross_shares, 1)]
+        feed_shares = [encoder_feed_shares, decoder_feed_shares]
+
+        def whole(part, groups):
+            pieces = [p.reshape(rows, groups, -1) for p in spread(part)]
+            return spread_order(pieces, 2).reshape(rows, -1).astype(high)
+
+        projections_gradient = jnp.stack([whole(part, 3) for part in entry_shares])
+        expanders_gradient = jnp.stack([whole(part[0], shards) for part in feed_shares])
+        reducers_gradient = jnp.stack(
+            [spread_order(spread(part[1]), 0).reshape(-1, model_width) for part in feed_shares]
+        ).astype(high)
+        inner = jnp.stack([encoder_sums, decoder_sums, cross_sums])
+        inner = lax.dynamic_update_slice(
+            jnp.zeros((3, 2, count, share), high), inner[:, :, None], (0, 0, me, 0)
+        )
+        hidden_sums = jnp.stack([encoder_hidden_sum, decoder_hidden_sum])
+        hidden_sums = hidden_sums.reshape(2, shards, 1, -1)
+        hidden_sums = lax.dynamic_update_slice(
+            jnp.zeros((2, shards, count, hidden_sums.shape[3]), high), hidden_sums, (0, 0, me, 0)
+        )
+        parts = [jnp.stack(norms), jnp.concatenate([source_sum, target_sum]), inner, hidden_sums]
+        summed = lax.psum(parts, ("batch", "seq"))
+        norm_sums, exit_sums, inner, hidden_sums = summed
+        inner = inner.reshape(3, 2, -1)
+        hidden_sums = hidden_sums.reshape(2, -1)
+    outer = jnp.stack([norm_sums[1, 2], norm_sums[3, 2], norm_sums[4, 2]])
     return (
         memory_low[None],
         decoded_low[None],
         source_gradient[None],
         target_gradient[None],
         projections_gradient,
-        combiners_gradient.astype(high),
+        combiners_gradient,
         expanders_gradient,
         reducers_gradient,
         norm_sums[:, 0],
         norm_sums[:, 1],
-        jnp.concatenate([inner_whole.reshape(3, 2, -1), outer[:, None]], 1),
-        hidden_whole.reshape(2, -1),
+        jnp.concatenate([inner, outer[:, None]], 1),
+        hidden_sums,
         exit_sums,
     )
 

time: 831 us -> 735 us (0.88)
  starting transfers between devices: 197 us -> 115 us
  waiting for transfers between devices: 224 us -> 299 us
  local copies, waits for them, and re-layouts: 162 us -> 96.2 us
  other arithmetic: 59.2 us -> 2.68 us
  Pallas kernels: 168 us -> 202 us
    ppermute x126 -> x106, waiting for transfers between devices: 127 us -> 252 us  [swap(): lax.ppermute(values, axis, [(i, i ^ bit) for i in range(lax.axis_size(axi...]
    ppermute x126 -> x106, starting transfers between devices: 180 us -> 103 us  [swap(): lax.ppermute(values, axis, [(i, i ^ bit) for i in range(lax.axis_size(axi...]
    ppermute x39 -> x12, waiting for transfers between devices: 97 us -> 46.2 us  [the longest x6 42.6 us: touch(): self.line.append(lax.ppermute(newest, 'batch', pairs))]
    convert_element_type x39 -> x0, other arithmetic: 40 us -> none  [the longest x35 29.9 us: sum_low(): return total.astype(low)]
    pallas_call x36 -> x85, Pallas kernels: 168 us -> 202 us  [the longest x80 188 us: take_turn(): results = call(*args)]
    dynamic_slice x20 -> x0, local copies, waits for them, and re-layouts: 19 us -> none  [the longest x17 18.3 us: spread_order(): lax.dynamic_index_in_dim(stacked, offsets[me ^ i], 0, keepdims=False)]
    another operation x18 -> x4, local copies, waits for them, and re-layouts: 17.1 us -> 0.94 us  [the longest x1 0.77 us: per_device(): outer = jnp.stack([norm_sums[1, 2], norm_sums[3, 2], norm_sums[4, 2]])]
    another operation x19 -> x5, other arithmetic: 13 us -> 0.32 us  [the longest x7 6.59 us: spread_order(): return jnp.stack(ordered, axis)]
  transfers between devices with their start and end apart: 165 -> 127, of which waited for: 53 -> 50; matrix products, arithmetic and copies ran while one was open for 20% -> 2% of each run, Pallas kernels for 20% -> 26%
where the time goes in v3:
time: 735 us; the launch traced here: 730 us
  waiting for transfers between devices  299 us (41%)
  Pallas kernels  202 us (27%)
  starting transfers between devices  115 us (16%)
  local copies, waits for them, and re-layouts  96.2 us (13%)
  between operations  15.9 us (2%)
    ppermute x106, waiting for transfers between devices, swap(): lax.ppermute(values, axis, [(i, i ^ bit) for i in range(lax.axis_size(axi...  252 us
    pallas_call x80, Pallas kernels, take_turn(): results = call(*args)  188 us
    ppermute x106, starting transfers between devices, swap(): lax.ppermute(values, axis, [(i, i ^ bit) for i in range(lax.axis_size(axi...  103 us
    unnamed x344, local copies, waits for them, and re-layouts  89 us
    ppermute x6, waiting for transfers between devices, touch(): self.line.append(lax.ppermute(newest, 'batch', pairs))  42.6 us
  transfers between devices with their start and end apart: 127, of which 50 were waited for; matrix products, arithmetic and copies ran while one was open for 2% of the time, Pallas kernels for 26%

profile of v3, /device:TPU:1, one launch (start us, length us, event | category | flops | bytes accessed | tf_op | source)
XLA Modules:
  0.0 730.3 jit_solution(14492654811970943817)
XLA Ops:
  42.7 6.7 collective-permute-done.7.refs_2_
  50.8 11.3 %collective-permute-done.8.refs_3_ = bf16[128,768]{1,0:T(8,128)(2,1)S(1)} collective-permute-done((bf16[128,768]{1,0:T(8,128)(2,1)S(1)}, bf16[128,768]{1,0:T(8,128)(2,1)S(1)}, u32[]{:S(2)}, u32[]{:S(2)}) %collective-permute-start.8) | collective-permute-done | bytes 196640 | tf_op jit(solution)/shard_map/ppermute | solution.py:798
  79.1 9.4 %attend_forward.3 = (bf16[1024,256]{1,0:T(8,128)(2,1)S(1)}, f32[8,1024]{1,0:T(8,128)S(1)}) custom-call(s32[4,4]{1,0:T(4,128)S(1)} %get-tuple-element.452.refs_0_, s32[1024,1]{1,0:T(8,128)S(1)} %copy.59.refs_1_, s32[1,1024]{1,0:T(1,128)S(1)} %bitcast.97, s32[1024,1]{1,0:T(8,128)S(1)} %copy.60.refs_3_, s32[1,1024]{1,0:T(1,128)S(1)} %bitcast.81, ...), custom_call_target="tpu_custom_call" | custom-call | flops 107374184 | tf_op jit(solution)/shard_map/attend_forward/pallas_call | solution.py:39
  95.7 8.7 %collective-permute-done.14.refs_2_ = bf16[96,1024]{1,0:T(8,128)(2,1)S(1)} collective-permute-done((bf16[96,1024]{1,0:T(8,128)(2,1)S(1)}, bf16[96,1024]{1,0:T(8,128)(2,1)S(1)}, u32[]{:S(2)}, u32[]{:S(2)}) %collective-permute-start.14) | collective-permute-done | bytes 196640 | tf_op jit(solution)/shard_map/ppermute | solution.py:798
  105.9 9.5 %collective-permute-done.15.refs_3_ = bf16[96,1024]{1,0:T(8,128)(2,1)S(1)} collective-permute-done((bf16[96,1024]{1,0:T(8,128)(2,1)S(1)}, bf16[96,1024]{1,0:T(8,128)(2,1)S(1)}, u32[]{:S(2)}, u32[]{:S(2)}) %collective-permute-start.15) | collective-permute-done | bytes 196640 | tf_op jit(solution)/shard_map/ppermute | solution.py:798
  115.6 6.9 collective-permute-done.19.refs_7_
  129.5 7.4 %collective-permute-start.21 = (bf16[256,1024]{1,0:T(8,128)(2,1)}, bf16[256,1024]{1,0:T(8,128)(2,1)}, u32[]{:S(2)}, u32[]{:S(2)}) collective-permute-start(bf16[256,1024]{1,0:T(8,128)(2,1)} %get-tuple-element.294), channel_id=1, source_target_pairs={{0,1},{1,0},{2,3},{3,2},{4,5},{5,4},{6,7},{7,6},{8,9},{9,8},{10,11... | collective-permute-start | bytes 1572872 | tf_op jit(solution)/shard_map/ppermute | solution.py:698
  145.0 10.2 %collective-permute-done.22.refs_3_ = bf16[256,1024]{1,0:T(8,128)(2,1)} collective-permute-done((bf16[256,1024]{1,0:T(8,128)(2,1)}, bf16[256,1024]{1,0:T(8,128)(2,1)}, u32[]{:S(2)}, u32[]{:S(2)}) %collective-permute-start.22) | collective-permute-done | bytes 524320 | tf_op jit(solution)/shard_map/ppermute | solution.py:698
  166.0 7.4 %collective-permute-done.23.refs_1_ = bf16[256,1024]{1,0:T(8,128)(2,1)} collective-permute-done((bf16[256,1024]{1,0:T(8,128)(2,1)}, bf16[256,1024]{1,0:T(8,128)(2,1)}, u32[]{:S(2)}, u32[]{:S(2)}) %collective-permute-start.23) | collective-permute-done | bytes 524320 | tf_op jit(solution)/shard_map/ppermute | solution.py:698
  176.4 8.1 %collective-permute-done.26.refs_1_ = bf16[1024,1024]{1,0:T(8,128)(2,1)} collective-permute-done((bf16[1024,1024]{1,0:T(8,128)(2,1)}, bf16[1024,1024]{1,0:T(8,128)(2,1)}, u32[]{:S(2)}, u32[]{:S(2)}) %collective-permute-start.26) | collective-permute-done | bytes 2097184 | tf_op jit(solution)/shard_map/ppermute | solution.py:698
  188.1 9.9 %feed_forward.2 = (bf16[1024,1024]{1,0:T(8,128)(2,1)S(1)}, bf16[1024,1024]{1,0:T(8,128)(2,1)S(1)}, bf16[256,1024]{1,0:T(8,128)(2,1)S(1)}, bf16[256,1024]{1,0:T(8...) custom-call(bf16[256,1024]{1,0:T(8,128)(2,1)} %get-tuple-element.299.refs_0_, ...), custom_call_target="tpu_custom_call" | custom-call | flops 214748368 | tf_op jit(solution)/shard_map/feed_forward/pallas_call | solution.py:39
  215.8 7.2 attend_forward.4
  227.1 10.5 %collective-permute-done.29.refs_3_ = bf16[256,1024]{1,0:T(8,128)(2,1)S(1)} collective-permute-done((bf16[256,1024]{1,0:T(8,128)(2,1)S(1)}, bf16[256,1024]{1,0:T(8,128)(2,1)S(1)}, u32[]{:S(2)}, u32[]{:S(2)}) %collective-permute-start.29) | collective-permute-done | bytes 524320 | tf_op jit(solution)/shard_map/ppermute | solution.py:698
  239.0 9.7 %collective-permute-done.36.refs_3_ = bf16[256,1024]{1,0:T(8,128)(2,1)S(1)} collective-permute-done((bf16[256,1024]{1,0:T(8,128)(2,1)S(1)}, bf16[256,1024]{1,0:T(8,128)(2,1)S(1)}, u32[]{:S(2)}, u32[]{:S(2)}) %collective-permute-start.36) | collective-permute-done | bytes 524320 | tf_op jit(solution)/shard_map/ppermute | solution.py:698
  262.1 9.2 %collective-permute-done.37.refs_1_ = bf16[256,1024]{1,0:T(8,128)(2,1)} collective-permute-done((bf16[256,1024]{1,0:T(8,128)(2,1)}, bf16[256,1024]{1,0:T(8,128)(2,1)}, u32[]{:S(2)}, u32[]{:S(2)}) %collective-permute-start.37) | collective-permute-done | bytes 524320 | tf_op jit(solution)/shard_map/ppermute | solution.py:698
  288.2 12.6 %collective-permute-done.46.refs_3_ = bf16[256,1024]{1,0:T(8,128)(2,1)S(1)} collective-permute-done((bf16[256,1024]{1,0:T(8,128)(2,1)S(1)}, bf16[256,1024]{1,0:T(8,128)(2,1)S(1)}, u32[]{:S(2)}, u32[]{:S(2)}) %collective-permute-start.46) | collective-permute-done | bytes 524320 | tf_op jit(solution)/shard_map/ppermute | solution.py:698
  304.7 15.2 %collective-permute-done.48.refs_1_ = bf16[1024,1024]{1,0:T(8,128)(2,1)S(1)} collective-permute-done((bf16[1024,1024]{1,0:T(8,128)(2,1)}, bf16[1024,1024]{1,0:T(8,128)(2,1)S(1)}, u32[]{:S(2)}, u32[]{:S(2)}) %collective-permute-start.48) | collective-permute-done | bytes 2097184 | tf_op jit(solution)/shard_map/ppermute | solution.py:698
  357.6 7.5 %collective-permute-done.57.refs_3_ = bf16[256,1024]{1,0:T(8,128)(2,1)S(1)} collective-permute-done((bf16[256,1024]{1,0:T(8,128)(2,1)S(1)}, bf16[256,1024]{1,0:T(8,128)(2,1)S(1)}, u32[]{:S(2)}, u32[]{:S(2)}) %collective-permute-start.57) | collective-permute-done | bytes 524320 | tf_op jit(solution)/shard_map/ppermute | solution.py:698
  366.1 10.2 %collective-permute-done.60.refs_6_.refs_2_ = bf16[256,1024]{1,0:T(8,128)(2,1)S(1)} collective-permute-done((bf16[256,1024]{1,0:T(8,128)(2,1)S(1)}, bf16[256,1024]{1,0:T(8,128)(2,1)S(1)}, u32[]{:S(2)}, u32[]{:S(2)}) %collective-permute-start.60) | collective-permute-done | bytes 524320 | tf_op jit(solution)/shard_map/ppermute | solution.py:698
  378.8 12.7 %attend_backward.3 = (bf16[1024,768]{1,0:T(8,128)(2,1)S(1)}, f32[2,256]{1,0:T(2,128)S(1)}, bf16[256,1024]{1,0:T(8,128)(2,1)S(1)}, bf16[256,1024]{1,0:T(8,128)(2,...) custom-call(s32[4,4]{1,0:T(4,128)S(1)} %copy-done.132, ...), custom_call_target="tpu_custom_call" | custom-call | flops 402653184 | tf_op jit(solution)/shard_map/attend_backward/pallas_call | solution.py:39
  406.3 11.8 %collective-permute-done.66.refs_4_ = bf16[256,1024]{1,0:T(8,128)(2,1)} collective-permute-done((bf16[256,1024]{1,0:T(8,128)(2,1)}, bf16[256,1024]{1,0:T(8,128)(2,1)}, u32[]{:S(2)}, u32[]{:S(2)}) %collective-permute-start.66) | collective-permute-done | bytes 524320 | tf_op jit(solution)/shard_map/ppermute | solution.py:698
  425.4 9.1 %collective-permute-done.68.refs_1_.refs_7_ = bf16[256,1024]{1,0:T(8,128)(2,1)S(1)} collective-permute-done((bf16[256,1024]{1,0:T(8,128)(2,1)S(1)}, bf16[256,1024]{1,0:T(8,128)(2,1)S(1)}, u32[]{:S(2)}, u32[]{:S(2)}) %collective-permute-start.68) | collective-permute-done | bytes 524320 | tf_op jit(solution)/shard_map/ppermute | solution.py:698
  451.8 7.5 %collective-permute-done.73.refs_5_ = bf16[256,1024]{1,0:T(8,128)(2,1)S(1)} collective-permute-done((bf16[256,1024]{1,0:T(8,128)(2,1)S(1)}, bf16[256,1024]{1,0:T(8,128)(2,1)S(1)}, u32[]{:S(2)}, u32[]{:S(2)}) %collective-permute-start.73) | collective-permute-done | bytes 524320 | tf_op jit(solution)/shard_map/ppermute | solution.py:698
  461.1 8.0 %feed_weights.3 = (bf16[4,256,1024]{2,1,0:T(8,128)(2,1)S(1)}, bf16[4,256,1024]{2,1,0:T(8,128)(2,1)}) custom-call(s32[8]{0:T(128)S(1)} %get-tuple-element.457.order_ref, bf16[256,1024]{1,0:T(8,128)(2,1)} %get-tuple-element.299.refs_0_, bf16[256,1024]{1,0:T(8,128)(2,1)} %collective-permute-done.23.refs_1_, bf16[256,1024]{1,0:T(8,128)(2,1)} %collective-permute-done.24.refs_2_, ...), custom_call_target="tpu_custom_call" | custom-call | flops 214748368 | tf_op jit(solution)/shard_map/feed_weights/pallas_call | solution.py:39
  492.7 15.1 %attend_backward.4 = (bf16[1024,768]{1,0:T(8,128)(2,1)S(1)}, f32[2,256]{1,0:T(2,128)S(1)}, bf16[256,1024]{1,0:T(8,128)(2,1)S(1)}, bf16[256,1024]{1,0:T(8,128)(2,...) custom-call(s32[4,4]{1,0:T(4,128)S(1)} %copy-done.131, s32[1024,1]{1,0:T(8,128)S(1)} %copy-done.14, ...), custom_call_target="tpu_custom_call" | custom-call | flops 402653184 | tf_op jit(solution)/shard_map/attend_backward/pallas_call | solution.py:39
  513.9 8.8 %collective-permute-done.81.refs_2_.refs_6_ = bf16[256,1024]{1,0:T(8,128)(2,1)} collective-permute-done((bf16[256,1024]{1,0:T(8,128)(2,1)}, bf16[256,1024]{1,0:T(8,128)(2,1)}, u32[]{:S(2)}, u32[]{:S(2)}) %collective-permute-start.81) | collective-permute-done | bytes 524320 | tf_op jit(solution)/shard_map/ppermute | solution.py:698
  544.7 19.8 %attend_backward.5 = (bf16[1024,768]{1,0:T(8,128)(2,1)S(1)}, f32[2,256]{1,0:T(2,128)S(1)}, bf16[256,1024]{1,0:T(8,128)(2,1)S(1)}, bf16[256,1024]{1,0:T(8,128)(2,...) custom-call(s32[4,4]{1,0:T(4,128)S(1)} %copy-done.130, s32[1024,1]{1,0:T(8,128)S(1)} %copy.59.refs_1_, ...), custom_call_target="tpu_custom_call" | custom-call | flops 402653184 | tf_op jit(solution)/shard_map/attend_backward/pallas_call | solution.py:39
  576.4 12.9 %collective-permute-done.87.refs_1_ = bf16[4,128,768]{2,1,0:T(8,128)(2,1)S(1)} collective-permute-done((bf16[4,128,768]{2,1,0:T(8,128)(2,1)}, bf16[4,128,768]{2,1,0:T(8,128)(2,1)S(1)}, u32[]{:S(2)}, u32[]{:S(2)}) %collective-permute-start.87) | collective-permute-done | bytes 786464 | tf_op jit(solution)/shard_map/ppermute | solution.py:698
  595.0 10.9 %collective-permute-done.89.refs_5_ = bf16[256,1024]{1,0:T(8,128)(2,1)} collective-permute-done((bf16[256,1024]{1,0:T(8,128)(2,1)S(1)}, bf16[256,1024]{1,0:T(8,128)(2,1)}, u32[]{:S(2)}, u32[]{:S(2)}) %collective-permute-start.89) | collective-permute-done | bytes 524320 | tf_op jit(solution)/shard_map/ppermute | solution.py:698
  643.0 14.6 %collective-permute-done.96.refs_1_ = f32[32,1024]{1,0:T(8,128)S(1)} collective-permute-done((f32[32,1024]{1,0:T(8,128)S(1)}, f32[32,1024]{1,0:T(8,128)S(1)}, u32[]{:S(2)}, u32[]{:S(2)}) %collective-permute-start.96) | collective-permute-done | bytes 131104 | tf_op jit(solution)/shard_map/ppermute | solution.py:698
  670.0 7.1 collective-permute-done.101.other_ref
  683.2 9.3 %collective-permute-done.109.refs_1_ = bf16[128,768]{1,0:T(8,128)(2,1)S(1)} collective-permute-done((bf16[128,768]{1,0:T(8,128)(2,1)S(1)}, bf16[128,768]{1,0:T(8,128)(2,1)S(1)}, u32[]{:S(2)}, u32[]{:S(2)}) %collective-permute-start.109) | collective-permute-done | bytes 196640 | tf_op jit(solution)/shard_map/ppermute | solution.py:698
  (717 shorter events, 388.8 us)
Async XLA Ops:
  7.2 129.8 %all-gather.6.cloned.1.call-start = ((), (), s32[]{:S(2)}) async-start(), calls=%async_computation.7 | async-start | bytes 2621440 | tf_op jit(solution)/shard_map/all_gather | solution.py:806
  24.0 138.8 %all-gather.4.cloned.1.call-start = ((), (), s32[]{:S(2)}) async-start(), calls=%async_computation.6 | async-start | bytes 1966080 | tf_op jit(solution)/shard_map/all_gather | solution.py:806
  26.9 35.2 %collective-permute-start.9 = (bf16[128,768]{1,0:T(8,128)(2,1)S(1)}, bf16[128,768]{1,0:T(8,128)(2,1)S(1)}, u32[]{:S(2)}, u32[]{:S(2)}) collective-permute-start(bf16[128,768]{1,0:T(8,128)(2,1)S(1)} %get-tuple-element.272.refs_0_), channel_id=1, source_target_pairs={{0,4},{4,0},{8,12},{12,8},{16,20},{20,16},{24,28},{28,24},{1,5},{5... | collective-permute-start | bytes 589832 | tf_op jit(solution)/shard_map/ppermute | solution.py:698
  28.2 45.8 %collective-permute-start.4 = (bf16[256,1024]{1,0:T(8,128)(2,1)S(1)}, bf16[256,1024]{1,0:T(8,128)(2,1)}, u32[]{:S(2)}, u32[]{:S(2)}) collective-permute-start(bf16[256,1024]{1,0:T(8,128)(2,1)S(1)} %bitcast.72), channel_id=1, source_target_pairs={{0,1},{1,0},{2,3},{3,2},{4,5},{5,4},{6,7},{7,6},{8,9},{9,8},{10,11... | collective-permute-start | bytes 1572872 | tf_op jit(solution)/shard_map/ppermute | solution.py:698
  37.5 36.6 %collective-permute-start.5 = (bf16[256,1024]{1,0:T(8,128)(2,1)}, bf16[256,1024]{1,0:T(8,128)(2,1)S(1)}, u32[]{:S(2)}, u32[]{:S(2)}) collective-permute-start(bf16[256,1024]{1,0:T(8,128)(2,1)} %collective-permute-done.refs_1_), channel_id=1, source_target_pairs={{0,1},{1,0},{2,3},{3,2},{4,5},{5,4},{6,7},{7,6},{8,9},{9,8},{10,11... | collective-permute-start | bytes 1572872 | tf_op jit(solution)/shard_map/ppermute | solution.py:698
  89.3 183.2 %all-gather.8.cloned.1.call-start = ((), (), s32[]{:S(2)}) async-start(), calls=%async_computation.8 | async-start | bytes 2621440 | tf_op jit(solution)/shard_map/all_gather | solution.py:806
  136.9 47.6 %collective-permute-start.26 = (bf16[1024,1024]{1,0:T(8,128)(2,1)}, bf16[1024,1024]{1,0:T(8,128)(2,1)}, u32[]{:S(2)}, u32[]{:S(2)}) collective-permute-start(bf16[1024,1024]{1,0:T(8,128)(2,1)} %all-gather.6.cloned.1.call-done.refs_0_), channel_id=1, source_target_pairs={{0,4},{4,0},{8,12},{12,8},{16,20},{20,16},{24,28},{28,24},{1,5},{5... | collective-permute-start | bytes 6291464 | tf_op jit(solution)/shard_map/ppermute | solution.py:698
  161.2 362.4 %reduce-scatter.9.cloned.1.call-start = ((), (), s32[]{:S(2)}) async-start(), calls=%async_computation.10 | async-start | bytes 2621440 | tf_op jit(solution)/shard_map/reduce_scatter | solution.py:820
  161.5 26.6 %collective-permute-start.24 = (bf16[256,1024]{1,0:T(8,128)(2,1)}, bf16[256,1024]{1,0:T(8,128)(2,1)}, u32[]{:S(2)}, u32[]{:S(2)}) collective-permute-start(bf16[256,1024]{1,0:T(8,128)(2,1)} %get-tuple-element.299.refs_0_), channel_id=1, source_target_pairs={{0,1},{1,0},{2,3},{3,2},{4,5},{5,4},{6,7},{7,6},{8,9},{9,8},{10,11... | collective-permute-start | bytes 1572872 | tf_op jit(solution)/shard_map/ppermute | solution.py:698
  175.5 28.6 %collective-permute-start.30 = (bf16[256,1024]{1,0:T(8,128)(2,1)}, bf16[256,1024]{1,0:T(8,128)(2,1)}, u32[]{:S(2)}, u32[]{:S(2)}) collective-permute-start(bf16[256,1024]{1,0:T(8,128)(2,1)} %bitcast.19.refs_0_), channel_id=1, source_target_pairs={{0,2},{1,3},{2,0},{3,1},{4,6},{5,7},{6,4},{7,5},{8,10},{9,11},{10,... | collective-permute-start | bytes 1572872 | tf_op jit(solution)/shard_map/ppermute | solution.py:698
  175.9 32.4 %collective-permute-start.33 = (bf16[512,768]{1,0:T(8,128)(2,1)}, bf16[512,768]{1,0:T(8,128)(2,1)}, u32[]{:S(2)}, u32[]{:S(2)}) collective-permute-start(bf16[512,768]{1,0:T(8,128)(2,1)} %part_rows.2.refs_0_), channel_id=1, source_target_pairs={{0,4},{4,0},{8,12},{12,8},{16,20},{20,16},{24,28},{28,24},{1,5},{5... | collective-permute-start | bytes 2359304 | tf_op jit(solution)/shard_map/ppermute | solution.py:698
  226.7 45.8 %collective-permute-start.43 = (bf16[512,768]{1,0:T(8,128)(2,1)}, bf16[512,768]{1,0:T(8,128)(2,1)}, u32[]{:S(2)}, u32[]{:S(2)}) collective-permute-start(bf16[512,768]{1,0:T(8,128)(2,1)} %part_rows.3.refs_0_), channel_id=1, source_target_pairs={{0,4},{4,0},{8,12},{12,8},{16,20},{20,16},{24,28},{28,24},{1,5},{5... | collective-permute-start | bytes 2359304 | tf_op jit(solution)/shard_map/ppermute | solution.py:698
  272.5 47.4 %collective-permute-start.48 = (bf16[1024,1024]{1,0:T(8,128)(2,1)}, bf16[1024,1024]{1,0:T(8,128)(2,1)S(1)}, u32[]{:S(2)}, u32[]{:S(2)}) collective-permute-start(bf16[1024,1024]{1,0:T(8,128)(2,1)} %all-gather.8.cloned.1.call-done.refs_0_), channel_id=1, source_target_pairs={{0,4},{4,0},{8,12},{12,8},{16,20},{20,16},{24,28},{28,24},{1,5},{5... | collective-permute-start | bytes 6291464 | tf_op jit(solution)/shard_map/ppermute | solution.py:698
  346.2 55.8 %collective-permute-start.64 = (bf16[4,256,1024]{2,1,0:T(8,128)(2,1)S(1)}, bf16[4,256,1024]{2,1,0:T(8,128)(2,1)S(1)}, u32[]{:S(2)}, u32[]{:S(2)}) collective-permute-start(bf16[4,256,1024]{2,1,0:T(8,128)(2,1)S(1)} %get-tuple-element.399), channel_id=1, source_target_pairs={{0,4},{4,0},{8,12},{12,8},{16,20},{20,16},{24,28},{28,24},{1,5},{5... | collective-permute-start | bytes 6291464 | tf_op jit(solution)/shard_map/ppermute | solution.py:698
  403.8 190.2 %reduce-scatter.7.cloned.1.call-start = ((), (), s32[]{:S(2)}) async-start(), calls=%async_computation.9 | async-start | bytes 983040 | tf_op jit(solution)/shard_map/reduce_scatter | solution.py:820
  446.2 36.9 %collective-permute-start.76 = (bf16[4,128,768]{2,1,0:T(8,128)(2,1)S(1)}, bf16[4,128,768]{2,1,0:T(8,128)(2,1)S(1)}, u32[]{:S(2)}, u32[]{:S(2)}) collective-permute-start(bf16[4,128,768]{2,1,0:T(8,128)(2,1)S(1)} %copy-done.142), channel_id=1, source_target_pairs={{0,4},{4,0},{8,12},{12,8},{16,20},{20,16},{24,28},{28,24},{1,5},{5... | collective-permute-start | bytes 2359304 | tf_op jit(solution)/shard_map/ppermute | solution.py:698
  450.3 25.5 %collective-permute-start.75 = (bf16[256,1024]{1,0:T(8,128)(2,1)S(1)}, bf16[256,1024]{1,0:T(8,128)(2,1)S(1)}, u32[]{:S(2)}, u32[]{:S(2)}) collective-permute-start(bf16[256,1024]{1,0:T(8,128)(2,1)S(1)} %add_low.32), channel_id=1, source_target_pairs={{0,2},{1,3},{2,0},{3,1},{4,6},{5,7},{6,4},{7,5},{8,10},{9,11},{10,... | collective-permute-start | bytes 1572872 | tf_op jit(solution)/shard_map/ppermute | solution.py:698
  470.5 63.2 %collective-permute-start.84 = (bf16[4,256,1024]{2,1,0:T(8,128)(2,1)}, bf16[4,256,1024]{2,1,0:T(8,128)(2,1)}, u32[]{:S(2)}, u32[]{:S(2)}) collective-permute-start(bf16[4,256,1024]{2,1,0:T(8,128)(2,1)} %get-tuple-element.451), channel_id=1, source_target_pairs={{0,4},{4,0},{8,12},{12,8},{16,20},{20,16},{24,28},{28,24},{1,5},{5... | collective-permute-start | bytes 6291464 | tf_op jit(solution)/shard_map/ppermute | solution.py:698
  484.5 139.2 %reduce-scatter.13.cloned.1.call-start = ((), (), s32[]{:S(2)}) async-start(), calls=%async_computation.12 | async-start | bytes 2621440 | tf_op jit(solution)/shard_map/reduce_scatter | solution.py:820
  537.1 93.2 %reduce-scatter.15.cloned.1.call-start = ((), (), s32[]{:S(2)}) async-start(), calls=%async_computation.13 | async-start | bytes 983040 | tf_op jit(solution)/shard_map/reduce_scatter | solution.py:820
  537.5 30.6 %collective-permute-start.85 = (bf16[4,96,1024]{2,1,0:T(8,128)(2,1)}, bf16[4,96,1024]{2,1,0:T(8,128)(2,1)S(1)}, u32[]{:S(2)}, u32[]{:S(2)}) collective-permute-start(bf16[4,96,1024]{2,1,0:T(8,128)(2,1)} %copy-done.145), channel_id=1, source_target_pairs={{0,4},{4,0},{8,12},{12,8},{16,20},{20,16},{24,28},{28,24},{1,5},{5... | collective-permute-start | bytes 2359304 | tf_op jit(solution)/shard_map/ppermute | solution.py:698
  570.1 87.5 %reduce-scatter.17.cloned.1.call-start = ((), (), s32[]{:S(2)}) async-start(), calls=%async_computation.14 | async-start | bytes 983040 | tf_op jit(solution)/shard_map/reduce_scatter | solution.py:820
  590.4 113.9 %reduce-scatter.11.cloned.1.call-start = ((), (), s32[]{:S(2)}) async-start(), calls=%async_computation.11 | async-start | bytes 983040 | tf_op jit(solution)/shard_map/reduce_scatter | solution.py:820
  590.7 30.7 %collective-permute-start.92 = (bf16[4,128,768]{2,1,0:T(8,128)(2,1)}, bf16[4,128,768]{2,1,0:T(8,128)(2,1)}, u32[]{:S(2)}, u32[]{:S(2)}) collective-permute-start(bf16[4,128,768]{2,1,0:T(8,128)(2,1)} %copy-done.144), channel_id=1, source_target_pairs={{0,4},{4,0},{8,12},{12,8},{16,20},{20,16},{24,28},{28,24},{1,5},{5... | collective-permute-start | bytes 2359304 | tf_op jit(solution)/shard_map/ppermute | solution.py:698
  592.6 24.6 %collective-permute-start.91 = (bf16[256,1024]{1,0:T(8,128)(2,1)}, bf16[256,1024]{1,0:T(8,128)(2,1)}, u32[]{:S(2)}, u32[]{:S(2)}) collective-permute-start(bf16[256,1024]{1,0:T(8,128)(2,1)} %copy-done.92), channel_id=1, source_target_pairs={{0,2},{1,3},{2,0},{3,1},{4,6},{5,7},{6,4},{7,5},{8,10},{9,11},{10,... | collective-permute-start | bytes 1572872 | tf_op jit(solution)/shard_map/ppermute | solution.py:698
  631.3 27.3 %collective-permute-start.97 = (bf16[96,1024]{1,0:T(8,128)(2,1)S(1)}, bf16[96,1024]{1,0:T(8,128)(2,1)S(1)}, u32[]{:S(2)}, u32[]{:S(2)}) collective-permute-start(bf16[96,1024]{1,0:T(8,128)(2,1)S(1)} %add_low.43.refs_0_), channel_id=1, source_target_pairs={{8,0},{12,4},{17,9},{21,13},{26,18},{30,22},{3,27},{7,31}} | collective-permute-start | bytes 589832 | tf_op jit(solution)/shard_map/ppermute | solution.py:869
  631.9 26.7 %collective-permute-start.98 = (bf16[96,1024]{1,0:T(8,128)(2,1)S(1)}, bf16[96,1024]{1,0:T(8,128)(2,1)S(1)}, u32[]{:S(2)}, u32[]{:S(2)}) collective-permute-start(bf16[96,1024]{1,0:T(8,128)(2,1)S(1)} %add_low.43.refs_0_), channel_id=1, source_target_pairs={{16,0},{20,4},{25,9},{29,13},{2,18},{6,22},{11,27},{15,31}} | collective-permute-start | bytes 589832 | tf_op jit(solution)/shard_map/ppermute | solution.py:869
  632.6 26.0 %collective-permute-start.99 = (bf16[96,1024]{1,0:T(8,128)(2,1)S(1)}, bf16[96,1024]{1,0:T(8,128)(2,1)S(1)}, u32[]{:S(2)}, u32[]{:S(2)}) collective-permute-start(bf16[96,1024]{1,0:T(8,128)(2,1)S(1)} %add_low.43.refs_0_), channel_id=1, source_target_pairs={{24,0},{28,4},{1,9},{5,13},{10,18},{14,22},{19,27},{23,31}} | collective-permute-start | bytes 589832 | tf_op jit(solution)/shard_map/ppermute | solution.py:869
  659.3 35.4 %collective-permute-start.116 = (bf16[256,1024]{1,0:T(8,128)(2,1)S(1)}, bf16[256,1024]{1,0:T(8,128)(2,1)}, u32[]{:S(2)}, u32[]{:S(2)}) collective-permute-start(bf16[256,1024]{1,0:T(8,128)(2,1)S(1)} %copy-done.39), channel_id=1, source_target_pairs={{0,1},{1,0},{2,3},{3,2},{4,5},{5,4},{6,7},{7,6},{8,9},{9,8},{10,11... | collective-permute-start | bytes 1572872 | tf_op jit(solution)/shard_map/ppermute | solution.py:698
  660.6 34.1 %collective-permute-start.117 = (bf16[256,1024]{1,0:T(8,128)(2,1)}, bf16[256,1024]{1,0:T(8,128)(2,1)}, u32[]{:S(2)}, u32[]{:S(2)}) collective-permute-start(bf16[256,1024]{1,0:T(8,128)(2,1)} %collective-permute-done.115.refs_1_), channel_id=1, source_target_pairs={{0,1},{1,0},{2,3},{3,2},{4,5},{5,4},{6,7},{7,6},{8,9},{9,8},{10,11... | collective-permute-start | bytes 1572872 | tf_op jit(solution)/shard_map/ppermute | solution.py:698
  664.4 37.1 %collective-permute-start.112 = (bf16[256,1024]{1,0:T(8,128)(2,1)S(1)}, bf16[256,1024]{1,0:T(8,128)(2,1)}, u32[]{:S(2)}, u32[]{:S(2)}) collective-permute-start(bf16[256,1024]{1,0:T(8,128)(2,1)S(1)} %add_low.42.refs_0_), channel_id=1, source_target_pairs={{0,2},{1,3},{2,0},{3,1},{4,6},{5,7},{6,4},{7,5},{8,10},{9,11},{10,... | collective-permute-start | bytes 1572872 | tf_op jit(solution)/shard_map/ppermute | solution.py:698
  679.2 29.7 %collective-permute-start.102 = (bf16[3,128,1024]{2,1,0:T(8,128)(2,1)S(1)}, bf16[3,128,1024]{2,1,0:T(8,128)(2,1)S(1)}, u32[]{:S(2)}, u32[]{:S(2)}) collective-permute-start(bf16[3,128,1024]{2,1,0:T(8,128)(2,1)S(1)} %choose.2.one_ref), channel_id=1, source_target_pairs={{0,1},{1,0},{2,3},{3,2},{4,5},{5,4},{6,7},{7,6},{8,9},{9,8},{10,11... | collective-permute-start | bytes 2359304 | tf_op jit(solution)/shard_map/ppermute | solution.py:698
  (267 other events, 2371.0 us)
Sparse Core Ops, SparseCore 0:
  24.1 58.6 all-gather.5
  89.4 44.9 all-gather.3
  161.3 50.1 all-gather.7
  403.9 49.3 reduce-scatter.8
  484.6 27.4 reduce-scatter.6
  537.2 49.1 reduce-scatter.12
  588.7 21.4 reduce-scatter.14
  612.6 22.4 reduce-scatter.16
  638.0 26.1 reduce-scatter.10

commit v4 on v3

--- a/solution.py
+++ b/solution.py
@@ -22,6 +22,7 @@
 
 class Turn:
     last = None
+    done = None
 
 
 def after(values, earlier):
@@ -480,19 +481,45 @@
     return run(kernel, outs, [order, *flat], name, flops, scratch, scalars=1)
 
 
-def order_combiners(exits, table):
-    shards = table.shape[0]
-    rows = exits[0].shape[0] // shards
-
-    def kernel(table_ref, *refs):
+def join_blocks(blocks, exits, table):
+    keep, sent = blocks
+    half, height, width = keep.shape
+    rows, full = exits[0].shape[0] // (2 * half), exits[0].shape[1]
+    rest = full - width
+    tall = rows * len(exits)
+
+    def kernel(table_ref, keep_ref, sent_ref, *refs):
         sources = refs[: len(exits)]
         for i, (target, at) in enumerate(block_targets(refs[len(exits) :])):
+            former = keep_ref if i < half else sent_ref
+            target[at, :height, :] = former[at]
             where = pl.ds(pl.multiple_of(table_ref[i], rows), rows)
             for block, source in enumerate(sources):
-                target[at, block * rows : (block + 1) * rows, :] = source[where, :]
-
-    outs = blocks_out(shards, rows * len(exits), exits[0].shape[1])
-    return run(kernel, outs, [table, *exits], "order_combiners", 1, scalars=1)
+                top = height + block * rows
+                target[at, top : top + rows, :] = source[where, :width]
+                side = slice(block * rest, (block + 1) * rest)
+                target[at, height + tall : height + tall + rows, side] = source[where, width:]
+
+    outs = [shape((half, height + tall + rows, width), low)] * 2
+    return run(kernel, outs, [table, keep, sent, *exits], "join_blocks", 1, scalars=1)
+
+
+def part_blocks(share, height, blocks, rows, full):
+    width = share.shape[1]
+    rest = full - width
+    tall = rows * blocks
+
+    def kernel(share_ref, first_ref, second_ref):
+        first_ref[...] = share_ref[:height, :]
+        for block in range(blocks):
+            where = slice(block * rows, (block + 1) * rows)
+            top = height + block * rows
+            second_ref[where, :width] = share_ref[top : top + rows, :]
+            side = slice(block * rest, (block + 1) * rest)
+            second_ref[where, width:] = share_ref[height + tall : height + tall + rows, side]
+
+    outs = [shape((height, width), low), shape((tall, full), low)]
+    return run(kernel, outs, [share], "part_blocks", 1)
 
 
 def cut(arrays, table, moves, outs, name):
@@ -517,7 +544,7 @@
         in_specs=[SMEM] + [anywhere] * len(arrays),
         out_specs=[VMEM] * len(outs),
         scratch_shapes=[pltpu.SemaphoreType.DMA((len(moves),))],
-        compiler_params=pltpu.CompilerParams(vmem_limit_bytes=16 << 20),
+        compiler_params=pltpu.CompilerParams(vmem_limit_bytes=60 << 20),
         cost_estimate=pl.CostEstimate(flops=1, bytes_accessed=0, transcendentals=0),
         name=name,
     )
@@ -528,10 +555,12 @@
     count = len(pieces)
 
     def kernel(table_ref, *refs):
-        sources = refs[:count]
-        refs = refs[count + len(former) :]
-        targets, buffers, semaphore = refs[: len(outputs)], refs[len(outputs) : -1], refs[-1]
+        sources, begun_ref = refs[:count], refs[count]
+        refs = refs[count + 1 + len(former) :]
+        targets, done_ref = refs[: len(outputs)], refs[len(outputs)]
+        buffers, semaphore = refs[len(outputs) + 1 : -1], refs[-1]
         copies = []
+        done_ref[...] = begun_ref[...]
         for i, ((_, block, moves), target, buffer) in enumerate(zip(outputs, targets, buffers)):
             for which, source in enumerate(sources):
                 owner = table_ref[which]
@@ -548,12 +577,12 @@
             started.wait()
 
     anywhere = pl.BlockSpec(memory_space=pl.ANY)
-    aliases = {1 + count + i: i for i in range(len(former))}
+    aliases = {2 + count + i: i for i in range(len(former))}
     call = pl.pallas_call(
         kernel,
-        out_shape=[shape(size, high) for size, _, _ in outputs],
-        in_specs=[SMEM] + [VMEM] * count + [anywhere] * len(former),
-        out_specs=[anywhere] * len(outputs),
+        out_shape=[shape(size, high) for size, _, _ in outputs] + [shape(Turn.done.shape, high)],
+        in_specs=[SMEM] + [VMEM] * (count + 1) + [anywhere] * len(former),
+        out_specs=[anywhere] * len(outputs) + [VMEM],
         scratch_shapes=[pltpu.VMEM(size[1:], high) for size, _, _ in outputs]
         + [pltpu.SemaphoreType.DMA((len(outputs),))],
         input_output_aliases=aliases,
@@ -561,8 +590,9 @@
         cost_estimate=pl.CostEstimate(flops=1, bytes_accessed=0, transcendentals=0),
         name=name,
     )
-    table = hold(table)
-    return call(table, *pieces, *former)
+    *results, Turn.done = call(hold(table), *pieces, Turn.done, *former)
+    Turn.last = Turn.done
+    return results
 
 
 def lay_sums(rows, shares, hidden, me, shards):
@@ -958,7 +988,7 @@
     source_cotangent,
     target_cotangent,
 ):
-    Turn.last = None
+    Turn.last, Turn.done = None, norm_gains[:, :128]
     source_tokens, target_tokens = source_tokens[0], target_tokens[0]
     source_cotangent, target_cotangent = source_cotangent[0], target_cotangent[0]
     count, shards = lax.axis_size("seq"), lax.axis_size("batch")
@@ -1130,10 +1160,10 @@
     )
     mixture, total = attend_forward(*self_view, *projected, heads, True)
     decoder_stored = (*projected, mixture, total)
+    memory_low = residual_low(middle, memory_partials.finish(), reducer_biases[0:1])
+    memory_spread = Spread(memory_low)
     decoder_partials = Collect(project_out(mixture, leaves[1], count))
     decoder_partials.turn()
-    memory_low = residual_low(middle, memory_partials.finish(), reducer_biases[0:1])
-    memory_spread = Spread(memory_low)
     if quick():
         last_other = to_side(hold(last_line))
     self_out, self_normed = residual_norm(
@@ -1244,25 +1274,25 @@
     self_incoming_pieces = self_incoming_spread.finish()
     if quick():
         cross_shares.turn()
+    decoder_exit = exit_gradient(decoder_stored, self_incoming_pieces)
     decoder_joined, decoder_sums, decoder_partials, _ = attend_backward(
         *self_view, self_incoming_pieces, leaves[1], decoder_entry, decoder_stored, heads, True, False
     )
     decoder_partials = Collect(decoder_partials)
-    decoder_shares = sums_over_batch(
-        outer_sums([([decoder_normed], [decoder_joined], 0, 3 * share)], order, "attention_weights")
-    )
-    decoder_partials.turn()
+    decoder_blocks = outer_sums(
+        [([decoder_normed], [decoder_joined], 0, 3 * share)], order, "attention_weights"
+    )
     middle_incoming_pieces = middle_incoming_spread.finish()
-    if quick():
-        decoder_feed_spread = Spread(decoder_feed_shares.finish())
-    decoder_exit = exit_gradient(decoder_stored, self_incoming_pieces)
     encoder_exit = exit_gradient(encoder_stored, middle_incoming_pieces)
     exits = [encoder_exit, decoder_exit, cross_exit]
     if quick():
         table = ((order % 2) * 4 + order // 2) * piece
-        exit_scatter = Scatter(order_combiners(exits, table))
+        decoder_shares = Scatter(join_blocks(decoder_blocks, exits, table))
         encoder_feed_shares.turn()
-        decoder_feed_pieces = decoder_feed_spread.finish()
+        decoder_feed_share, cross_share = decoder_feed_shares.finish(), cross_shares.finish()
+    else:
+        decoder_shares = sums_over_batch(decoder_blocks)
+    decoder_partials.turn()
     encoder_joined, encoder_sums, encoder_partials, _ = attend_backward(
         *encoder_view,
         middle_incoming_pieces,
@@ -1274,15 +1304,14 @@
         False,
     )
     encoder_partials = Collect(encoder_partials)
-    if quick():
-        exit_scatter.turn()
     encoder_shares = sums_over_batch(
         outer_sums([([encoder_normed], [encoder_joined], 0, 3 * share)], order, "attention_weights")
     )
     encoder_partials.turn()
     if quick():
         decoder_shares.turn()
-        cross_spread = Spread(cross_shares.finish())
+        encoder_feed_share = encoder_feed_shares.finish()
+        decoder_feed_spread = Spread(decoder_feed_share)
     target_gradient, _, norm_two = norm_backward(
         target_tokens, gain(2), self_incoming, decoder_partials.finish()
     )
@@ -1292,14 +1321,6 @@
 
     norms = (norm_zero, norm_one, norm_two, norm_three, norm_four)
     if quick():
-        laid = lay_sums(
-            [*norms, source_sum, target_sum],
-            [encoder_sums, decoder_sums, cross_sums],
-            [encoder_hidden_sum, decoder_hidden_sum],
-            me[None],
-            shards,
-        )
-        summed = Sum(laid)
         owners = me ^ jnp.array(seq_offsets(), jnp.int32)
         entry_moves = [
             ((0, rows), (part * share, share), (0, 0), (part * model_width, share))
@@ -1322,24 +1343,36 @@
             ]
             return finish(shares, owners, former, outputs, "finish_feed")
 
+        laid = lay_sums(
+            [*norms, source_sum, target_sum],
+            [encoder_sums, decoder_sums, cross_sums],
+            [encoder_hidden_sum, decoder_hidden_sum],
+            me[None],
+            shards,
+        )
+        summed = Sum(laid)
         encoder_shares.turn()
+        cross_spread = Spread(cross_share)
+        feeds_whole = finish_feed(1, decoder_feed_spread.finish(), [])
         summed.turn()
-        feeds_whole = finish_feed(1, decoder_feed_pieces, [])
-        feed_spread = Spread(encoder_feed_shares.finish())
+        feed_spread = Spread(encoder_feed_share)
+        entry_whole = finish_entry(2, cross_spread.finish(), [])
         summed.turn()
-        entry_whole = finish_entry(2, cross_spread.finish(), [])
-        exit_return = Return(exit_scatter.finish(), 3)
+        decoder_share, exit_share = part_blocks(
+            decoder_shares.finish(), rows, 3, piece, model_width
+        )
+        feeds_whole = finish_feed(0, feed_spread.finish(), feeds_whole)
+        exit_return = Return(exit_share, 3)
         summed.turn()
-        feeds_whole = finish_feed(0, feed_spread.finish(), feeds_whole)
+        decoder_spread = Spread(decoder_share)
         summed.turn()
-        decoder_spread = Spread(decoder_shares.finish())
         exit_return.turn()
+        entry_whole = finish_entry(1, decoder_spread.finish(), entry_whole)
         summed.turn()
         summed = summed.values
         exit_return.turn()
-        entry_whole = finish_entry(1, decoder_spread.finish(), entry_whole)
+        combiners_gradient = exit_return.finish()
         encoder_spread = Spread(encoder_shares.finish())
-        combiners_gradient = exit_return.finish()
         entry_whole = finish_entry(0, encoder_spread.finish(), entry_whole)
         projections_gradient = entry_whole[0]
         expanders_gradient, reducers_gradient = feeds_whole

time: 735 us -> 715 us (0.973)
  waiting for transfers between devices: 299 us -> 288 us
  local copies, waits for them, and re-layouts: 96.2 us -> 87.8 us
    ppermute x6, waiting for transfers between devices: 42.6 us -> 29.2 us  [touch(): self.line.append(lax.ppermute(newest, 'batch', pairs))]
    unnamed x344 -> x338, local copies, waits for them, and re-layouts: 89 us -> 81.7 us
    ppermute x106 -> x105, waiting for transfers between devices: 252 us -> 248 us  [swap(): lax.ppermute(values, axis, [(i, i ^ bit) for i in range(lax.axis_size(axi...]
    pallas_call x80 -> x79, Pallas kernels: 188 us -> 184 us  [take_turn(): results = call(*args)]
    ppermute x106 -> x105, starting transfers between devices: 103 us -> 99.9 us  [swap(): lax.ppermute(values, axis, [(i, i ^ bit) for i in range(lax.axis_size(axi...]
  transfers between devices with their start and end apart: 127 -> 125, of which waited for: 50 -> 52; matrix products, arithmetic and copies ran while one was open for 2% -> 2% of each run, Pallas kernels for 26% -> 26%
where the time goes in v4:
time: 715 us; the launch traced here: 705 us
  waiting for transfers between devices  288 us (40%)
  Pallas kernels  196 us (27%)
  starting transfers between devices  113 us (16%)
  local copies, waits for them, and re-layouts  87.8 us (12%)
  between operations  16.6 us (2%)
    ppermute x105, waiting for transfers between devices, swap(): lax.ppermute(values, axis, [(i, i ^ bit) for i in range(lax.axis_size(axi...  248 us
    pallas_call x79, Pallas kernels, take_turn(): results = call(*args)  184 us
    ppermute x105, starting transfers between devices, swap(): lax.ppermute(values, axis, [(i, i ^ bit) for i in range(lax.axis_size(axi...  99.9 us
    unnamed x338, local copies, waits for them, and re-layouts  81.7 us
    ppermute x6, waiting for transfers between devices, touch(): self.line.append(lax.ppermute(newest, 'batch', pairs))  29.2 us
  transfers between devices with their start and end apart: 125, of which 52 were waited for; matrix products, arithmetic and copies ran while one was open for 2% of the time, Pallas kernels for 26%

profile of v4, /device:TPU:1, one launch (start us, length us, event | category | flops | bytes accessed | tf_op | source)
XLA Modules:
  0.0 705.3 jit_solution(5862612585791555892)
XLA Ops:
  27.4 6.1 collective-permute-start.4
  35.4 10.7 %collective-permute-done.7.refs_2_ = bf16[128,768]{1,0:T(8,128)(2,1)S(1)} collective-permute-done((bf16[128,768]{1,0:T(8,128)(2,1)S(1)}, bf16[128,768]{1,0:T(8,128)(2,1)S(1)}, u32[]{:S(2)}, u32[]{:S(2)}) %collective-permute-start.7) | collective-permute-done | bytes 196640 | tf_op jit(solution)/shard_map/ppermute | solution.py:828
  49.5 8.7 %collective-permute-done.8.refs_3_ = bf16[128,768]{1,0:T(8,128)(2,1)S(1)} collective-permute-done((bf16[128,768]{1,0:T(8,128)(2,1)S(1)}, bf16[128,768]{1,0:T(8,128)(2,1)S(1)}, u32[]{:S(2)}, u32[]{:S(2)}) %collective-permute-start.8) | collective-permute-done | bytes 196640 | tf_op jit(solution)/shard_map/ppermute | solution.py:828
  82.5 6.8 attend_forward.3
  91.0 6.6 collective-permute-done.14.refs_2_
  120.4 10.3 %collective-permute-start.21 = (bf16[256,1024]{1,0:T(8,128)(2,1)}, bf16[256,1024]{1,0:T(8,128)(2,1)}, u32[]{:S(2)}, u32[]{:S(2)}) collective-permute-start(bf16[256,1024]{1,0:T(8,128)(2,1)} %get-tuple-element.301), channel_id=1, source_target_pairs={{0,1},{1,0},{2,3},{3,2},{4,5},{5,4},{6,7},{7,6},{8,9},{9,8},{10,11... | collective-permute-start | bytes 1572872 | tf_op jit(solution)/shard_map/ppermute | solution.py:728
  139.5 9.5 %collective-permute-done.22.refs_3_ = bf16[256,1024]{1,0:T(8,128)(2,1)} collective-permute-done((bf16[256,1024]{1,0:T(8,128)(2,1)}, bf16[256,1024]{1,0:T(8,128)(2,1)}, u32[]{:S(2)}, u32[]{:S(2)}) %collective-permute-start.22) | collective-permute-done | bytes 524320 | tf_op jit(solution)/shard_map/ppermute | solution.py:728
  159.4 7.8 %collective-permute-done.23.refs_1_ = bf16[256,1024]{1,0:T(8,128)(2,1)} collective-permute-done((bf16[256,1024]{1,0:T(8,128)(2,1)}, bf16[256,1024]{1,0:T(8,128)(2,1)}, u32[]{:S(2)}, u32[]{:S(2)}) %collective-permute-start.23) | collective-permute-done | bytes 524320 | tf_op jit(solution)/shard_map/ppermute | solution.py:728
  170.1 8.1 %collective-permute-done.26.refs_1_ = bf16[1024,1024]{1,0:T(8,128)(2,1)} collective-permute-done((bf16[1024,1024]{1,0:T(8,128)(2,1)}, bf16[1024,1024]{1,0:T(8,128)(2,1)}, u32[]{:S(2)}, u32[]{:S(2)}) %collective-permute-start.26) | collective-permute-done | bytes 2097184 | tf_op jit(solution)/shard_map/ppermute | solution.py:728
  181.8 9.7 %feed_forward.2 = (bf16[1024,1024]{1,0:T(8,128)(2,1)S(1)}, bf16[1024,1024]{1,0:T(8,128)(2,1)S(1)}, bf16[256,1024]{1,0:T(8,128)(2,1)S(1)}, bf16[256,1024]{1,0:T(8...) custom-call(bf16[256,1024]{1,0:T(8,128)(2,1)} %get-tuple-element.306.refs_0_, ...), custom_call_target="tpu_custom_call" | custom-call | flops 214748368 | tf_op jit(solution)/shard_map/feed_forward/pallas_call | solution.py:40
  198.6 15.8 %collective-permute-done.33.refs_1_ = bf16[512,768]{1,0:T(8,128)(2,1)} collective-permute-done((bf16[512,768]{1,0:T(8,128)(2,1)}, bf16[512,768]{1,0:T(8,128)(2,1)}, u32[]{:S(2)}, u32[]{:S(2)}) %collective-permute-start.33) | collective-permute-done | bytes 786464 | tf_op jit(solution)/shard_map/ppermute | solution.py:728
  221.9 7.2 %attend_forward.4 = (bf16[1024,256]{1,0:T(8,128)(2,1)S(1)}, f32[8,1024]{1,0:T(8,128)S(1)}) custom-call(s32[4,4]{1,0:T(4,128)S(1)} %copy-done.135, s32[1024,1]{1,0:T(8,128)S(1)} %copy-done.9, s32[1,1024]{1,0:T(1,128)S(1)} %bitcast.88, s32[1024,1]{1,0:T(8,128)S(1)} %copy.60.refs_3_, s32[1,1024]{1,0:T(1,128)S(1)} %bitcast.81, ...), custom_call_target="tpu_custom_call" | custom-call | flops 107374184 | tf_op jit(solution)/shard_map/attend_forward/pallas_call | solution.py:40
  236.6 11.7 %collective-permute-done.36.refs_3_ = bf16[256,1024]{1,0:T(8,128)(2,1)S(1)} collective-permute-done((bf16[256,1024]{1,0:T(8,128)(2,1)S(1)}, bf16[256,1024]{1,0:T(8,128)(2,1)S(1)}, u32[]{:S(2)}, u32[]{:S(2)}) %collective-permute-start.36) | collective-permute-done | bytes 524320 | tf_op jit(solution)/shard_map/ppermute | solution.py:728
  253.7 5.8 collective-permute-done.40.refs_5_.refs_6_
  261.5 9.2 %collective-permute-done.37.refs_1_ = bf16[256,1024]{1,0:T(8,128)(2,1)} collective-permute-done((bf16[256,1024]{1,0:T(8,128)(2,1)}, bf16[256,1024]{1,0:T(8,128)(2,1)}, u32[]{:S(2)}, u32[]{:S(2)}) %collective-permute-start.37) | collective-permute-done | bytes 524320 | tf_op jit(solution)/shard_map/ppermute | solution.py:728
  277.8 6.3 attend_forward.5
  287.6 12.6 %collective-permute-done.46.refs_3_ = bf16[256,1024]{1,0:T(8,128)(2,1)S(1)} collective-permute-done((bf16[256,1024]{1,0:T(8,128)(2,1)S(1)}, bf16[256,1024]{1,0:T(8,128)(2,1)S(1)}, u32[]{:S(2)}, u32[]{:S(2)}) %collective-permute-start.46) | collective-permute-done | bytes 524320 | tf_op jit(solution)/shard_map/ppermute | solution.py:728
  304.1 15.3 %collective-permute-done.48.refs_1_ = bf16[1024,1024]{1,0:T(8,128)(2,1)S(1)} collective-permute-done((bf16[1024,1024]{1,0:T(8,128)(2,1)}, bf16[1024,1024]{1,0:T(8,128)(2,1)S(1)}, u32[]{:S(2)}, u32[]{:S(2)}) %collective-permute-start.48) | collective-permute-done | bytes 2097184 | tf_op jit(solution)/shard_map/ppermute | solution.py:728
  326.4 6.2 feed_forward.3
  357.0 7.5 %collective-permute-done.57.refs_3_ = bf16[256,1024]{1,0:T(8,128)(2,1)S(1)} collective-permute-done((bf16[256,1024]{1,0:T(8,128)(2,1)S(1)}, bf16[256,1024]{1,0:T(8,128)(2,1)S(1)}, u32[]{:S(2)}, u32[]{:S(2)}) %collective-permute-start.57) | collective-permute-done | bytes 524320 | tf_op jit(solution)/shard_map/ppermute | solution.py:728
  365.5 10.2 %collective-permute-done.60.refs_6_.refs_2_ = bf16[256,1024]{1,0:T(8,128)(2,1)S(1)} collective-permute-done((bf16[256,1024]{1,0:T(8,128)(2,1)S(1)}, bf16[256,1024]{1,0:T(8,128)(2,1)S(1)}, u32[]{:S(2)}, u32[]{:S(2)}) %collective-permute-start.60) | collective-permute-done | bytes 524320 | tf_op jit(solution)/shard_map/ppermute | solution.py:728
  378.2 12.7 %attend_backward.3 = (bf16[1024,768]{1,0:T(8,128)(2,1)S(1)}, f32[2,256]{1,0:T(2,128)S(1)}, bf16[256,1024]{1,0:T(8,128)(2,1)S(1)}, bf16[256,1024]{1,0:T(8,128)(2,...) custom-call(s32[4,4]{1,0:T(4,128)S(1)} %copy-done.136, ...), custom_call_target="tpu_custom_call" | custom-call | flops 402653184 | tf_op jit(solution)/shard_map/attend_backward/pallas_call | solution.py:40
  405.8 11.8 %collective-permute-done.66.refs_4_ = bf16[256,1024]{1,0:T(8,128)(2,1)} collective-permute-done((bf16[256,1024]{1,0:T(8,128)(2,1)}, bf16[256,1024]{1,0:T(8,128)(2,1)}, u32[]{:S(2)}, u32[]{:S(2)}) %collective-permute-start.66) | collective-permute-done | bytes 524320 | tf_op jit(solution)/shard_map/ppermute | solution.py:728
  424.8 9.1 %collective-permute-done.68.refs_1_.refs_7_ = bf16[256,1024]{1,0:T(8,128)(2,1)S(1)} collective-permute-done((bf16[256,1024]{1,0:T(8,128)(2,1)S(1)}, bf16[256,1024]{1,0:T(8,128)(2,1)S(1)}, u32[]{:S(2)}, u32[]{:S(2)}) %collective-permute-start.68) | collective-permute-done | bytes 524320 | tf_op jit(solution)/shard_map/ppermute | solution.py:728
  449.4 9.4 %collective-permute-done.73.refs_5_ = bf16[256,1024]{1,0:T(8,128)(2,1)S(1)} collective-permute-done((bf16[256,1024]{1,0:T(8,128)(2,1)S(1)}, bf16[256,1024]{1,0:T(8,128)(2,1)S(1)}, u32[]{:S(2)}, u32[]{:S(2)}) %collective-permute-start.73) | collective-permute-done | bytes 524320 | tf_op jit(solution)/shard_map/ppermute | solution.py:728
  460.6 8.0 %feed_weights.3 = (bf16[4,256,1024]{2,1,0:T(8,128)(2,1)S(1)}, bf16[4,256,1024]{2,1,0:T(8,128)(2,1)}) custom-call(s32[8]{0:T(128)S(1)} %get-tuple-element.465.order_ref, bf16[256,1024]{1,0:T(8,128)(2,1)} %get-tuple-element.306.refs_0_, bf16[256,1024]{1,0:T(8,128)(2,1)} %collective-permute-done.23.refs_1_, bf16[256,1024]{1,0:T(8,128)(2,1)} %collective-permute-done.24.refs_2_, ...), custom_call_target="tpu_custom_call" | custom-call | flops 214748368 | tf_op jit(solution)/shard_map/feed_weights/pallas_call | solution.py:40
  493.8 14.8 %attend_backward.4 = (bf16[1024,768]{1,0:T(8,128)(2,1)S(1)}, f32[2,256]{1,0:T(2,128)S(1)}, bf16[256,1024]{1,0:T(8,128)(2,1)S(1)}, bf16[256,1024]{1,0:T(8,128)(2,...) custom-call(s32[4,4]{1,0:T(4,128)S(1)} %copy-done.135, s32[1024,1]{1,0:T(8,128)S(1)} %copy-done.10, ...), custom_call_target="tpu_custom_call" | custom-call | flops 402653184 | tf_op jit(solution)/shard_map/attend_backward/pallas_call | solution.py:40
  536.2 13.9 %attend_backward.5 = (bf16[1024,768]{1,0:T(8,128)(2,1)S(1)}, f32[2,256]{1,0:T(2,128)S(1)}, bf16[256,1024]{1,0:T(8,128)(2,1)S(1)}, bf16[256,1024]{1,0:T(8,128)(2,...) custom-call(s32[4,4]{1,0:T(4,128)S(1)} %copy-done.134, s32[1024,1]{1,0:T(8,128)S(1)} %copy.59.refs_1_, ...), custom_call_target="tpu_custom_call" | custom-call | flops 402653184 | tf_op jit(solution)/shard_map/attend_backward/pallas_call | solution.py:40
  595.1 5.5 collective-permute-done.92.refs_1_
  608.2 11.3 %collective-permute-done.96.refs_1_ = bf16[128,768]{1,0:T(8,128)(2,1)S(1)} collective-permute-done((bf16[128,768]{1,0:T(8,128)(2,1)S(1)}, bf16[128,768]{1,0:T(8,128)(2,1)S(1)}, u32[]{:S(2)}, u32[]{:S(2)}) %collective-permute-start.96) | collective-permute-done | bytes 196640 | tf_op jit(solution)/shard_map/ppermute | solution.py:728
  642.2 7.3 %collective-permute-start.112 = (bf16[3,128,1024]{2,1,0:T(8,128)(2,1)S(1)}, bf16[3,128,1024]{2,1,0:T(8,128)(2,1)S(1)}, u32[]{:S(2)}, u32[]{:S(2)}) collective-permute-start(bf16[3,128,1024]{2,1,0:T(8,128)(2,1)S(1)} %stack_places.1.one_ref), channel_id=1, source_target_pairs={{0,2},{1,3},{2,0},{3,1},{4,6},{5,7},{6,4},{7,5},{8,10},{9,11},{10,... | collective-permute-start | bytes 2359304 | tf_op jit(solution)/shard_map/ppermute | solution.py:728
  649.7 22.1 %collective-permute-done.108.refs_1_ = bf16[128,768]{1,0:T(8,128)(2,1)S(1)} collective-permute-done((bf16[128,768]{1,0:T(8,128)(2,1)S(1)}, bf16[128,768]{1,0:T(8,128)(2,1)S(1)}, u32[]{:S(2)}, u32[]{:S(2)}) %collective-permute-start.108) | collective-permute-done | bytes 196640 | tf_op jit(solution)/shard_map/ppermute | solution.py:728
  (706 shorter events, 370.8 us)
Async XLA Ops:
  7.2 123.5 %all-gather.6.cloned.1.call-start = ((), (), s32[]{:S(2)}) async-start(), calls=%async_computation.6 | async-start | bytes 2621440 | tf_op jit(solution)/shard_map/all_gather | solution.py:836
  23.0 133.1 %all-gather.4.cloned.1.call-start = ((), (), s32[]{:S(2)}) async-start(), calls=%async_computation.5 | async-start | bytes 1966080 | tf_op jit(solution)/shard_map/all_gather | solution.py:836
  26.1 32.8 %collective-permute-start.9 = (bf16[128,768]{1,0:T(8,128)(2,1)S(1)}, bf16[128,768]{1,0:T(8,128)(2,1)S(1)}, u32[]{:S(2)}, u32[]{:S(2)}) collective-permute-start(bf16[128,768]{1,0:T(8,128)(2,1)S(1)} %copy-done.111), channel_id=1, source_target_pairs={{0,4},{4,0},{8,12},{12,8},{16,20},{20,16},{24,28},{28,24},{1,5},{5... | collective-permute-start | bytes 589832 | tf_op jit(solution)/shard_map/ppermute | solution.py:728
  27.4 48.6 %collective-permute-start.4 = (bf16[256,1024]{1,0:T(8,128)(2,1)S(1)}, bf16[256,1024]{1,0:T(8,128)(2,1)}, u32[]{:S(2)}, u32[]{:S(2)}) collective-permute-start(bf16[256,1024]{1,0:T(8,128)(2,1)S(1)} %bitcast.71), channel_id=1, source_target_pairs={{0,1},{1,0},{2,3},{3,2},{4,5},{5,4},{6,7},{7,6},{8,9},{9,8},{10,11... | collective-permute-start | bytes 1572872 | tf_op jit(solution)/shard_map/ppermute | solution.py:728
  46.0 29.9 %collective-permute-start.5 = (bf16[256,1024]{1,0:T(8,128)(2,1)}, bf16[256,1024]{1,0:T(8,128)(2,1)}, u32[]{:S(2)}, u32[]{:S(2)}) collective-permute-start(bf16[256,1024]{1,0:T(8,128)(2,1)} %collective-permute-done.refs_1_), channel_id=1, source_target_pairs={{0,1},{1,0},{2,3},{3,2},{4,5},{5,4},{6,7},{7,6},{8,9},{9,8},{10,11... | collective-permute-start | bytes 1572872 | tf_op jit(solution)/shard_map/ppermute | solution.py:728
  62.5 28.4 %collective-permute-start.13 = (bf16[96,1024]{1,0:T(8,128)(2,1)S(1)}, bf16[96,1024]{1,0:T(8,128)(2,1)S(1)}, u32[]{:S(2)}, u32[]{:S(2)}) collective-permute-start(bf16[96,1024]{1,0:T(8,128)(2,1)S(1)} %add_dealt.1.refs_0_), channel_id=1, source_target_pairs={{0,8},{4,12},{8,16},{12,20},{16,24},{20,28},{24,0},{28,4},{1,9},{5... | collective-permute-start | bytes 589832 | tf_op jit(solution)/shard_map/ppermute | solution.py:828
  90.8 181.1 %all-gather.8.cloned.1.call-start = ((), (), s32[]{:S(2)}) async-start(), calls=%async_computation.7 | async-start | bytes 2621440 | tf_op jit(solution)/shard_map/all_gather | solution.py:836
  130.7 47.6 %collective-permute-start.26 = (bf16[1024,1024]{1,0:T(8,128)(2,1)}, bf16[1024,1024]{1,0:T(8,128)(2,1)}, u32[]{:S(2)}, u32[]{:S(2)}) collective-permute-start(bf16[1024,1024]{1,0:T(8,128)(2,1)} %all-gather.6.cloned.1.call-done.refs_0_), channel_id=1, source_target_pairs={{0,4},{4,0},{8,12},{12,8},{16,20},{20,16},{24,28},{28,24},{1,5},{5... | collective-permute-start | bytes 6291464 | tf_op jit(solution)/shard_map/ppermute | solution.py:728
  155.0 26.8 %collective-permute-start.24 = (bf16[256,1024]{1,0:T(8,128)(2,1)}, bf16[256,1024]{1,0:T(8,128)(2,1)}, u32[]{:S(2)}, u32[]{:S(2)}) collective-permute-start(bf16[256,1024]{1,0:T(8,128)(2,1)} %get-tuple-element.306.refs_0_), channel_id=1, source_target_pairs={{0,1},{1,0},{2,3},{3,2},{4,5},{5,4},{6,7},{7,6},{8,9},{9,8},{10,11... | collective-permute-start | bytes 1572872 | tf_op jit(solution)/shard_map/ppermute | solution.py:728
  169.3 355.6 %reduce-scatter.10.cloned.1.call-start = ((), (), s32[]{:S(2)}) async-start(), calls=%async_computation.10 | async-start | bytes 2621440 | tf_op jit(solution)/shard_map/reduce_scatter | solution.py:850
  169.8 25.6 %collective-permute-start.30 = (bf16[256,1024]{1,0:T(8,128)(2,1)}, bf16[256,1024]{1,0:T(8,128)(2,1)}, u32[]{:S(2)}, u32[]{:S(2)}) collective-permute-start(bf16[256,1024]{1,0:T(8,128)(2,1)} %bitcast.19.refs_0_), channel_id=1, source_target_pairs={{0,2},{1,3},{2,0},{3,1},{4,6},{5,7},{6,4},{7,5},{8,10},{9,11},{10,... | collective-permute-start | bytes 1572872 | tf_op jit(solution)/shard_map/ppermute | solution.py:728
  195.5 33.6 %collective-permute-start.27 = (bf16[256,1024]{1,0:T(8,128)(2,1)}, bf16[256,1024]{1,0:T(8,128)(2,1)}, u32[]{:S(2)}, u32[]{:S(2)}) collective-permute-start(bf16[256,1024]{1,0:T(8,128)(2,1)} %get-tuple-element.319), channel_id=1, source_target_pairs={{0,1},{1,0},{2,3},{3,2},{4,5},{5,4},{6,7},{7,6},{8,9},{9,8},{10,11... | collective-permute-start | bytes 1572872 | tf_op jit(solution)/shard_map/ppermute | solution.py:728
  197.5 31.7 %collective-permute-start.29 = (bf16[256,1024]{1,0:T(8,128)(2,1)}, bf16[256,1024]{1,0:T(8,128)(2,1)}, u32[]{:S(2)}, u32[]{:S(2)}) collective-permute-start(bf16[256,1024]{1,0:T(8,128)(2,1)} %add_low.22), channel_id=1, source_target_pairs={{0,2},{1,3},{2,0},{3,1},{4,6},{5,7},{6,4},{7,5},{8,10},{9,11},{10,... | collective-permute-start | bytes 1572872 | tf_op jit(solution)/shard_map/ppermute | solution.py:728
  235.0 36.9 %collective-permute-start.43 = (bf16[512,768]{1,0:T(8,128)(2,1)}, bf16[512,768]{1,0:T(8,128)(2,1)}, u32[]{:S(2)}, u32[]{:S(2)}) collective-permute-start(bf16[512,768]{1,0:T(8,128)(2,1)} %part_rows.3.refs_0_), channel_id=1, source_target_pairs={{0,4},{4,0},{8,12},{12,8},{16,20},{20,16},{24,28},{28,24},{1,5},{5... | collective-permute-start | bytes 2359304 | tf_op jit(solution)/shard_map/ppermute | solution.py:728
  271.9 47.4 %collective-permute-start.48 = (bf16[1024,1024]{1,0:T(8,128)(2,1)}, bf16[1024,1024]{1,0:T(8,128)(2,1)S(1)}, u32[]{:S(2)}, u32[]{:S(2)}) collective-permute-start(bf16[1024,1024]{1,0:T(8,128)(2,1)} %all-gather.8.cloned.1.call-done.refs_0_), channel_id=1, source_target_pairs={{0,4},{4,0},{8,12},{12,8},{16,20},{20,16},{24,28},{28,24},{1,5},{5... | collective-permute-start | bytes 6291464 | tf_op jit(solution)/shard_map/ppermute | solution.py:728
  345.6 55.9 %collective-permute-start.64 = (bf16[4,256,1024]{2,1,0:T(8,128)(2,1)S(1)}, bf16[4,256,1024]{2,1,0:T(8,128)(2,1)S(1)}, u32[]{:S(2)}, u32[]{:S(2)}) collective-permute-start(bf16[4,256,1024]{2,1,0:T(8,128)(2,1)S(1)} %get-tuple-element.408), channel_id=1, source_target_pairs={{0,4},{4,0},{8,12},{12,8},{16,20},{20,16},{24,28},{28,24},{1,5},{5... | collective-permute-start | bytes 6291464 | tf_op jit(solution)/shard_map/ppermute | solution.py:728
  403.2 123.6 %reduce-scatter.8.cloned.1.call-start = ((), (), s32[]{:S(2)}) async-start(), calls=%async_computation.9 | async-start | bytes 983040 | tf_op jit(solution)/shard_map/reduce_scatter | solution.py:850
  445.8 28.3 %collective-permute-start.76 = (bf16[4,128,768]{2,1,0:T(8,128)(2,1)S(1)}, bf16[4,128,768]{2,1,0:T(8,128)(2,1)S(1)}, u32[]{:S(2)}, u32[]{:S(2)}) collective-permute-start(bf16[4,128,768]{2,1,0:T(8,128)(2,1)S(1)} %copy-done.150), channel_id=1, source_target_pairs={{0,4},{4,0},{8,12},{12,8},{16,20},{20,16},{24,28},{28,24},{1,5},{5... | collective-permute-start | bytes 2359304 | tf_op jit(solution)/shard_map/ppermute | solution.py:728
  447.0 24.3 %collective-permute-start.74 = (bf16[256,1024]{1,0:T(8,128)(2,1)S(1)}, bf16[256,1024]{1,0:T(8,128)(2,1)S(1)}, u32[]{:S(2)}, u32[]{:S(2)}) collective-permute-start(bf16[256,1024]{1,0:T(8,128)(2,1)S(1)} %get-tuple-element.436), channel_id=1, source_target_pairs={{0,1},{1,0},{2,3},{3,2},{4,5},{5,4},{6,7},{7,6},{8,9},{9,8},{10,11... | collective-permute-start | bytes 1572872 | tf_op jit(solution)/shard_map/ppermute | solution.py:728
  470.0 50.1 %collective-permute-start.83 = (bf16[4,256,1024]{2,1,0:T(8,128)(2,1)}, bf16[4,256,1024]{2,1,0:T(8,128)(2,1)}, u32[]{:S(2)}, u32[]{:S(2)}) collective-permute-start(bf16[4,256,1024]{2,1,0:T(8,128)(2,1)} %get-tuple-element.456), channel_id=1, source_target_pairs={{0,4},{4,0},{8,12},{12,8},{16,20},{20,16},{24,28},{28,24},{1,5},{5... | collective-permute-start | bytes 6291464 | tf_op jit(solution)/shard_map/ppermute | solution.py:728
  475.4 97.7 %reduce-scatter.6.cloned.1.call-start = ((), (), s32[]{:S(2)}) async-start(), calls=%async_computation.8 | async-start | bytes 2621440 | tf_op jit(solution)/shard_map/reduce_scatter | solution.py:850
  485.8 27.6 %collective-permute-start.80 = (bf16[256,1024]{1,0:T(8,128)(2,1)}, bf16[256,1024]{1,0:T(8,128)(2,1)S(1)}, u32[]{:S(2)}, u32[]{:S(2)}) collective-permute-start(bf16[256,1024]{1,0:T(8,128)(2,1)} %copy-done.55), channel_id=1, source_target_pairs={{0,2},{1,3},{2,0},{3,1},{4,6},{5,7},{6,4},{7,5},{8,10},{9,11},{10,... | collective-permute-start | bytes 1572872 | tf_op jit(solution)/shard_map/ppermute | solution.py:728
  485.9 27.9 %collective-permute-start.81 = (bf16[256,1024]{1,0:T(8,128)(2,1)}, bf16[256,1024]{1,0:T(8,128)(2,1)S(1)}, u32[]{:S(2)}, u32[]{:S(2)}) collective-permute-start(bf16[256,1024]{1,0:T(8,128)(2,1)} %copy-done.55), channel_id=1, source_target_pairs={{0,1},{1,0},{2,3},{3,2},{4,5},{5,4},{6,7},{7,6},{8,9},{9,8},{10,11... | collective-permute-start | bytes 1572872 | tf_op jit(solution)/shard_map/ppermute | solution.py:728
  523.5 102.0 %reduce-scatter.14.cloned.1.call-start = ((), (), s32[]{:S(2)}) async-start(), calls=%async_computation.12 | async-start | bytes 1966080 | tf_op jit(solution)/shard_map/reduce_scatter | solution.py:850
  523.9 36.0 %collective-permute-start.86 = (bf16[4,256,768]{2,1,0:T(8,128)(2,1)}, bf16[4,256,768]{2,1,0:T(8,128)(2,1)}, u32[]{:S(2)}, u32[]{:S(2)}) collective-permute-start(bf16[4,256,768]{2,1,0:T(8,128)(2,1)} %copy-done.148), channel_id=1, source_target_pairs={{0,4},{4,0},{8,12},{12,8},{16,20},{20,16},{24,28},{28,24},{1,5},{5... | collective-permute-start | bytes 4718600 | tf_op jit(solution)/shard_map/ppermute | solution.py:728
  562.9 122.1 %reduce-scatter.12.cloned.1.call-start = ((), (), s32[]{:S(2)}) async-start(), calls=%async_computation.11 | async-start | bytes 983040 | tf_op jit(solution)/shard_map/reduce_scatter | solution.py:850
  564.3 28.5 %collective-permute-start.91 = (bf16[4,128,768]{2,1,0:T(8,128)(2,1)}, bf16[4,128,768]{2,1,0:T(8,128)(2,1)}, u32[]{:S(2)}, u32[]{:S(2)}) collective-permute-start(bf16[4,128,768]{2,1,0:T(8,128)(2,1)} %copy-done.151), channel_id=1, source_target_pairs={{0,4},{4,0},{8,12},{12,8},{16,20},{20,16},{24,28},{28,24},{1,5},{5... | collective-permute-start | bytes 2359304 | tf_op jit(solution)/shard_map/ppermute | solution.py:728
  567.5 33.1 %collective-permute-start.92 = (bf16[256,1024]{1,0:T(8,128)(2,1)S(1)}, bf16[256,1024]{1,0:T(8,128)(2,1)}, u32[]{:S(2)}, u32[]{:S(2)}) collective-permute-start(bf16[256,1024]{1,0:T(8,128)(2,1)S(1)} %copy-done.38), channel_id=1, source_target_pairs={{0,2},{1,3},{2,0},{3,1},{4,6},{5,7},{6,4},{7,5},{8,10},{9,11},{10,... | collective-permute-start | bytes 1572872 | tf_op jit(solution)/shard_map/ppermute | solution.py:728
  578.1 26.4 %collective-permute-start.93 = (bf16[256,1024]{1,0:T(8,128)(2,1)S(1)}, bf16[256,1024]{1,0:T(8,128)(2,1)}, u32[]{:S(2)}, u32[]{:S(2)}) collective-permute-start(bf16[256,1024]{1,0:T(8,128)(2,1)S(1)} %copy-done.38), channel_id=1, source_target_pairs={{0,1},{1,0},{2,3},{3,2},{4,5},{5,4},{6,7},{7,6},{8,9},{9,8},{10,11... | collective-permute-start | bytes 1572872 | tf_op jit(solution)/shard_map/ppermute | solution.py:728
  601.8 24.8 %collective-permute-start.100 = (bf16[256,1024]{1,0:T(8,128)(2,1)S(1)}, bf16[256,1024]{1,0:T(8,128)(2,1)S(1)}, u32[]{:S(2)}, u32[]{:S(2)}) collective-permute-start(bf16[256,1024]{1,0:T(8,128)(2,1)S(1)} %add_low.38.refs_0_), channel_id=1, source_target_pairs={{0,2},{1,3},{2,0},{3,1},{4,6},{5,7},{6,4},{7,5},{8,10},{9,11},{10,... | collective-permute-start | bytes 1572872 | tf_op jit(solution)/shard_map/ppermute | solution.py:728
  642.2 38.2 %collective-permute-start.112 = (bf16[3,128,1024]{2,1,0:T(8,128)(2,1)S(1)}, bf16[3,128,1024]{2,1,0:T(8,128)(2,1)S(1)}, u32[]{:S(2)}, u32[]{:S(2)}) collective-permute-start(bf16[3,128,1024]{2,1,0:T(8,128)(2,1)S(1)} %stack_places.1.one_ref), channel_id=1, source_target_pairs={{0,2},{1,3},{2,0},{3,1},{4,6},{5,7},{6,4},{7,5},{8,10},{9,11},{10,... | collective-permute-start | bytes 2359304 | tf_op jit(solution)/shard_map/ppermute | solution.py:728
  649.6 24.6 %collective-permute-start.109 = (bf16[128,768]{1,0:T(8,128)(2,1)S(1)}, bf16[128,768]{1,0:T(8,128)(2,1)S(1)}, u32[]{:S(2)}, u32[]{:S(2)}) collective-permute-start(bf16[128,768]{1,0:T(8,128)(2,1)S(1)} %get-tuple-element.498.refs_0_), channel_id=1, source_target_pairs={{0,1},{1,0},{2,3},{3,2},{4,5},{5,4},{6,7},{7,6},{8,9},{9,8},{10,11... | collective-permute-start | bytes 589832 | tf_op jit(solution)/shard_map/ppermute | solution.py:728
  (262 other events, 2097.6 us)
Sparse Core Ops, SparseCore 0:
  23.1 62.8 all-gather.5
  91.0 45.6 all-gather.3
  169.4 45.7 all-gather.7
  403.4 50.3 reduce-scatter.9
  475.3 30.9 reduce-scatter.7
  523.6 49.4 reduce-scatter.5
  576.0 34.5 reduce-scatter.13
  649.7 22.6 reduce-scatter.11

commit v5 on v4

--- a/solution.py
+++ b/solution.py
@@ -1090,7 +1090,7 @@
         whole_rows = shards * rows
         dealt = add_dealt(deals[0], sent, (place == me).astype(jnp.int32)[None])
         leave_relay = Relay(dealt)
-        feed_line = gather_line(hold(feed_zero))
+        rest_line = gather_line(hold(entry_rest))
         source_pieces = source_spread.finish()
         encoder_entry = assemble(
             entry_relay.pieces(), (relayed * rows)[None], [(0, rows, whole_rows)], rows
@@ -1115,29 +1115,43 @@
     target_pieces = target_spread.finish()
     if quick():
         leave_relay.touch()
-        rest_line = gather_line(hold(entry_rest))
+        feed_line = gather_line(hold(feed_zero))
+        one_line = part_rows(rest_line, 2 * rows, 0, rows)
+        two_line = part_rows(rest_line, 2 * rows, rows, rows)
         leaves = assemble(
             leave_relay.pieces(),
             jnp.stack([((relayed % 2) * 4 + relayed // 2) * piece] * 3),
             [(i * piece, piece, shards * piece) for i in range(3)],
             3 * piece,
         )
-        feed_other = to_side(hold(feed_line))
+        one_other = to_side(hold(one_line))
     encoder_partials = Collect(project_out(mixture, leaves[0], count))
     encoder_partials.turn()
+    if quick():
+        decoder_entry = assemble(
+            [one_line, one_other], entry_table, [(0, rows, whole_rows)], rows
+        )[0]
+    decoder_normed, *projected = project_self(
+        target_pieces, gain(2), shift(2), decoder_entry, entry_biases[1]
+    )
+    if quick():
+        feed_other = to_side(hold(feed_line))
+        last_line = gather_line(hold(feed_one))
+    mixture, total = attend_forward(*self_view, *projected, heads, True)
+    decoder_stored = (*projected, mixture, total)
+    middle, middle_normed = residual_norm(
+        source_tokens, encoder_partials.finish(), exit_bias(0), gain(1), shift(1)
+    )
+    middle_spread = Spread(middle_normed)
+    decoder_partials = Collect(project_out(mixture, leaves[1], count))
+    decoder_partials.turn()
     target_incoming, target_incoming_low, target_sum = join_gradient(
         target_cotangent, target_keep, []
     )
-    if quick():
-        last_line = gather_line(hold(feed_one))
-    middle, middle_normed = residual_norm(
-        source_tokens, encoder_partials.finish(), exit_bias(0), gain(1), shift(1)
-    )
-    middle_spread = Spread(middle_normed)
-    if quick():
-        one_line = part_rows(rest_line, 2 * rows, 0, rows)
-        two_line = part_rows(rest_line, 2 * rows, rows, rows)
-        one_other = to_side(one_line)
+    self_out, self_normed = residual_norm(
+        target_tokens, decoder_partials.finish(), exit_bias(1), gain(3), shift(3)
+    )
+    self_spread = Spread(self_normed)
     middle_pieces = middle_spread.finish()
     if quick():
         expand, reduce = [None, None], [None, None]
@@ -1145,37 +1159,22 @@
         feed_table = jnp.stack([order * rows, order * feed_rows])
         height = rows + feed_rows
         expand[0], reduce[0] = assemble([feed_line, feed_other], feed_table, feed_parts, height)
+        two_other = to_side(hold(two_line))
     encoder_active, encoder_slope, partials = feed_forward(
         middle_pieces, expand[0], reduce[0], hidden_biases[0]
     )
     memory_partials = Collect(partials)
     memory_partials.turn()
-    if quick():
-        decoder_entry = assemble(
-            [one_line, one_other], entry_table, [(0, rows, whole_rows)], rows
-        )[0]
-        two_other = to_side(hold(two_line))
-    decoder_normed, *projected = project_self(
-        target_pieces, gain(2), shift(2), decoder_entry, entry_biases[1]
-    )
-    mixture, total = attend_forward(*self_view, *projected, heads, True)
-    decoder_stored = (*projected, mixture, total)
-    memory_low = residual_low(middle, memory_partials.finish(), reducer_biases[0:1])
-    memory_spread = Spread(memory_low)
-    decoder_partials = Collect(project_out(mixture, leaves[1], count))
-    decoder_partials.turn()
-    if quick():
-        last_other = to_side(hold(last_line))
-    self_out, self_normed = residual_norm(
-        target_tokens, decoder_partials.finish(), exit_bias(1), gain(3), shift(3)
-    )
-    self_spread = Spread(self_normed)
-    memory_pieces = memory_spread.finish()
-    self_pieces = self_spread.finish()
     if quick():
         cross_entry = assemble(
             [two_line, two_other], entry_table, [(0, rows, whole_rows)], rows
         )[0]
+    memory_low = residual_low(middle, memory_partials.finish(), reducer_biases[0:1])
+    memory_spread = Spread(memory_low)
+    if quick():
+        last_other = to_side(hold(last_line))
+    memory_pieces = memory_spread.finish()
+    self_pieces = self_spread.finish()
     target_incoming_spread = Spread(hold(target_incoming_low))
     cross_projected = project_cross(self_pieces, memory_pieces, cross_entry, entry_biases[2])
     mixture, total = attend_forward(*cross_view, *cross_projected, heads, False)
@@ -1247,14 +1246,14 @@
             "attention_weights",
         )
     )
-    if quick():
-        decoder_feed_shares.turn()
     source_incoming, source_incoming_low, source_sum = join_gradient(
         source_cotangent, source_keep, memory_partials.finish()
     )
     source_incoming_spread = Spread(source_incoming_low)
     partials.turn()
     source_incoming_pieces = source_incoming_spread.finish()
+    if quick():
+        decoder_feed_shares.turn()
     hidden, encoder_hidden_sum, feed_partials = feed_backward(
         source_incoming_pieces, expand[0], reduce[0], encoder_slope
     )

time: 715 us -> 703 us (0.983)
  waiting for transfers between devices: 288 us -> 273 us
    ppermute x105, waiting for transfers between devices: 248 us -> 218 us  [swap(): lax.ppermute(values, axis, [(i, i ^ bit) for i in range(lax.axis_size(axi...]
    ppermute x6, waiting for transfers between devices: 29.2 us -> 44.8 us  [touch(): self.line.append(lax.ppermute(newest, 'batch', pairs))]
    ppermute x105, starting transfers between devices: 99.9 us -> 89 us  [swap(): lax.ppermute(values, axis, [(i, i ^ bit) for i in range(lax.axis_size(axi...]
    ppermute x3, starting transfers between devices: 5.65 us -> 13.6 us  [__init__(): lax.ppermute(pieces, ('batch', 'seq'), line_pairs(step, 4, True))]
    unnamed x338 -> x364, local copies, waits for them, and re-layouts: 81.7 us -> 83.7 us
  transfers between devices with their start and end apart: 125 -> 125, of which waited for: 52 -> 52; matrix products, arithmetic and copies ran while one was open for 2% -> 1% of each run, Pallas kernels for 26% -> 27%
where the time goes in v5:
time: 703 us; the launch traced here: 696 us
  waiting for transfers between devices  273 us (39%)
  Pallas kernels  203 us (29%)
  starting transfers between devices  110 us (16%)
  local copies, waits for them, and re-layouts  89 us (13%)
  between operations  16.6 us (2%)
    ppermute x105, waiting for transfers between devices, swap(): lax.ppermute(values, axis, [(i, i ^ bit) for i in range(lax.axis_size(axi...  218 us
    pallas_call x79, Pallas kernels, take_turn(): results = call(*args)  190 us
    ppermute x105, starting transfers between devices, swap(): lax.ppermute(values, axis, [(i, i ^ bit) for i in range(lax.axis_size(axi...  89 us
    unnamed x364, local copies, waits for them, and re-layouts  83.7 us
    ppermute x6, waiting for transfers between devices, touch(): self.line.append(lax.ppermute(newest, 'batch', pairs))  44.8 us
  transfers between devices with their start and end apart: 125, of which 52 were waited for; matrix products, arithmetic and copies ran while one was open for 1% of the time, Pallas kernels for 27%

profile of v5, /device:TPU:1, one launch (start us, length us, event | category | flops | bytes accessed | tf_op | source)
XLA Modules:
  0.0 696.3 jit_solution(12442516609222821372)
XLA Ops:
  27.4 6.1 collective-permute-start.4
  41.9 6.6 collective-permute-done.7.refs_2_
  49.9 11.3 %collective-permute-done.8.refs_3_ = bf16[128,768]{1,0:T(8,128)(2,1)S(1)} collective-permute-done((bf16[128,768]{1,0:T(8,128)(2,1)S(1)}, bf16[128,768]{1,0:T(8,128)(2,1)S(1)}, u32[]{:S(2)}, u32[]{:S(2)}) %collective-permute-start.8) | collective-permute-done | bytes 196640 | tf_op jit(solution)/shard_map/ppermute | solution.py:828
  78.2 9.4 %attend_forward.3 = (bf16[1024,256]{1,0:T(8,128)(2,1)S(1)}, f32[8,1024]{1,0:T(8,128)S(1)}) custom-call(s32[4,4]{1,0:T(4,128)S(1)} %get-tuple-element.464.refs_0_, s32[1024,1]{1,0:T(8,128)S(1)} %copy.59.refs_1_, s32[1,1024]{1,0:T(1,128)S(1)} %bitcast.101, s32[1024,1]{1,0:T(8,128)S(1)} %copy.60.refs_3_, s32[1,1024]{1,0:T(1,128)S(1)} %bitcast.86, ...), custom_call_target="tpu_custom_call" | custom-call | flops 107374184 | tf_op jit(solution)/shard_map/attend_forward/pallas_call | solution.py:40
  89.0 6.3 collective-permute-done.13.refs_1_
  95.3 11.0 %collective-permute-done.14.refs_2_ = bf16[96,1024]{1,0:T(8,128)(2,1)} collective-permute-done((bf16[96,1024]{1,0:T(8,128)(2,1)S(1)}, bf16[96,1024]{1,0:T(8,128)(2,1)}, u32[]{:S(2)}, u32[]{:S(2)}) %collective-permute-start.14) | collective-permute-done | bytes 196640 | tf_op jit(solution)/shard_map/ppermute | solution.py:828
  108.1 9.6 %collective-permute-done.15.refs_3_ = bf16[96,1024]{1,0:T(8,128)(2,1)} collective-permute-done((bf16[96,1024]{1,0:T(8,128)(2,1)}, bf16[96,1024]{1,0:T(8,128)(2,1)}, u32[]{:S(2)}, u32[]{:S(2)}) %collective-permute-start.15) | collective-permute-done | bytes 196640 | tf_op jit(solution)/shard_map/ppermute | solution.py:828
  157.2 6.8 attend_forward.4
  170.9 5.6 collective-permute-start.29
  187.0 7.9 %collective-permute-done.30.refs_3_ = bf16[256,1024]{1,0:T(8,128)(2,1)} collective-permute-done((bf16[256,1024]{1,0:T(8,128)(2,1)}, bf16[256,1024]{1,0:T(8,128)(2,1)}, u32[]{:S(2)}, u32[]{:S(2)}) %collective-permute-start.30) | collective-permute-done | bytes 524320 | tf_op jit(solution)/shard_map/ppermute | solution.py:728
  200.5 5.6 collective-permute-done.27.refs_1_
  211.0 8.8 %feed_forward.2 = (bf16[1024,1024]{1,0:T(8,128)(2,1)S(1)}, bf16[1024,1024]{1,0:T(8,128)(2,1)S(1)}, bf16[256,1024]{1,0:T(8,128)(2,1)S(1)}, bf16[256,1024]{1,0:T(8...) custom-call(bf16[256,1024]{1,0:T(8,128)(2,1)S(1)} %copy-done.87, ...), custom_call_target="tpu_custom_call" | custom-call | flops 214748368 | tf_op jit(solution)/shard_map/feed_forward/pallas_call | solution.py:40
  224.8 15.2 %collective-permute-done.37.refs_1_ = bf16[512,768]{1,0:T(8,128)(2,1)S(1)} collective-permute-done((bf16[512,768]{1,0:T(8,128)(2,1)S(1)}, bf16[512,768]{1,0:T(8,128)(2,1)S(1)}, u32[]{:S(2)}, u32[]{:S(2)}) %collective-permute-start.37) | collective-permute-done | bytes 786464 | tf_op jit(solution)/shard_map/ppermute | solution.py:728
  249.5 9.7 %collective-permute-done.41.refs_5_.refs_6_ = bf16[256,1024]{1,0:T(8,128)(2,1)} collective-permute-done((bf16[256,1024]{1,0:T(8,128)(2,1)}, bf16[256,1024]{1,0:T(8,128)(2,1)}, u32[]{:S(2)}, u32[]{:S(2)}) %collective-permute-start.41) | collective-permute-done | bytes 524320 | tf_op jit(solution)/shard_map/ppermute | solution.py:728
  268.4 7.3 %attend_forward.5 = (bf16[1024,256]{1,0:T(8,128)(2,1)S(1)}, f32[8,1024]{1,0:T(8,128)S(1)}) custom-call(s32[4,4]{1,0:T(4,128)S(1)} %copy-done.151, s32[1024,1]{1,0:T(8,128)S(1)} %copy.59.refs_1_, s32[1,1024]{1,0:T(1,128)S(1)} %bitcast.95, s32[1024,1]{1,0:T(8,128)S(1)} %copy.60.refs_3_, s32[1,1024]{1,0:T(1,128)S(1)} %bitcast.88, ...), custom_call_target="tpu_custom_call" | custom-call | flops 107374184 | tf_op jit(solution)/shard_map/attend_forward/pallas_call | solution.py:40
  279.1 12.6 %collective-permute-done.46.refs_3_ = bf16[256,1024]{1,0:T(8,128)(2,1)S(1)} collective-permute-done((bf16[256,1024]{1,0:T(8,128)(2,1)S(1)}, bf16[256,1024]{1,0:T(8,128)(2,1)S(1)}, u32[]{:S(2)}, u32[]{:S(2)}) %collective-permute-start.46) | collective-permute-done | bytes 524320 | tf_op jit(solution)/shard_map/ppermute | solution.py:728
  295.6 12.1 %collective-permute-done.48.refs_1_ = bf16[1024,1024]{1,0:T(8,128)(2,1)S(1)} collective-permute-done((bf16[1024,1024]{1,0:T(8,128)(2,1)}, bf16[1024,1024]{1,0:T(8,128)(2,1)S(1)}, u32[]{:S(2)}, u32[]{:S(2)}) %collective-permute-start.48) | collective-permute-done | bytes 2097184 | tf_op jit(solution)/shard_map/ppermute | solution.py:728
  309.5 6.4 collective-permute-done.52.refs_1_.refs_7_
  317.9 6.1 feed_forward.3
  333.3 6.8 feed_weights.2
  348.4 7.4 %collective-permute-done.57.refs_3_ = bf16[256,1024]{1,0:T(8,128)(2,1)S(1)} collective-permute-done((bf16[256,1024]{1,0:T(8,128)(2,1)S(1)}, bf16[256,1024]{1,0:T(8,128)(2,1)S(1)}, u32[]{:S(2)}, u32[]{:S(2)}) %collective-permute-start.57) | collective-permute-done | bytes 524320 | tf_op jit(solution)/shard_map/ppermute | solution.py:728
  356.9 10.2 %collective-permute-done.60.refs_6_.refs_2_ = bf16[256,1024]{1,0:T(8,128)(2,1)S(1)} collective-permute-done((bf16[256,1024]{1,0:T(8,128)(2,1)S(1)}, bf16[256,1024]{1,0:T(8,128)(2,1)S(1)}, u32[]{:S(2)}, u32[]{:S(2)}) %collective-permute-start.60) | collective-permute-done | bytes 524320 | tf_op jit(solution)/shard_map/ppermute | solution.py:728
  369.4 14.5 %attend_backward.3 = (bf16[1024,768]{1,0:T(8,128)(2,1)S(1)}, f32[2,256]{1,0:T(2,128)S(1)}, bf16[256,1024]{1,0:T(8,128)(2,1)S(1)}, bf16[256,1024]{1,0:T(8,128)(2,...) custom-call(s32[4,4]{1,0:T(4,128)S(1)} %copy-done.151, ...), custom_call_target="tpu_custom_call" | custom-call | flops 402653184 | tf_op jit(solution)/shard_map/attend_backward/pallas_call | solution.py:40
  413.7 10.9 %collective-permute-done.68.refs_1_.refs_7_ = bf16[256,1024]{1,0:T(8,128)(2,1)S(1)} collective-permute-done((bf16[256,1024]{1,0:T(8,128)(2,1)}, bf16[256,1024]{1,0:T(8,128)(2,1)S(1)}, u32[]{:S(2)}, u32[]{:S(2)}) %collective-permute-start.68) | collective-permute-done | bytes 524320 | tf_op jit(solution)/shard_map/ppermute | solution.py:728
  441.8 10.8 %collective-permute-done.73.refs_5_ = bf16[256,1024]{1,0:T(8,128)(2,1)S(1)} collective-permute-done((bf16[256,1024]{1,0:T(8,128)(2,1)S(1)}, bf16[256,1024]{1,0:T(8,128)(2,1)S(1)}, u32[]{:S(2)}, u32[]{:S(2)}) %collective-permute-start.73) | collective-permute-done | bytes 524320 | tf_op jit(solution)/shard_map/ppermute | solution.py:728
  454.4 7.9 %feed_weights.3 = (bf16[4,256,1024]{2,1,0:T(8,128)(2,1)S(1)}, bf16[4,256,1024]{2,1,0:T(8,128)(2,1)}) custom-call(s32[8]{0:T(128)S(1)} %get-tuple-element.467.order_ref, bf16[256,1024]{1,0:T(8,128)(2,1)S(1)} %copy-done.88, bf16[256,1024]{1,0:T(8,128)(2,1)} %collective-permute-done.27.refs_1_, bf16[256,1024]{1,0:T(8,128)(2,1)} %collective-permute-done.31.refs_2_, ...), custom_call_target="tpu_custom_call" | custom-call | flops 214748368 | tf_op jit(solution)/shard_map/feed_weights/pallas_call | solution.py:40
  486.3 14.8 %attend_backward.4 = (bf16[1024,768]{1,0:T(8,128)(2,1)S(1)}, f32[2,256]{1,0:T(2,128)S(1)}, bf16[256,1024]{1,0:T(8,128)(2,1)S(1)}, bf16[256,1024]{1,0:T(8,128)(2,...) custom-call(s32[4,4]{1,0:T(4,128)S(1)} %copy-done.150, s32[1024,1]{1,0:T(8,128)S(1)} %copy-done.13, ...), custom_call_target="tpu_custom_call" | custom-call | flops 402653184 | tf_op jit(solution)/shard_map/attend_backward/pallas_call | solution.py:40
  527.3 18.8 %attend_backward.5 = (bf16[1024,768]{1,0:T(8,128)(2,1)S(1)}, f32[2,256]{1,0:T(2,128)S(1)}, bf16[256,1024]{1,0:T(8,128)(2,1)S(1)}, bf16[256,1024]{1,0:T(8,128)(2,...) custom-call(s32[4,4]{1,0:T(4,128)S(1)} %copy-done.149, s32[1024,1]{1,0:T(8,128)S(1)} %copy.59.refs_1_, ...), custom_call_target="tpu_custom_call" | custom-call | flops 402653184 | tf_op jit(solution)/shard_map/attend_backward/pallas_call | solution.py:40
  585.9 5.6 collective-permute-done.92.refs_1_
  598.6 11.5 %collective-permute-done.96.refs_1_ = bf16[128,768]{1,0:T(8,128)(2,1)S(1)} collective-permute-done((bf16[128,768]{1,0:T(8,128)(2,1)S(1)}, bf16[128,768]{1,0:T(8,128)(2,1)S(1)}, u32[]{:S(2)}, u32[]{:S(2)}) %collective-permute-start.96) | collective-permute-done | bytes 196640 | tf_op jit(solution)/shard_map/ppermute | solution.py:728
  620.8 12.3 %collective-permute-start.107 = (bf16[96,1024]{1,0:T(8,128)(2,1)S(1)}, bf16[96,1024]{1,0:T(8,128)(2,1)S(1)}, u32[]{:S(2)}, u32[]{:S(2)}) collective-permute-start(bf16[96,1024]{1,0:T(8,128)(2,1)S(1)} %get-tuple-element.509.refs_0_), channel_id=1, source_target_pairs={{24,0},{28,4},{1,9},{5,13},{10,18},{14,22},{19,27},{23,31}} | collective-permute-start | bytes 589832 | tf_op jit(solution)/shard_map/ppermute | solution.py:899
  642.3 20.6 %collective-permute-done.108.refs_1_ = bf16[128,768]{1,0:T(8,128)(2,1)S(1)} collective-permute-done((bf16[128,768]{1,0:T(8,128)(2,1)S(1)}, bf16[128,768]{1,0:T(8,128)(2,1)S(1)}, u32[]{:S(2)}, u32[]{:S(2)}) %collective-permute-start.108) | collective-permute-done | bytes 196640 | tf_op jit(solution)/shard_map/ppermute | solution.py:728
  (732 shorter events, 363.5 us)
Async XLA Ops:
  7.2 111.8 %all-gather.4.cloned.1.call-start = ((), (), s32[]{:S(2)}) async-start(), calls=%async_computation.5 | async-start | bytes 1966080 | tf_op jit(solution)/shard_map/all_gather | solution.py:836
  23.1 126.8 %all-gather.6.cloned.1.call-start = ((), (), s32[]{:S(2)}) async-start(), calls=%async_computation.6 | async-start | bytes 2621440 | tf_op jit(solution)/shard_map/all_gather | solution.py:836
  26.2 35.0 %collective-permute-start.9 = (bf16[128,768]{1,0:T(8,128)(2,1)S(1)}, bf16[128,768]{1,0:T(8,128)(2,1)S(1)}, u32[]{:S(2)}, u32[]{:S(2)}) collective-permute-start(bf16[128,768]{1,0:T(8,128)(2,1)S(1)} %copy-done.137), channel_id=1, source_target_pairs={{0,4},{4,0},{8,12},{12,8},{16,20},{20,16},{24,28},{28,24},{1,5},{5... | collective-permute-start | bytes 589832 | tf_op jit(solution)/shard_map/ppermute | solution.py:728
  27.4 45.7 %collective-permute-start.4 = (bf16[256,1024]{1,0:T(8,128)(2,1)S(1)}, bf16[256,1024]{1,0:T(8,128)(2,1)}, u32[]{:S(2)}, u32[]{:S(2)}) collective-permute-start(bf16[256,1024]{1,0:T(8,128)(2,1)S(1)} %bitcast.76), channel_id=1, source_target_pairs={{0,1},{1,0},{2,3},{3,2},{4,5},{5,4},{6,7},{7,6},{8,9},{9,8},{10,11... | collective-permute-start | bytes 1572872 | tf_op jit(solution)/shard_map/ppermute | solution.py:728
  36.8 36.3 %collective-permute-start.5 = (bf16[256,1024]{1,0:T(8,128)(2,1)}, bf16[256,1024]{1,0:T(8,128)(2,1)S(1)}, u32[]{:S(2)}, u32[]{:S(2)}) collective-permute-start(bf16[256,1024]{1,0:T(8,128)(2,1)} %collective-permute-done.refs_1_), channel_id=1, source_target_pairs={{0,1},{1,0},{2,3},{3,2},{4,5},{5,4},{6,7},{7,6},{8,9},{9,8},{10,11... | collective-permute-start | bytes 1572872 | tf_op jit(solution)/shard_map/ppermute | solution.py:728
  88.9 171.3 %all-gather.8.cloned.1.call-start = ((), (), s32[]{:S(2)}) async-start(), calls=%async_computation.7 | async-start | bytes 2621440 | tf_op jit(solution)/shard_map/all_gather | solution.py:836
  106.4 27.9 %collective-permute-start.23 = (bf16[256,1024]{1,0:T(8,128)(2,1)}, bf16[256,1024]{1,0:T(8,128)(2,1)}, u32[]{:S(2)}, u32[]{:S(2)}) collective-permute-start(bf16[256,1024]{1,0:T(8,128)(2,1)} %bitcast.70), channel_id=1, source_target_pairs={{0,2},{1,3},{2,0},{3,1},{4,6},{5,7},{6,4},{7,5},{8,10},{9,11},{10,... | collective-permute-start | bytes 1572872 | tf_op jit(solution)/shard_map/ppermute | solution.py:728
  134.8 29.2 %collective-permute-start.20 = (bf16[256,1024]{1,0:T(8,128)(2,1)}, bf16[256,1024]{1,0:T(8,128)(2,1)}, u32[]{:S(2)}, u32[]{:S(2)}) collective-permute-start(bf16[256,1024]{1,0:T(8,128)(2,1)} %get-tuple-element.302), channel_id=1, source_target_pairs={{0,1},{1,0},{2,3},{3,2},{4,5},{5,4},{6,7},{7,6},{8,9},{9,8},{10,11... | collective-permute-start | bytes 1572872 | tf_op jit(solution)/shard_map/ppermute | solution.py:728
  136.7 27.4 %collective-permute-start.22 = (bf16[256,1024]{1,0:T(8,128)(2,1)}, bf16[256,1024]{1,0:T(8,128)(2,1)}, u32[]{:S(2)}, u32[]{:S(2)}) collective-permute-start(bf16[256,1024]{1,0:T(8,128)(2,1)} %add_low.21), channel_id=1, source_target_pairs={{0,2},{1,3},{2,0},{3,1},{4,6},{5,7},{6,4},{7,5},{8,10},{9,11},{10,... | collective-permute-start | bytes 1572872 | tf_op jit(solution)/shard_map/ppermute | solution.py:728
  149.9 57.5 %collective-permute-start.33 = (bf16[1024,1024]{1,0:T(8,128)(2,1)}, bf16[1024,1024]{1,0:T(8,128)(2,1)}, u32[]{:S(2)}, u32[]{:S(2)}) collective-permute-start(bf16[1024,1024]{1,0:T(8,128)(2,1)} %all-gather.6.cloned.1.call-done.refs_0_), channel_id=1, source_target_pairs={{0,4},{4,0},{8,12},{12,8},{16,20},{20,16},{24,28},{28,24},{1,5},{5... | collective-permute-start | bytes 6291464 | tf_op jit(solution)/shard_map/ppermute | solution.py:728
  176.5 339.5 %reduce-scatter.10.cloned.1.call-start = ((), (), s32[]{:S(2)}) async-start(), calls=%async_computation.10 | async-start | bytes 2621440 | tf_op jit(solution)/shard_map/reduce_scatter | solution.py:850
  181.4 24.7 %collective-permute-start.27 = (bf16[256,1024]{1,0:T(8,128)(2,1)}, bf16[256,1024]{1,0:T(8,128)(2,1)}, u32[]{:S(2)}, u32[]{:S(2)}) collective-permute-start(bf16[256,1024]{1,0:T(8,128)(2,1)} %copy-done.86), channel_id=1, source_target_pairs={{0,2},{1,3},{2,0},{3,1},{4,6},{5,7},{6,4},{7,5},{8,10},{9,11},{10,... | collective-permute-start | bytes 1572872 | tf_op jit(solution)/shard_map/ppermute | solution.py:728
  182.9 28.1 %collective-permute-start.31 = (bf16[256,1024]{1,0:T(8,128)(2,1)}, bf16[256,1024]{1,0:T(8,128)(2,1)}, u32[]{:S(2)}, u32[]{:S(2)}) collective-permute-start(bf16[256,1024]{1,0:T(8,128)(2,1)} %copy-done.86), channel_id=1, source_target_pairs={{0,1},{1,0},{2,3},{3,2},{4,5},{5,4},{6,7},{7,6},{8,9},{9,8},{10,11... | collective-permute-start | bytes 1572872 | tf_op jit(solution)/shard_map/ppermute | solution.py:728
  223.3 24.7 %collective-permute-start.38 = (bf16[256,1024]{1,0:T(8,128)(2,1)}, bf16[256,1024]{1,0:T(8,128)(2,1)}, u32[]{:S(2)}, u32[]{:S(2)}) collective-permute-start(bf16[256,1024]{1,0:T(8,128)(2,1)} %get-tuple-element.347.refs_0_), channel_id=1, source_target_pairs={{0,2},{1,3},{2,0},{3,1},{4,6},{5,7},{6,4},{7,5},{8,10},{9,11},{10,... | collective-permute-start | bytes 1572872 | tf_op jit(solution)/shard_map/ppermute | solution.py:728
  260.2 47.5 %collective-permute-start.48 = (bf16[1024,1024]{1,0:T(8,128)(2,1)}, bf16[1024,1024]{1,0:T(8,128)(2,1)S(1)}, u32[]{:S(2)}, u32[]{:S(2)}) collective-permute-start(bf16[1024,1024]{1,0:T(8,128)(2,1)} %all-gather.8.cloned.1.call-done.refs_0_), channel_id=1, source_target_pairs={{0,4},{4,0},{8,12},{12,8},{16,20},{20,16},{24,28},{28,24},{1,5},{5... | collective-permute-start | bytes 6291464 | tf_op jit(solution)/shard_map/ppermute | solution.py:728
  346.4 61.8 %collective-permute-start.67 = (bf16[4,256,1024]{2,1,0:T(8,128)(2,1)}, bf16[4,256,1024]{2,1,0:T(8,128)(2,1)}, u32[]{:S(2)}, u32[]{:S(2)}) collective-permute-start(bf16[4,256,1024]{2,1,0:T(8,128)(2,1)} %get-tuple-element.418), channel_id=1, source_target_pairs={{0,4},{4,0},{8,12},{12,8},{16,20},{20,16},{24,28},{28,24},{1,5},{5... | collective-permute-start | bytes 6291464 | tf_op jit(solution)/shard_map/ppermute | solution.py:728
  411.7 106.2 %reduce-scatter.8.cloned.1.call-start = ((), (), s32[]{:S(2)}) async-start(), calls=%async_computation.9 | async-start | bytes 983040 | tf_op jit(solution)/shard_map/reduce_scatter | solution.py:850
  439.5 27.1 %collective-permute-start.76 = (bf16[4,128,768]{2,1,0:T(8,128)(2,1)S(1)}, bf16[4,128,768]{2,1,0:T(8,128)(2,1)S(1)}, u32[]{:S(2)}, u32[]{:S(2)}) collective-permute-start(bf16[4,128,768]{2,1,0:T(8,128)(2,1)S(1)} %copy-done.162), channel_id=1, source_target_pairs={{0,4},{4,0},{8,12},{12,8},{16,20},{20,16},{24,28},{28,24},{1,5},{5... | collective-permute-start | bytes 2359304 | tf_op jit(solution)/shard_map/ppermute | solution.py:728
  439.5 24.3 %collective-permute-start.74 = (bf16[256,1024]{1,0:T(8,128)(2,1)S(1)}, bf16[256,1024]{1,0:T(8,128)(2,1)S(1)}, u32[]{:S(2)}, u32[]{:S(2)}) collective-permute-start(bf16[256,1024]{1,0:T(8,128)(2,1)S(1)} %get-tuple-element.438), channel_id=1, source_target_pairs={{0,1},{1,0},{2,3},{3,2},{4,5},{5,4},{6,7},{7,6},{8,9},{9,8},{10,11... | collective-permute-start | bytes 1572872 | tf_op jit(solution)/shard_map/ppermute | solution.py:728
  463.6 45.8 %collective-permute-start.83 = (bf16[4,256,1024]{2,1,0:T(8,128)(2,1)}, bf16[4,256,1024]{2,1,0:T(8,128)(2,1)}, u32[]{:S(2)}, u32[]{:S(2)}) collective-permute-start(bf16[4,256,1024]{2,1,0:T(8,128)(2,1)} %get-tuple-element.458), channel_id=1, source_target_pairs={{0,4},{4,0},{8,12},{12,8},{16,20},{20,16},{24,28},{28,24},{1,5},{5... | collective-permute-start | bytes 6291464 | tf_op jit(solution)/shard_map/ppermute | solution.py:728
  467.7 95.7 %reduce-scatter.6.cloned.1.call-start = ((), (), s32[]{:S(2)}) async-start(), calls=%async_computation.8 | async-start | bytes 2621440 | tf_op jit(solution)/shard_map/reduce_scatter | solution.py:850
  478.3 25.3 %collective-permute-start.80 = (bf16[256,1024]{1,0:T(8,128)(2,1)}, bf16[256,1024]{1,0:T(8,128)(2,1)S(1)}, u32[]{:S(2)}, u32[]{:S(2)}) collective-permute-start(bf16[256,1024]{1,0:T(8,128)(2,1)} %copy-done.73), channel_id=1, source_target_pairs={{0,2},{1,3},{2,0},{3,1},{4,6},{5,7},{6,4},{7,5},{8,10},{9,11},{10,... | collective-permute-start | bytes 1572872 | tf_op jit(solution)/shard_map/ppermute | solution.py:728
  478.4 25.6 %collective-permute-start.81 = (bf16[256,1024]{1,0:T(8,128)(2,1)}, bf16[256,1024]{1,0:T(8,128)(2,1)S(1)}, u32[]{:S(2)}, u32[]{:S(2)}) collective-permute-start(bf16[256,1024]{1,0:T(8,128)(2,1)} %copy-done.73), channel_id=1, source_target_pairs={{0,1},{1,0},{2,3},{3,2},{4,5},{5,4},{6,7},{7,6},{8,9},{9,8},{10,11... | collective-permute-start | bytes 1572872 | tf_op jit(solution)/shard_map/ppermute | solution.py:728
  512.9 103.1 %reduce-scatter.14.cloned.1.call-start = ((), (), s32[]{:S(2)}) async-start(), calls=%async_computation.12 | async-start | bytes 1966080 | tf_op jit(solution)/shard_map/reduce_scatter | solution.py:850
  513.1 38.2 %collective-permute-start.86 = (bf16[4,256,768]{2,1,0:T(8,128)(2,1)}, bf16[4,256,768]{2,1,0:T(8,128)(2,1)}, u32[]{:S(2)}, u32[]{:S(2)}) collective-permute-start(bf16[4,256,768]{2,1,0:T(8,128)(2,1)} %copy-done.160), channel_id=1, source_target_pairs={{0,4},{4,0},{8,12},{12,8},{16,20},{20,16},{24,28},{28,24},{1,5},{5... | collective-permute-start | bytes 4718600 | tf_op jit(solution)/shard_map/ppermute | solution.py:728
  554.4 121.4 %reduce-scatter.12.cloned.1.call-start = ((), (), s32[]{:S(2)}) async-start(), calls=%async_computation.11 | async-start | bytes 983040 | tf_op jit(solution)/shard_map/reduce_scatter | solution.py:850
  555.3 28.3 %collective-permute-start.91 = (bf16[4,128,768]{2,1,0:T(8,128)(2,1)}, bf16[4,128,768]{2,1,0:T(8,128)(2,1)}, u32[]{:S(2)}, u32[]{:S(2)}) collective-permute-start(bf16[4,128,768]{2,1,0:T(8,128)(2,1)} %copy-done.163), channel_id=1, source_target_pairs={{0,4},{4,0},{8,12},{12,8},{16,20},{20,16},{24,28},{28,24},{1,5},{5... | collective-permute-start | bytes 2359304 | tf_op jit(solution)/shard_map/ppermute | solution.py:728
  556.0 24.2 %collective-permute-start.90 = (bf16[256,1024]{1,0:T(8,128)(2,1)}, bf16[256,1024]{1,0:T(8,128)(2,1)}, u32[]{:S(2)}, u32[]{:S(2)}) collective-permute-start(bf16[256,1024]{1,0:T(8,128)(2,1)} %add_low.36), channel_id=1, source_target_pairs={{0,2},{1,3},{2,0},{3,1},{4,6},{5,7},{6,4},{7,5},{8,10},{9,11},{10,... | collective-permute-start | bytes 1572872 | tf_op jit(solution)/shard_map/ppermute | solution.py:728
  558.0 33.4 %collective-permute-start.92 = (bf16[256,1024]{1,0:T(8,128)(2,1)S(1)}, bf16[256,1024]{1,0:T(8,128)(2,1)S(1)}, u32[]{:S(2)}, u32[]{:S(2)}) collective-permute-start(bf16[256,1024]{1,0:T(8,128)(2,1)S(1)} %copy-done.53), channel_id=1, source_target_pairs={{0,2},{1,3},{2,0},{3,1},{4,6},{5,7},{6,4},{7,5},{8,10},{9,11},{10,... | collective-permute-start | bytes 1572872 | tf_op jit(solution)/shard_map/ppermute | solution.py:728
  568.9 26.1 %collective-permute-start.93 = (bf16[256,1024]{1,0:T(8,128)(2,1)S(1)}, bf16[256,1024]{1,0:T(8,128)(2,1)}, u32[]{:S(2)}, u32[]{:S(2)}) collective-permute-start(bf16[256,1024]{1,0:T(8,128)(2,1)S(1)} %copy-done.53), channel_id=1, source_target_pairs={{0,1},{1,0},{2,3},{3,2},{4,5},{5,4},{6,7},{7,6},{8,9},{9,8},{10,11... | collective-permute-start | bytes 1572872 | tf_op jit(solution)/shard_map/ppermute | solution.py:728
  592.3 24.8 %collective-permute-start.100 = (bf16[256,1024]{1,0:T(8,128)(2,1)S(1)}, bf16[256,1024]{1,0:T(8,128)(2,1)S(1)}, u32[]{:S(2)}, u32[]{:S(2)}) collective-permute-start(bf16[256,1024]{1,0:T(8,128)(2,1)S(1)} %add_low.38.refs_0_), channel_id=1, source_target_pairs={{0,2},{1,3},{2,0},{3,1},{4,6},{5,7},{6,4},{7,5},{8,10},{9,11},{10,... | collective-permute-start | bytes 1572872 | tf_op jit(solution)/shard_map/ppermute | solution.py:728
  640.6 27.7 %collective-permute-start.112 = (bf16[3,128,1024]{2,1,0:T(8,128)(2,1)S(1)}, bf16[3,128,1024]{2,1,0:T(8,128)(2,1)S(1)}, u32[]{:S(2)}, u32[]{:S(2)}) collective-permute-start(bf16[3,128,1024]{2,1,0:T(8,128)(2,1)S(1)} %stack_places.1.one_ref), channel_id=1, source_target_pairs={{0,2},{1,3},{2,0},{3,1},{4,6},{5,7},{6,4},{7,5},{8,10},{9,11},{10,... | collective-permute-start | bytes 2359304 | tf_op jit(solution)/shard_map/ppermute | solution.py:728
  (275 other events, 2225.4 us)
Sparse Core Ops, SparseCore 0:
  23.2 48.9 all-gather.3
  88.5 53.5 all-gather.5
  176.7 47.9 all-gather.7
  411.8 49.0 reduce-scatter.9
  467.8 30.8 reduce-scatter.7
  513.0 50.3 reduce-scatter.5
  566.3 34.5 reduce-scatter.13
  640.9 21.1 reduce-scatter.11
